TPU v7x, 32 devices: a whole 2x2x4 slice. The times are simulated.
32 devices in a mesh: row: 8 (over z, x), col: 4 (over y, core).
Axes of the slice: x: 2, y: 2, z: 4, core: 2. Of those that a mesh axis runs over, the one named last changes fastest.
Arguments:
- off_blocks: bfloat16 [2048, 4, 96, 96], P(('row', 'col')), may hold values from -0.625 to 0.625
- neighbour: int32 [2048, 4], P(('row', 'col')), may hold values from 0 to 5
- active: int32 [2048, 4], P(('row', 'col')), may hold values 0 or 1
- diag_blocks: bfloat16 [2048, 96, 96], P(('row', 'col')), may hold values from -0.625 to 0.625
- diag_inverse: bfloat16 [2048, 96, 96], P(('row', 'col')), may hold values from -0.625 to 0.625
- tentative: bfloat16 [2048, 96, 96], P(('row', 'col')), may hold values from -0.21875 to 0.21875
- aggregate: int32 [2048], P(('row', 'col')), may hold values from 0 to 1
- owner_row: int32 [256, 1], P('row'), may hold values from 0 to 7; in each aligned block of 32 rows (0 to 31, 32 to 63, ...) at most 8 rows name the same one
- owner_group: int32 [256], P('row'), may hold values from 0 to 7
Outputs:
- coarse_blocks: float32 [64, 192, 192], P('row', 'col')
Inputs may be any that keep to these rules, and one draw needn't show every extreme that they name: `owner_row`: among the 32 clusters of one row tile at most 8 have the same owner row, and exactly 8 do in some tile.
All inputs are finite; a program needn't handle non-finite values. No bound on the sum of `active` on one device may be relied on, other than what follows from the above.
Results may differ from a plain program's by a relative error of at most 0.006.
Values may be sent and summed in bfloat16 or wider, within the bound.
No kernel may reach another device: no remote copies, remote signals or barrier semaphores. Data moves between devices by JAX's collectives and lax.ppermute only.
A program may use at most 128 MiB of HBM per device.

v0:
```python
import functools

import jax
import jax.numpy as jnp
from jax import lax
from jax.experimental import pallas as pl
from jax.experimental.pallas import tpu as pltpu
from jax.sharding import PartitionSpec as P


CW = 2
RQ = 2
G_DEV = 8
OMEGA = 0.6

EDGES = (0, 6, 12, 16)
STEP = 2


VMEM = pl.BlockSpec(memory_space=pltpu.VMEM)
SMEM = pl.BlockSpec(memory_space=pltpu.SMEM)
PARAMS = pltpu.CompilerParams(vmem_limit_bytes=67043328)


def step_of(first, count):
    return STEP if count % STEP == 0 and first % STEP == 0 else 1


def cost(flops, moved):
    return pl.CostEstimate(flops=int(flops), bytes_accessed=int(moved), transcendentals=0)


def pack_kernel(rows_ref, out_ref):
    per = rows_ref.shape[0] // out_ref.shape[0]
    width = rows_ref.shape[2]
    for m in range(out_ref.shape[0]):
        for j in range(per):
            out_ref[m, :, j * width : (j + 1) * width] = rows_ref[per * m + j]


def pack_rows(tentative, first, count):
    per = 2 * RQ
    _, high, width = tentative.shape
    step = step_of(first, count)
    return pl.pallas_call(
        pack_kernel,
        grid=(count // step,),
        in_specs=[pl.BlockSpec((per * step, high, width), lambda i: (i + first // step, 0, 0))],
        out_specs=pl.BlockSpec((step, high, per * width), lambda i: (i, 0, 0)),
        out_shape=jax.ShapeDtypeStruct((count, high, per * width), tentative.dtype),
        compiler_params=PARAMS,
        cost_estimate=cost(0, 5 * count * per * high * width),
    )(tentative)


def prolong_kernel(
    first, table, labels, off, diag, inverse, own, near_a, near_b, out, wide
):
    step = near_a.shape[0]
    slots, size = off.shape[1], off.shape[2]
    window = CW * size

    @pl.when(pl.program_id(0) == 0)
    def _():
        wide[3 * RQ] = jnp.zeros((size, window), wide.dtype)

    for m in range(step):
        for u in range(2):
            for k in range(RQ):
                j = u * RQ + k
                local = 2 * RQ * m + j
                row = 2 * RQ * (first + pl.program_id(0) * step + m) + j
                lanes = slice(j * size, (j + 1) * size)
                for side, block in enumerate(
                    (near_a[m, :, lanes], own[local], near_b[m, :, lanes])
                ):
                    label = labels[side, row]
                    for w in range(CW):
                        wide[side * RQ + k, :, w * size : (w + 1) * size] = jnp.where(
                            label == w, block, jnp.zeros_like(block)
                        )
            for k in range(RQ):
                j = u * RQ + k
                local = 2 * RQ * m + j
                row = 2 * RQ * (first + pl.program_id(0) * step + m) + j
                mine = wide[RQ + k]
                total = jnp.dot(diag[local], mine, preferred_element_type=jnp.float32)
                for s in range(slots):
                    total += jnp.dot(
                        off[local, s], wide[table[s, row]], preferred_element_type=jnp.float32
                    )
                change = jnp.dot(
                    inverse[local], total.astype(out.dtype), preferred_element_type=jnp.float32
                )
                out[2 * m + u, :, k * window : (k + 1) * window] = (
                    mine.astype(jnp.float32) - OMEGA * change
                ).astype(out.dtype)


def prolong_rows(table, labels, off, diag, inverse, tentative, near_a, near_b, first):
    per = 2 * RQ
    count, high, _ = near_a.shape
    slots, size = off.shape[1], off.shape[2]
    window = CW * size
    step = step_of(first, count)

    def rows(i):
        return (i + first // step, 0, 0)

    square = pl.BlockSpec((per * step, size, size), rows)
    packed = pl.BlockSpec((step, high, per * size), lambda i: (i, 0, 0))
    return pl.pallas_call(
        functools.partial(prolong_kernel, first),
        grid=(count // step,),
        in_specs=[
            SMEM,
            SMEM,
            pl.BlockSpec((per * step, slots, size, size), lambda i: rows(i) + (0,)),
            square,
            square,
            square,
            packed,
            packed,
        ],
        out_specs=pl.BlockSpec((2 * step, size, RQ * window), lambda i: (i, 0, 0)),
        out_shape=jax.ShapeDtypeStruct((2 * count, size, RQ * window), tentative.dtype),
        scratch_shapes=[pltpu.VMEM((3 * RQ + 1, size, window), tentative.dtype)],
        compiler_params=PARAMS,
        cost_estimate=cost(
            2 * count * per * (slots + 2) * size * size * window,
            2 * count * per * (slots + 7) * size * size,
        ),
    )(table, labels, off, diag, inverse, tentative, near_a, near_b)


def coarse_kernel(first, table, place, off, diag, own, near_a, near_b, keep, send, field, stiff, whole):
    step = keep.shape[1]
    slots, size = off.shape[1], off.shape[2]
    window = CW * size
    halves, high = keep.shape[0], keep.shape[2]
    col = place[0]

    @pl.when(pl.program_id(0) == 0)
    def _():
        field[3 * RQ] = jnp.zeros((size, window), field.dtype)

    for m in range(step):
        for u in range(2):
            for k in range(RQ):
                lanes = slice(k * window, (k + 1) * window)
                for side, source in enumerate((near_a, own, near_b)):
                    field[side * RQ + k] = source[2 * m + u, :, lanes]
            for k in range(RQ):
                j = u * RQ + k
                local = 2 * RQ * m + j
                row = 2 * RQ * (first + pl.program_id(0) * step + m) + j
                total = jnp.dot(diag[local], field[RQ + k], preferred_element_type=jnp.float32)
                for s in range(slots):
                    total += jnp.dot(
                        off[local, s], field[table[s, row]], preferred_element_type=jnp.float32
                    )
                stiff[k * size : (k + 1) * size, :] = total.astype(stiff.dtype)
            left = field[RQ : 2 * RQ].reshape(RQ * size, window)
            block = lax.dot_general(
                left, stiff[...], (((0,), (0,)), ((), ())), preferred_element_type=jnp.float32
            )
            for piece in range(2 * halves):
                whole[piece] = block[piece * high : (piece + 1) * high]
            lanes = slice(u * window, (u + 1) * window)
            for h in range(halves):
                keep[h, m, :, lanes] = whole[col ^ (2 * h)]
                send[h, m, :, lanes] = whole[col ^ (2 * h + 1)].astype(send.dtype)


def coarse_rows(table, place, off, diag, own, near_a, near_b, first, columns):
    per = 2 * RQ
    count = own.shape[0] // 2
    slots, size = off.shape[1], off.shape[2]
    window = CW * size
    halves, high = columns // 2, window // columns
    step = step_of(first, count)

    def rows(i):
        return (i + first // step, 0, 0)

    packed = pl.BlockSpec((2 * step, size, RQ * window), lambda i: (i, 0, 0))
    result = pl.BlockSpec((halves, step, high, 2 * window), lambda i: (0, i, 0, 0))
    shape = (halves, count, high, 2 * window)
    return pl.pallas_call(
        functools.partial(coarse_kernel, first),
        grid=(count // step,),
        in_specs=[
            SMEM,
            SMEM,
            pl.BlockSpec((per * step, slots, size, size), lambda i: rows(i) + (0,)),
            pl.BlockSpec((per * step, size, size), rows),
            packed,
            packed,
            packed,
        ],
        out_specs=[result, result],
        out_shape=[
            jax.ShapeDtypeStruct(shape, jnp.float32),
            jax.ShapeDtypeStruct(shape, own.dtype),
        ],
        scratch_shapes=[
            pltpu.VMEM((3 * RQ + 1, size, window), own.dtype),
            pltpu.VMEM((RQ * size, window), own.dtype),
            pltpu.VMEM((columns, high, window), jnp.float32),
        ],
        compiler_params=PARAMS,
        cost_estimate=cost(
            2 * count * per * (slots + 3) * size * size * window,
            2 * count * per * (slots + 12) * size * size,
        ),
    )(table, place, off, diag, own, near_a, near_b)


def add_groups(targets, place, sides, first, sums):
    groups = sums.shape[0] - 1
    window = sums.shape[2]
    row = place[1]
    for side, source in enumerate(sides):

        def one(m, carry, source=source, side=side):
            for u in range(2):
                target = targets[side, 2 * (first + m) + u]
                away = (target // G_DEV) ^ row
                spot = jnp.where(away % 2 == 0, away // 2 * G_DEV + target % G_DEV, groups)
                sums[spot] += source[m, :, u * window : (u + 1) * window].astype(jnp.float32)
            return carry

        count = source.shape[0]
        if count <= 4:
            for m in range(count):
                one(m, 0)
        else:
            lax.fori_loop(0, count, one, 0)


def gather_kernel(starts, targets, place, *refs):
    sums = refs[-1]
    sums[...] = jnp.zeros_like(sums)
    for part, first in enumerate(starts):
        add_groups(targets, place, refs[2 * part : 2 * part + 2], first, sums)


def gather_groups(targets, place, parts, starts, rows):
    _, high, lanes = parts[0][0].shape
    shape = (rows // 2 * G_DEV + 1, high, lanes // 2)
    flat = [array for pair in parts for array in pair]
    total = sum(array.size for array in flat)
    return pl.pallas_call(
        functools.partial(gather_kernel, starts),
        in_specs=[SMEM, SMEM] + [VMEM] * len(flat),
        out_specs=VMEM,
        out_shape=jax.ShapeDtypeStruct(shape, jnp.float32),
        compiler_params=PARAMS,
        cost_estimate=cost(total, 4 * total),
    )(targets, place, *flat)


def split_kernel(first, targets, place, early, mine, theirs, keep, send, sums):
    sums[...] = early[...]
    add_groups(targets, place, (mine, theirs), first, sums)
    window = sums.shape[2]
    for h in range(keep.shape[0]):
        for p in range(keep.shape[1]):
            for u in range(2):
                lanes = slice(u * window, (u + 1) * window)
                inner = 2 * p + u
                keep[h, p, :, lanes] = sums[2 * h * G_DEV + inner]
                send[h, p, :, lanes] = sums[(2 * h + 1) * G_DEV + inner].astype(send.dtype)


def split_groups(targets, place, early, mine, theirs, first, rows):
    _, high, lanes = mine.shape
    shape = (rows // 4, G_DEV // 2, high, lanes)
    return pl.pallas_call(
        functools.partial(split_kernel, first),
        in_specs=[SMEM, SMEM, VMEM, VMEM, VMEM],
        out_specs=[VMEM, VMEM],
        out_shape=[
            jax.ShapeDtypeStruct(shape, jnp.float32),
            jax.ShapeDtypeStruct(shape, mine.dtype),
        ],
        scratch_shapes=[pltpu.VMEM(early.shape, jnp.float32)],
        compiler_params=PARAMS,
        cost_estimate=cost(early.size, 10 * early.size),
    )(targets, place, early, mine, theirs)


def finish_kernel(keep_ref, *refs):
    others, out_ref = refs[:-1], refs[-1]
    window = out_ref.shape[2]
    for p in range(keep_ref.shape[1]):
        total = keep_ref[0, p]
        for other in others:
            total += other[0, p].astype(jnp.float32)
        for u in range(2):
            out_ref[2 * p + u] = total[:, u * window : (u + 1) * window]


def finish(keep, *others):
    _, pairs, high, lanes = keep.shape
    block = pl.BlockSpec((1, pairs, high, lanes), lambda i: (0, 0, 0, 0))
    return pl.pallas_call(
        finish_kernel,
        grid=(1,),
        in_specs=[block] * (1 + len(others)),
        out_specs=pl.BlockSpec((2 * pairs, high, lanes // 2), lambda i: (0, 0, 0)),
        out_shape=jax.ShapeDtypeStruct((2 * pairs, high, lanes // 2), jnp.float32),
        compiler_params=PARAMS,
        cost_estimate=cost(pairs * high * lanes, 10 * pairs * high * lanes),
    )(keep, *others)


def flip(count, bit):
    return [(i, i ^ bit) for i in range(count)]


def exchange(keep, send, axis, count, bit, link):
    terms = [keep]
    while True:
        terms.append(lax.ppermute(send, axis, flip(count, bit)))
        bit *= 2
        if bit == count:
            return terms
        send = sum(term[1::2].astype(jnp.float32) for term in terms).astype(link)
        terms = [term[0::2] for term in terms]


def on_device(
    off_blocks,
    neighbour,
    active,
    diag_blocks,
    diag_inverse,
    tentative,
    aggregate,
    owner_row,
    owner_group,
):
    columns, rows = lax.axis_size("col"), lax.axis_size("row")
    col, row = lax.axis_index("col"), lax.axis_index("row")
    assert columns & (columns - 1) == 0 and columns >= 2
    assert rows & (rows - 1) == 0 and rows >= 4
    link = tentative.dtype
    groups = tentative.shape[0] // (2 * RQ)

    pair_a = flip(columns, 1)
    pair_b = [(i, (i + 1) % columns if i % 2 else (i - 1) % columns) for i in range(columns)]

    bounds = [groups * edge // EDGES[-1] for edge in EDGES]
    spans = list(zip(bounds[:-1], bounds[1:]))

    def both(block):
        near_b = lax.ppermute(block, "col", pair_b)
        near_a = lax.ppermute(block, "col", pair_a)
        return near_a, near_b

    halos = []
    for low, high in spans:
        packed = pack_rows(tentative, low, high - low)
        halos.append(both(packed))
    label_a, label_b = both(aggregate)
    labels = jnp.stack([label_a, aggregate, label_b])
    targets = owner_row[:, 0] * G_DEV + owner_group
    other_targets = lax.ppermute(targets, "row", flip(rows, 1))
    targets = jnp.stack([targets, other_targets])
    side = neighbour // RQ
    side = jnp.where(col % 2 == 0, 2 - side, side)
    table = jnp.where(active != 0, side * RQ + neighbour % RQ, 3 * RQ).T
    place = jnp.stack([col, row])
    labels, targets, table, place = lax.optimization_barrier((labels, targets, table, place))

    fields = []
    for (low, high), (near_a, near_b) in zip(spans, halos):
        field = prolong_rows(
            table, labels, off_blocks, diag_blocks, diag_inverse, tentative, near_a, near_b, low
        )
        fields.append((field, *both(field)))
    parts = []
    for (low, high), (field, near_a, near_b) in zip(spans, fields):
        keep, send = coarse_rows(
            table, place, off_blocks, diag_blocks, field, near_a, near_b, low, columns
        )
        terms = exchange(keep, send, "col", columns, 1, link)
        total = sum(term[0].astype(jnp.float32) for term in terms).astype(link)
        other = lax.ppermute(total, "row", flip(rows, 1))
        parts.append((total, other))
    early = gather_groups(targets, place, parts[:-1], [low for low, _ in spans[:-1]], rows)
    keep, send = split_groups(targets, place, early, *parts[-1], spans[-1][0], rows)
    return finish(*exchange(keep, send, "row", rows, 2, link))


def solution(mesh):
    return jax.shard_map(
        on_device,
        mesh=mesh,
        in_specs=(
            P(("row", "col"), None, None, None),
            P(("row", "col"), None),
            P(("row", "col"), None),
            P(("row", "col"), None, None),
            P(("row", "col"), None, None),
            P(("row", "col"), None, None),
            P(("row", "col")),
            P("row", None),
            P("row"),
        ),
        out_specs=P("row", "col", None),
        check_vma=False,
    )
```

profile of v0, /device:TPU:0, one launch (start us, length us, event | category | flops | bytes accessed | tf_op | source)
XLA Modules:
  0.0 165.8 jit_solution(4703444416976046444)
XLA Ops:
  0.0 2.4 %collective-permute-start.1 = (s32[64]{0:T(128)}, s32[64]{0:T(128)}, u32[]{:S(2)}, u32[]{:S(2)}) collective-permute-start(s32[64]{0:T(128)} %param.15), channel_id=1, source_target_pairs={{0,3},{1,2},{2,1},{3,0},{4,7},{5,6},{6,5},{7,4},{8,11},{9,10},{10,... | collective-permute-start | bytes 776 | tf_op jit(solution)/shard_map/ppermute | solution.py:358
  2.4 0.7 collective-permute-start
  3.1 1.9 %shard_map.98 = bf16[4,96,384]{2,1,0:T(8,128)(2,1)} custom-call(bf16[64,96,96]{2,1,0:T(8,128)(2,1)} %own.5), custom_call_target="tpu_custom_call" | custom-call | bytes 737280 | tf_op jit(solution)/shard_map/pallas_call | solution.py:45
  5.0 1.2 bitcast_add_fusion
  6.2 2.1 %collective-permute-start.2 = (s32[32]{0:T(128)}, s32[32]{0:T(128)}, u32[]{:S(2)}, u32[]{:S(2)}) collective-permute-start(s32[32]{0:T(128)} %bitcast_add_fusion), channel_id=1, source_target_pairs={{0,4},{4,0},{8,12},{12,8},{16,20},{20,16},{24,28},{28,24},{1,5},{5... | collective-permute-start | bytes 392 | tf_op jit(solution)/shard_map/ppermute | solution.py:369
  8.3 1.3 fusion.6.table
  9.6 0.6 pad_add_fusion.2.place
  10.2 2.9 %shard_map.91 = bf16[6,96,384]{2,1,0:T(8,128)(2,1)} custom-call(bf16[64,96,96]{2,1,0:T(8,128)(2,1)} %own.5), custom_call_target="tpu_custom_call" | custom-call | bytes 1105920 | tf_op jit(solution)/shard_map/pallas_call | solution.py:45
  13.1 1.2 pad_add_fusion.1.targets
  14.3 1.6 collective-permute-start.4
  16.0 1.3 pad_add_fusion.labels
  17.3 7.4 %shard_map.99.own = bf16[8,96,384]{2,1,0:T(8,128)(2,1)} custom-call(s32[4,64]{1,0:T(4,128)} %fusion.6.table, s32[3,64]{1,0:T(4,128)} %pad_add_fusion.labels, bf16[64,4,96,96]{3,2,1,0:T(8,128)(2,1)} %off.11, bf16[64,96,96]{2,1,0:T(8,128)(2,1)} %diag.11, bf16[64,96,96]{2,1,0:T(8,128)(2,1)} %inverse.5, bf16[64,96,96]{2,1,0:T(8,128)(2,1)} %own.5, ...), custom_call_target="tpu_custom_call" | custom-call | flops 339738624 | bytes 3244032 | tf_op jit(solution)/shard_map/pallas_call | solution.py:112
  24.7 2.9 %shard_map.94 = bf16[6,96,384]{2,1,0:T(8,128)(2,1)} custom-call(bf16[64,96,96]{2,1,0:T(8,128)(2,1)} %own.5), custom_call_target="tpu_custom_call" | custom-call | bytes 1105920 | tf_op jit(solution)/shard_map/pallas_call | solution.py:45
  27.5 0.5 collective-permute-start.10
  28.2 10.0 %shard_map.92.own = bf16[12,96,384]{2,1,0:T(8,128)(2,1)} custom-call(s32[4,64]{1,0:T(4,128)} %fusion.6.table, s32[3,64]{1,0:T(4,128)} %pad_add_fusion.labels, bf16[64,4,96,96]{3,2,1,0:T(8,128)(2,1)} %off.11, bf16[64,96,96]{2,1,0:T(8,128)(2,1)} %diag.11, bf16[64,96,96]{2,1,0:T(8,128)(2,1)} %inverse.5, bf16[64,96,96]{2,1,0:T(8,128)(2,1)} %own.5, ...), custom_call_target="tpu_custom_call" | custom-call | flops 509607936 | bytes 4866048 | tf_op jit(solution)/shard_map/pallas_call | solution.py:112
  38.1 0.5 collective-permute-start.5
  38.6 1.2 collective-permute-start.6
  39.8 0.8 collective-permute-done.11.near_b
  40.6 10.0 %shard_map.95.own = bf16[12,96,384]{2,1,0:T(8,128)(2,1)} custom-call(s32[4,64]{1,0:T(4,128)} %fusion.6.table, s32[3,64]{1,0:T(4,128)} %pad_add_fusion.labels, bf16[64,4,96,96]{3,2,1,0:T(8,128)(2,1)} %off.11, bf16[64,96,96]{2,1,0:T(8,128)(2,1)} %diag.11, bf16[64,96,96]{2,1,0:T(8,128)(2,1)} %inverse.5, bf16[64,96,96]{2,1,0:T(8,128)(2,1)} %own.5, ...), custom_call_target="tpu_custom_call" | custom-call | flops 509607936 | bytes 4866048 | tf_op jit(solution)/shard_map/pallas_call | solution.py:112
  50.7 0.5 collective-permute-start.13
  51.2 1.2 collective-permute-start.20
  52.5 39.8 %collective-permute-done.20.near_b = bf16[8,96,384]{2,1,0:T(8,128)(2,1)} collective-permute-done((bf16[8,96,384]{2,1,0:T(8,128)(2,1)}, bf16[8,96,384]{2,1,0:T(8,128)(2,1)}, u32[]{:S(2)}, u32[]{:S(2)}) %collective-permute-start.20) | collective-permute-done | bytes 589856 | tf_op jit(solution)/shard_map/ppermute | solution.py:358
  92.2 5.6 %shard_map.100 = (f32[2,4,48,384]{3,2,1,0:T(8,128)}, bf16[2,4,48,384]{3,2,1,0:T(8,128)(2,1)}) custom-call(s32[4,64]{1,0:T(4,128)} %fusion.6.table, s32[2]{0:T(128)} %pad_add_fusion.2.place, bf16[64,4,96,96]{3,2,1,0:T(8,128)(2,1)} %off.11, bf16[64,96,96]{2,1,0:T(8,128)(2,1)} %diag.11, bf16[8,96,384]{2,1,0:T(8,128)(2,1)} %shard_map.99.own, ...), custom_call_target="tpu_custom_call" | custom-call | flops 396361728 | bytes 4718592 | tf_op jit(solution)/shard_map/pallas_call | solution.py:189
  98.0 7.4 %shard_map.93 = (f32[2,6,48,384]{3,2,1,0:T(8,128)}, bf16[2,6,48,384]{3,2,1,0:T(8,128)(2,1)}) custom-call(s32[4,64]{1,0:T(4,128)} %fusion.6.table, s32[2]{0:T(128)} %pad_add_fusion.2.place, bf16[64,4,96,96]{3,2,1,0:T(8,128)(2,1)} %off.11, bf16[64,96,96]{2,1,0:T(8,128)(2,1)} %diag.11, bf16[12,96,384]{2,1,0:T(8,128)(2,1)} %shard_map.92.own, ...), custom_call_target="tpu_custom_call" | custom-call | flops 594542592 | bytes 7077888 | tf_op jit(solution)/shard_map/pallas_call | solution.py:189
  105.8 7.4 %shard_map.96 = (f32[2,6,48,384]{3,2,1,0:T(8,128)}, bf16[2,6,48,384]{3,2,1,0:T(8,128)(2,1)}) custom-call(s32[4,64]{1,0:T(4,128)} %fusion.6.table, s32[2]{0:T(128)} %pad_add_fusion.2.place, bf16[64,4,96,96]{3,2,1,0:T(8,128)(2,1)} %off.11, bf16[64,96,96]{2,1,0:T(8,128)(2,1)} %diag.11, bf16[12,96,384]{2,1,0:T(8,128)(2,1)} %shard_map.95.own, ...), custom_call_target="tpu_custom_call" | custom-call | flops 594542592 | bytes 7077888 | tf_op jit(solution)/shard_map/pallas_call | solution.py:189
  113.4 1.1 add_convert_fusion.6
  114.5 1.6 collective-permute-start.22
  116.1 1.1 add_convert_fusion.3
  117.2 0.5 collective-permute-start.8
  117.8 1.1 add_convert_fusion.1
  118.8 1.6 collective-permute-start.15
  120.4 5.6 %collective-permute-done.8 = bf16[1,6,48,384]{3,2,1,0:T(8,128)(2,1)S(1)} collective-permute-done((bf16[1,6,48,384]{3,2,1,0:T(8,128)(2,1)S(1)}, bf16[1,6,48,384]{3,2,1,0:T(8,128)(2,1)S(1)}, u32[]{:S(2)}, u32[]{:S(2)}) %collective-permute-start.8) | collective-permute-done | bytes 221216 | tf_op jit(solution)/shard_map/ppermute | solution.py:325
  126.0 1.0 fusion.refs_0_
  127.2 2.9 %collective-permute-done.15 = bf16[1,6,48,384]{3,2,1,0:T(8,128)(2,1)S(1)} collective-permute-done((bf16[1,6,48,384]{3,2,1,0:T(8,128)(2,1)S(1)}, bf16[1,6,48,384]{3,2,1,0:T(8,128)(2,1)S(1)}, u32[]{:S(2)}, u32[]{:S(2)}) %collective-permute-start.15) | collective-permute-done | bytes 221216 | tf_op jit(solution)/shard_map/ppermute | solution.py:325
  130.6 1.6 fusion.2.mine
  132.2 1.7 %collective-permute-start.23 = (bf16[4,48,384]{2,1,0:T(8,128)(2,1)}, bf16[4,48,384]{2,1,0:T(8,128)(2,1)}, u32[]{:S(2)}, u32[]{:S(2)}) collective-permute-start(bf16[4,48,384]{2,1,0:T(8,128)(2,1)} %fusion.2.mine), channel_id=1, source_target_pairs={{0,4},{4,0},{8,12},{12,8},{16,20},{20,16},{24,28},{28,24},{1,5},{5... | collective-permute-start | bytes 442376 | tf_op jit(solution)/shard_map/ppermute | solution.py:390
  134.2 0.7 copy-done.5
  134.9 4.2 %collective-permute-done.16.refs_3_ = bf16[6,48,384]{2,1,0:T(8,128)(2,1)} collective-permute-done((bf16[6,48,384]{2,1,0:T(8,128)(2,1)S(1)}, bf16[6,48,384]{2,1,0:T(8,128)(2,1)}, u32[]{:S(2)}, u32[]{:S(2)}) %collective-permute-start.16) | collective-permute-done | bytes 221216 | tf_op jit(solution)/shard_map/ppermute | solution.py:390
  139.0 4.4 %shard_map.97.early = f32[33,48,192]{2,1,0:T(8,128)} custom-call(s32[2,32]{1,0:T(2,128)} %pad_add_fusion.1.targets, s32[2]{0:T(128)} %pad_add_fusion.2.place, bf16[6,48,384]{2,1,0:T(8,128)(2,1)} %copy-done.2, bf16[6,48,384]{2,1,0:T(8,128)(2,1)} %copy-done.5, bf16[6,48,384]{2,1,0:T(8,128)(2,1)} %copy-done.3, bf16[6,48,384]{2,1,0:T(8,128)(2,1)} %collective-permute-done.16.refs_3_), custom_call_target="tpu_custom_call" | custom-call | flops 442368 | bytes 1769472 | tf_op jit(solution)/shard_map/pallas_call | solution.py:253
  143.5 2.9 %shard_map.101 = (f32[2,4,48,384]{3,2,1,0:T(8,128)}, bf16[2,4,48,384]{3,2,1,0:T(8,128)(2,1)}) custom-call(s32[2,32]{1,0:T(2,128)} %pad_add_fusion.1.targets, s32[2]{0:T(128)} %pad_add_fusion.2.place, f32[33,48,192]{2,1,0:T(8,128)} %shard_map.97.early, bf16[4,48,384]{2,1,0:T(8,128)(2,1)} %fusion.2.mine, bf16[4,48,384]{2,1,0:T(8,128)(2,1)} %collective-permute-done.23.theirs), custom_call_target="tpu_custom_call" | custom-call | flops 304128 | bytes 3041280 | tf_op jit(solution)/shard_map/pallas_call | solution.py:279
  146.4 1.6 collective-permute-start.24
  148.0 5.8 %collective-permute-done.24 = bf16[2,4,48,384]{3,2,1,0:T(8,128)(2,1)S(1)} collective-permute-done((bf16[2,4,48,384]{3,2,1,0:T(8,128)(2,1)}, bf16[2,4,48,384]{3,2,1,0:T(8,128)(2,1)S(1)}, u32[]{:S(2)}, u32[]{:S(2)}) %collective-permute-start.24) | collective-permute-done | bytes 294944 | tf_op jit(solution)/shard_map/ppermute | solution.py:325
  153.7 1.8 %add_convert_fusion.4 = (bf16[1,4,48,384]{3,2,1,0:T(8,128)(2,1)S(1)}, f32[1,4,48,384]{3,2,1,0:T(8,128)}) fusion(f32[2,4,48,384]{3,2,1,0:T(8,128)} %get-tuple-element.27, bf16[2,4,48,384]{3,2,1,0:T(8,128)(2,1)S(1)} %collective-permute-done.24), kind=kLoop, calls=%fused_computation.4 | loop fusion | flops 221184 | bytes 1179648 | tf_op jit(solution)/shard_map/convert_element_type | solution.py:329
  155.6 2.6 %collective-permute-start.25 = (bf16[1,4,48,384]{3,2,1,0:T(8,128)(2,1)S(1)}, bf16[1,4,48,384]{3,2,1,0:T(8,128)(2,1)S(1)}, u32[]{:S(2)}, u32[]{:S(2)}) collective-permute-start(bf16[1,4,48,384]{3,2,1,0:T(8,128)(2,1)S(1)} %get-tuple-element.29), channel_id=1, source_target_pairs={{0,16},{4,20},{8,24},{12,28},{16,0},{20,4},{24,8},{28,12},{1,17},{... | collective-permute-start | bytes 442376 | tf_op jit(solution)/shard_map/ppermute | solution.py:325
  158.2 0.7 slice.86.refs_0_
  158.8 4.3 %collective-permute-done.25.refs_1_ = bf16[1,4,48,384]{3,2,1,0:T(8,128)(2,1)S(1)} collective-permute-done((bf16[1,4,48,384]{3,2,1,0:T(8,128)(2,1)S(1)}, bf16[1,4,48,384]{3,2,1,0:T(8,128)(2,1)S(1)}, u32[]{:S(2)}, u32[]{:S(2)}) %collective-permute-start.25) | collective-permute-done | bytes 147488 | tf_op jit(solution)/shard_map/ppermute | solution.py:325
  163.2 0.6 copy-done.6
  163.8 1.9 %shard_map.102 = f32[8,48,192]{2,1,0:T(8,128)} custom-call(f32[1,4,48,384]{3,2,1,0:T(8,128)} %get-tuple-element.30.keep_ref, bf16[1,4,48,384]{3,2,1,0:T(8,128)(2,1)} %slice.86.refs_0_, bf16[1,4,48,384]{3,2,1,0:T(8,128)(2,1)} %copy-done.6), custom_call_target="tpu_custom_call" | custom-call | flops 73728 | bytes 737280 | tf_op jit(solution)/shard_map/pallas_call | solution.py:307
  (43 shorter events, 1.9 us)
Async XLA Ops:
  0.0 14.3 %collective-permute-start.1 = (s32[64]{0:T(128)}, s32[64]{0:T(128)}, u32[]{:S(2)}, u32[]{:S(2)}) collective-permute-start(s32[64]{0:T(128)} %param.15), channel_id=1, source_target_pairs={{0,3},{1,2},{2,1},{3,0},{4,7},{5,6},{6,5},{7,4},{8,11},{9,10},{10,... | collective-permute-start | bytes 776 | tf_op jit(solution)/shard_map/ppermute | solution.py:358
  2.4 13.5 %collective-permute-start = (s32[64]{0:T(128)}, s32[64]{0:T(128)}, u32[]{:S(2)}, u32[]{:S(2)}) collective-permute-start(s32[64]{0:T(128)} %param.15), channel_id=1, source_target_pairs={{0,1},{1,0},{2,3},{3,2},{4,5},{5,4},{6,7},{7,6},{8,9},{9,8},{10,11... | collective-permute-start | bytes 776 | tf_op jit(solution)/shard_map/ppermute | solution.py:359
  5.0 12.3 %collective-permute-start.17 = (bf16[4,96,384]{2,1,0:T(8,128)(2,1)}, bf16[4,96,384]{2,1,0:T(8,128)(2,1)}, u32[]{:S(2)}, u32[]{:S(2)}) collective-permute-start(bf16[4,96,384]{2,1,0:T(8,128)(2,1)} %shard_map.98), channel_id=1, source_target_pairs={{0,1},{1,0},{2,3},{3,2},{4,5},{5,4},{6,7},{7,6},{8,9},{9,8},{10,11... | collective-permute-start | bytes 884744 | tf_op jit(solution)/shard_map/ppermute | solution.py:359
  5.0 12.3 %collective-permute-start.18 = (bf16[4,96,384]{2,1,0:T(8,128)(2,1)}, bf16[4,96,384]{2,1,0:T(8,128)(2,1)}, u32[]{:S(2)}, u32[]{:S(2)}) collective-permute-start(bf16[4,96,384]{2,1,0:T(8,128)(2,1)} %shard_map.98), channel_id=1, source_target_pairs={{0,3},{1,2},{2,1},{3,0},{4,7},{5,6},{6,5},{7,4},{8,11},{9,10},{10,... | collective-permute-start | bytes 884744 | tf_op jit(solution)/shard_map/ppermute | solution.py:358
  6.2 6.9 %collective-permute-start.2 = (s32[32]{0:T(128)}, s32[32]{0:T(128)}, u32[]{:S(2)}, u32[]{:S(2)}) collective-permute-start(s32[32]{0:T(128)} %bitcast_add_fusion), channel_id=1, source_target_pairs={{0,4},{4,0},{8,12},{12,8},{16,20},{20,16},{24,28},{28,24},{1,5},{5... | collective-permute-start | bytes 392 | tf_op jit(solution)/shard_map/ppermute | solution.py:369
  13.1 15.0 %collective-permute-start.3 = (bf16[6,96,384]{2,1,0:T(8,128)(2,1)}, bf16[6,96,384]{2,1,0:T(8,128)(2,1)}, u32[]{:S(2)}, u32[]{:S(2)}) collective-permute-start(bf16[6,96,384]{2,1,0:T(8,128)(2,1)} %shard_map.91), channel_id=1, source_target_pairs={{0,1},{1,0},{2,3},{3,2},{4,5},{5,4},{6,7},{7,6},{8,9},{9,8},{10,11... | collective-permute-start | bytes 1327112 | tf_op jit(solution)/shard_map/ppermute | solution.py:359
  14.3 13.8 %collective-permute-start.4 = (bf16[6,96,384]{2,1,0:T(8,128)(2,1)}, bf16[6,96,384]{2,1,0:T(8,128)(2,1)}, u32[]{:S(2)}, u32[]{:S(2)}) collective-permute-start(bf16[6,96,384]{2,1,0:T(8,128)(2,1)} %shard_map.91), channel_id=1, source_target_pairs={{0,3},{1,2},{2,1},{3,0},{4,7},{5,6},{6,5},{7,4},{8,11},{9,10},{10,... | collective-permute-start | bytes 1327112 | tf_op jit(solution)/shard_map/ppermute | solution.py:358
  24.6 26.6 %collective-permute-start.19 = (bf16[8,96,384]{2,1,0:T(8,128)(2,1)}, bf16[8,96,384]{2,1,0:T(8,128)(2,1)}, u32[]{:S(2)}, u32[]{:S(2)}) collective-permute-start(bf16[8,96,384]{2,1,0:T(8,128)(2,1)} %shard_map.99.own), channel_id=1, source_target_pairs={{0,1},{1,0},{2,3},{3,2},{4,5},{5,4},{6,7},{7,6},{8,9},{9,8},{10,11... | collective-permute-start | bytes 1769480 | tf_op jit(solution)/shard_map/ppermute | solution.py:359
  27.5 12.3 %collective-permute-start.10 = (bf16[6,96,384]{2,1,0:T(8,128)(2,1)}, bf16[6,96,384]{2,1,0:T(8,128)(2,1)}, u32[]{:S(2)}, u32[]{:S(2)}) collective-permute-start(bf16[6,96,384]{2,1,0:T(8,128)(2,1)} %shard_map.94), channel_id=1, source_target_pairs={{0,1},{1,0},{2,3},{3,2},{4,5},{5,4},{6,7},{7,6},{8,9},{9,8},{10,11... | collective-permute-start | bytes 1327112 | tf_op jit(solution)/shard_map/ppermute | solution.py:359
  28.0 12.6 %collective-permute-start.11 = (bf16[6,96,384]{2,1,0:T(8,128)(2,1)}, bf16[6,96,384]{2,1,0:T(8,128)(2,1)}, u32[]{:S(2)}, u32[]{:S(2)}) collective-permute-start(bf16[6,96,384]{2,1,0:T(8,128)(2,1)} %shard_map.94), channel_id=1, source_target_pairs={{0,3},{1,2},{2,1},{3,0},{4,7},{5,6},{6,5},{7,4},{8,11},{9,10},{10,... | collective-permute-start | bytes 1327112 | tf_op jit(solution)/shard_map/ppermute | solution.py:358
  38.1 59.9 %collective-permute-start.5 = (bf16[12,96,384]{2,1,0:T(8,128)(2,1)}, bf16[12,96,384]{2,1,0:T(8,128)(2,1)}, u32[]{:S(2)}, u32[]{:S(2)}) collective-permute-start(bf16[12,96,384]{2,1,0:T(8,128)(2,1)} %shard_map.92.own), channel_id=1, source_target_pairs={{0,1},{1,0},{2,3},{3,2},{4,5},{5,4},{6,7},{7,6},{8,9},{9,8},{10,11... | collective-permute-start | bytes 2654216 | tf_op jit(solution)/shard_map/ppermute | solution.py:359
  38.6 59.4 %collective-permute-start.6 = (bf16[12,96,384]{2,1,0:T(8,128)(2,1)}, bf16[12,96,384]{2,1,0:T(8,128)(2,1)}, u32[]{:S(2)}, u32[]{:S(2)}) collective-permute-start(bf16[12,96,384]{2,1,0:T(8,128)(2,1)} %shard_map.92.own), channel_id=1, source_target_pairs={{0,3},{1,2},{2,1},{3,0},{4,7},{5,6},{6,5},{7,4},{8,11},{9,10},{10,... | collective-permute-start | bytes 2654216 | tf_op jit(solution)/shard_map/ppermute | solution.py:358
  50.6 55.2 %collective-permute-start.12 = (bf16[12,96,384]{2,1,0:T(8,128)(2,1)}, bf16[12,96,384]{2,1,0:T(8,128)(2,1)}, u32[]{:S(2)}, u32[]{:S(2)}) collective-permute-start(bf16[12,96,384]{2,1,0:T(8,128)(2,1)} %shard_map.95.own), channel_id=1, source_target_pairs={{0,1},{1,0},{2,3},{3,2},{4,5},{5,4},{6,7},{7,6},{8,9},{9,8},{10,11... | collective-permute-start | bytes 2654216 | tf_op jit(solution)/shard_map/ppermute | solution.py:359
  50.7 55.0 %collective-permute-start.13 = (bf16[12,96,384]{2,1,0:T(8,128)(2,1)}, bf16[12,96,384]{2,1,0:T(8,128)(2,1)}, u32[]{:S(2)}, u32[]{:S(2)}) collective-permute-start(bf16[12,96,384]{2,1,0:T(8,128)(2,1)} %shard_map.95.own), channel_id=1, source_target_pairs={{0,3},{1,2},{2,1},{3,0},{4,7},{5,6},{6,5},{7,4},{8,11},{9,10},{10,... | collective-permute-start | bytes 2654216 | tf_op jit(solution)/shard_map/ppermute | solution.py:358
  51.2 41.0 %collective-permute-start.20 = (bf16[8,96,384]{2,1,0:T(8,128)(2,1)}, bf16[8,96,384]{2,1,0:T(8,128)(2,1)}, u32[]{:S(2)}, u32[]{:S(2)}) collective-permute-start(bf16[8,96,384]{2,1,0:T(8,128)(2,1)} %shard_map.99.own), channel_id=1, source_target_pairs={{0,3},{1,2},{2,1},{3,0},{4,7},{5,6},{6,5},{7,4},{8,11},{9,10},{10,... | collective-permute-start | bytes 1769480 | tf_op jit(solution)/shard_map/ppermute | solution.py:358
  97.9 15.5 %collective-permute-start.21 = (bf16[2,4,48,384]{3,2,1,0:T(8,128)(2,1)}, bf16[2,4,48,384]{3,2,1,0:T(8,128)(2,1)}, u32[]{:S(2)}, u32[]{:S(2)}) collective-permute-start(bf16[2,4,48,384]{3,2,1,0:T(8,128)(2,1)} %get-tuple-element.26), channel_id=1, source_target_pairs={{0,1},{1,0},{2,3},{3,2},{4,5},{5,4},{6,7},{7,6},{8,9},{9,8},{10,11... | collective-permute-start | bytes 884744 | tf_op jit(solution)/shard_map/ppermute | solution.py:325
  105.4 10.7 %collective-permute-start.7 = (bf16[2,6,48,384]{3,2,1,0:T(8,128)(2,1)}, bf16[2,6,48,384]{3,2,1,0:T(8,128)(2,1)}, u32[]{:S(2)}, u32[]{:S(2)}) collective-permute-start(bf16[2,6,48,384]{3,2,1,0:T(8,128)(2,1)} %get-tuple-element.22), channel_id=1, source_target_pairs={{0,1},{1,0},{2,3},{3,2},{4,5},{5,4},{6,7},{7,6},{8,9},{9,8},{10,11... | collective-permute-start | bytes 1327112 | tf_op jit(solution)/shard_map/ppermute | solution.py:325
  113.2 12.8 %copy-start = (f32[2,6,48,384]{3,2,1,0:T(8,128)S(1)}, f32[2,6,48,384]{3,2,1,0:T(8,128)}, u32[]{:S(2)}) copy-start(f32[2,6,48,384]{3,2,1,0:T(8,128)} %get-tuple-element.21) | copy-start | bytes 2654212
  113.2 4.6 %collective-permute-start.14 = (bf16[2,6,48,384]{3,2,1,0:T(8,128)(2,1)}, bf16[2,6,48,384]{3,2,1,0:T(8,128)(2,1)S(1)}, u32[]{:S(2)}, u32[]{:S(2)}) collective-permute-start(bf16[2,6,48,384]{3,2,1,0:T(8,128)(2,1)} %get-tuple-element.24), channel_id=1, source_target_pairs={{0,1},{1,0},{2,3},{3,2},{4,5},{5,4},{6,7},{7,6},{8,9},{9,8},{10,11... | collective-permute-start | bytes 1327112 | tf_op jit(solution)/shard_map/ppermute | solution.py:325
  114.5 15.6 %copy-start.1 = (f32[2,6,48,384]{3,2,1,0:T(8,128)S(1)}, f32[2,6,48,384]{3,2,1,0:T(8,128)}, u32[]{:S(2)}) copy-start(f32[2,6,48,384]{3,2,1,0:T(8,128)} %get-tuple-element.23) | copy-start | bytes 2654212
  114.5 16.1 %collective-permute-start.22 = (bf16[1,4,48,384]{3,2,1,0:T(8,128)(2,1)S(1)}, bf16[1,4,48,384]{3,2,1,0:T(8,128)(2,1)S(1)}, u32[]{:S(2)}, u32[]{:S(2)}) collective-permute-start(bf16[1,4,48,384]{3,2,1,0:T(8,128)(2,1)S(1)} %add_convert_fusion.6), channel_id=1, source_target_pairs={{0,2},{1,3},{2,0},{3,1},{4,6},{5,7},{6,4},{7,5},{8,10},{9,11},{10,... | collective-permute-start | bytes 442376 | tf_op jit(solution)/shard_map/ppermute | solution.py:325
  117.2 13.4 %copy-start.4 = (f32[2,4,48,384]{3,2,1,0:T(8,128)S(1)}, f32[2,4,48,384]{3,2,1,0:T(8,128)}, u32[]{:S(2)}) copy-start(f32[2,4,48,384]{3,2,1,0:T(8,128)} %get-tuple-element.25) | copy-start | bytes 1769476
  117.2 8.8 %collective-permute-start.8 = (bf16[1,6,48,384]{3,2,1,0:T(8,128)(2,1)S(1)}, bf16[1,6,48,384]{3,2,1,0:T(8,128)(2,1)S(1)}, u32[]{:S(2)}, u32[]{:S(2)}) collective-permute-start(bf16[1,6,48,384]{3,2,1,0:T(8,128)(2,1)S(1)} %add_convert_fusion.3), channel_id=1, source_target_pairs={{0,2},{1,3},{2,0},{3,1},{4,6},{5,7},{6,4},{7,5},{8,10},{9,11},{10,... | collective-permute-start | bytes 663560 | tf_op jit(solution)/shard_map/ppermute | solution.py:325
  118.8 11.3 %collective-permute-start.15 = (bf16[1,6,48,384]{3,2,1,0:T(8,128)(2,1)S(1)}, bf16[1,6,48,384]{3,2,1,0:T(8,128)(2,1)S(1)}, u32[]{:S(2)}, u32[]{:S(2)}) collective-permute-start(bf16[1,6,48,384]{3,2,1,0:T(8,128)(2,1)S(1)} %add_convert_fusion.1), channel_id=1, source_target_pairs={{0,2},{1,3},{2,0},{3,1},{4,6},{5,7},{6,4},{7,5},{8,10},{9,11},{10,... | collective-permute-start | bytes 663560 | tf_op jit(solution)/shard_map/ppermute | solution.py:325
  127.0 3.1 %copy-start.2 = (bf16[6,48,384]{2,1,0:T(8,128)(2,1)}, bf16[6,48,384]{2,1,0:T(8,128)(2,1)S(1)}, u32[]{:S(2)}) copy-start(bf16[6,48,384]{2,1,0:T(8,128)(2,1)S(1)} %fusion.refs_0_) | copy-start | bytes 663556
  127.1 7.1 %collective-permute-start.9 = (bf16[6,48,384]{2,1,0:T(8,128)(2,1)S(1)}, bf16[6,48,384]{2,1,0:T(8,128)(2,1)S(1)}, u32[]{:S(2)}, u32[]{:S(2)}) collective-permute-start(bf16[6,48,384]{2,1,0:T(8,128)(2,1)S(1)} %fusion.refs_0_), channel_id=1, source_target_pairs={{0,4},{4,0},{8,12},{12,8},{16,20},{20,16},{24,28},{28,24},{1,5},{5... | collective-permute-start | bytes 663560 | tf_op jit(solution)/shard_map/ppermute | solution.py:390
  130.2 4.0 %copy-start.3 = (bf16[6,48,384]{2,1,0:T(8,128)(2,1)}, bf16[6,48,384]{2,1,0:T(8,128)(2,1)S(1)}, u32[]{:S(2)}) copy-start(bf16[6,48,384]{2,1,0:T(8,128)(2,1)S(1)} %fusion.1.refs_2_) | copy-start | bytes 663556
  130.2 8.8 %collective-permute-start.16 = (bf16[6,48,384]{2,1,0:T(8,128)(2,1)S(1)}, bf16[6,48,384]{2,1,0:T(8,128)(2,1)}, u32[]{:S(2)}, u32[]{:S(2)}) collective-permute-start(bf16[6,48,384]{2,1,0:T(8,128)(2,1)S(1)} %fusion.1.refs_2_), channel_id=1, source_target_pairs={{0,4},{4,0},{8,12},{12,8},{16,20},{20,16},{24,28},{28,24},{1,5},{5... | collective-permute-start | bytes 663560 | tf_op jit(solution)/shard_map/ppermute | solution.py:390
  132.2 11.2 %collective-permute-start.23 = (bf16[4,48,384]{2,1,0:T(8,128)(2,1)}, bf16[4,48,384]{2,1,0:T(8,128)(2,1)}, u32[]{:S(2)}, u32[]{:S(2)}) collective-permute-start(bf16[4,48,384]{2,1,0:T(8,128)(2,1)} %fusion.2.mine), channel_id=1, source_target_pairs={{0,4},{4,0},{8,12},{12,8},{16,20},{20,16},{24,28},{28,24},{1,5},{5... | collective-permute-start | bytes 442376 | tf_op jit(solution)/shard_map/ppermute | solution.py:390
  134.2 0.7 copy-start.5
  146.4 7.4 %collective-permute-start.24 = (bf16[2,4,48,384]{3,2,1,0:T(8,128)(2,1)}, bf16[2,4,48,384]{3,2,1,0:T(8,128)(2,1)S(1)}, u32[]{:S(2)}, u32[]{:S(2)}) collective-permute-start(bf16[2,4,48,384]{3,2,1,0:T(8,128)(2,1)} %get-tuple-element.28), channel_id=1, source_target_pairs={{0,8},{4,12},{8,0},{12,4},{16,24},{20,28},{24,16},{28,20},{1,9},{5... | collective-permute-start | bytes 884744 | tf_op jit(solution)/shard_map/ppermute | solution.py:325
  155.6 7.6 %collective-permute-start.25 = (bf16[1,4,48,384]{3,2,1,0:T(8,128)(2,1)S(1)}, bf16[1,4,48,384]{3,2,1,0:T(8,128)(2,1)S(1)}, u32[]{:S(2)}, u32[]{:S(2)}) collective-permute-start(bf16[1,4,48,384]{3,2,1,0:T(8,128)(2,1)S(1)} %get-tuple-element.29), channel_id=1, source_target_pairs={{0,16},{4,20},{8,24},{12,28},{16,0},{20,4},{24,8},{28,12},{1,17},{... | collective-permute-start | bytes 442376 | tf_op jit(solution)/shard_map/ppermute | solution.py:325
  163.2 0.7 copy-start.6
where the time goes:
time: 166 us
  Pallas kernels  64.7 us (39%)
  waiting for transfers between devices  63.6 us (38%)
  starting transfers between devices  21.9 us (13%)
  other arithmetic  13.5 us (8%)
  local copies, waits for them, and re-layouts  2.02 us (1%)
    ppermute x7, waiting for transfers between devices, both(): near_b = lax.ppermute(block, 'col', pair_b)  40.6 us
    pallas_call x3, Pallas kernels, prolong_rows(): pl.pallas_call(functools.partial(prolong_kernel, first), grid=(count // s...  27.4 us
    pallas_call x3, Pallas kernels, coarse_rows(): pl.pallas_call(functools.partial(coarse_kernel, first), grid=(count // st...  20.4 us
    ppermute x8, waiting for transfers between devices, exchange(): terms.append(lax.ppermute(send, axis, flip(count, bit)))  18.6 us
    ppermute x8, starting transfers between devices, exchange(): terms.append(lax.ppermute(send, axis, flip(count, bit)))  8.64 us
    pallas_call x3, Pallas kernels, pack_rows(): pl.pallas_call(pack_kernel, grid=(count // step,), in_specs=[pl.BlockSpec...  7.63 us
    ppermute x7, starting transfers between devices, both(): near_b = lax.ppermute(block, 'col', pair_b)  7.16 us
    convert_element_type x4, other arithmetic, exchange(): send = sum((term[1::2].astype(jnp.float32) for term in terms)).astype(link)  5.09 us
  transfers between devices with their start and end apart: 26, of which 8 were waited for; matrix products, arithmetic and copies ran while one was open for 7% of the time, Pallas kernels for 36%

commit v1 on v0

--- a/solution.py
+++ b/solution.py
@@ -13,7 +13,7 @@
 G_DEV = 8
 OMEGA = 0.6
 
-EDGES = (0, 6, 12, 16)
+EDGES = (0, 2, 8, 13, 16)
 STEP = 2
 
 
@@ -222,20 +222,15 @@
     row = place[1]
     for side, source in enumerate(sides):
 
-        def one(m, carry, source=source, side=side):
+        def one(m, source=source, side=side):
             for u in range(2):
                 target = targets[side, 2 * (first + m) + u]
                 away = (target // G_DEV) ^ row
                 spot = jnp.where(away % 2 == 0, away // 2 * G_DEV + target % G_DEV, groups)
                 sums[spot] += source[m, :, u * window : (u + 1) * window].astype(jnp.float32)
-            return carry
-
-        count = source.shape[0]
-        if count <= 4:
-            for m in range(count):
-                one(m, 0)
-        else:
-            lax.fori_loop(0, count, one, 0)
+
+        for m in range(source.shape[0]):
+            one(m)
 
 
 def gather_kernel(starts, targets, place, *refs):
@@ -260,30 +255,29 @@
     )(targets, place, *flat)
 
 
-def split_kernel(first, targets, place, early, mine, theirs, keep, send, sums):
+def split_kernel(first, targets, place, early, mine, theirs, keep, odd, even, sums):
     sums[...] = early[...]
     add_groups(targets, place, (mine, theirs), first, sums)
     window = sums.shape[2]
     for h in range(keep.shape[0]):
+        send = odd if h % 2 else even
         for p in range(keep.shape[1]):
             for u in range(2):
                 lanes = slice(u * window, (u + 1) * window)
                 inner = 2 * p + u
                 keep[h, p, :, lanes] = sums[2 * h * G_DEV + inner]
-                send[h, p, :, lanes] = sums[(2 * h + 1) * G_DEV + inner].astype(send.dtype)
+                send[h // 2, p, :, lanes] = sums[(2 * h + 1) * G_DEV + inner].astype(send.dtype)
 
 
 def split_groups(targets, place, early, mine, theirs, first, rows):
     _, high, lanes = mine.shape
     shape = (rows // 4, G_DEV // 2, high, lanes)
+    half = jax.ShapeDtypeStruct((rows // 8,) + shape[1:], mine.dtype)
     return pl.pallas_call(
         functools.partial(split_kernel, first),
         in_specs=[SMEM, SMEM, VMEM, VMEM, VMEM],
-        out_specs=[VMEM, VMEM],
-        out_shape=[
-            jax.ShapeDtypeStruct(shape, jnp.float32),
-            jax.ShapeDtypeStruct(shape, mine.dtype),
-        ],
+        out_specs=[VMEM, VMEM, VMEM],
+        out_shape=[jax.ShapeDtypeStruct(shape, jnp.float32), half, half],
         scratch_shapes=[pltpu.VMEM(early.shape, jnp.float32)],
         compiler_params=PARAMS,
         cost_estimate=cost(early.size, 10 * early.size),
@@ -322,12 +316,20 @@
 def exchange(keep, send, axis, count, bit, link):
     terms = [keep]
     while True:
-        terms.append(lax.ppermute(send, axis, flip(count, bit)))
+        route = flip(count, bit)
+        if isinstance(send, tuple):
+            odd = lax.ppermute(send[0], axis, route)
+            even = lax.ppermute(send[1], axis, route)
+        else:
+            even = lax.ppermute(send, axis, route)
+            if 2 * bit < count:
+                even, odd = even[0::2], even[1::2]
         bit *= 2
         if bit == count:
-            return terms
-        send = sum(term[1::2].astype(jnp.float32) for term in terms).astype(link)
-        terms = [term[0::2] for term in terms]
+            return terms + [even]
+        send = sum(term[1::2].astype(jnp.float32) for term in terms)
+        send = (send + odd.astype(jnp.float32)).astype(link)
+        terms = [term[0::2] for term in terms] + [even]
 
 
 def on_device(
@@ -344,7 +346,7 @@
     columns, rows = lax.axis_size("col"), lax.axis_size("row")
     col, row = lax.axis_index("col"), lax.axis_index("row")
     assert columns & (columns - 1) == 0 and columns >= 2
-    assert rows & (rows - 1) == 0 and rows >= 4
+    assert rows & (rows - 1) == 0 and rows >= 8
     link = tentative.dtype
     groups = tentative.shape[0] // (2 * RQ)
 
@@ -390,8 +392,8 @@
         other = lax.ppermute(total, "row", flip(rows, 1))
         parts.append((total, other))
     early = gather_groups(targets, place, parts[:-1], [low for low, _ in spans[:-1]], rows)
-    keep, send = split_groups(targets, place, early, *parts[-1], spans[-1][0], rows)
-    return finish(*exchange(keep, send, "row", rows, 2, link))
+    keep, *send = split_groups(targets, place, early, *parts[-1], spans[-1][0], rows)
+    return finish(*exchange(keep, tuple(send), "row", rows, 2, link))
 
 
 def solution(mesh):

time: 166 us -> 151 us (0.910)
  waiting for transfers between devices: 63.6 us -> 29.4 us
  Pallas kernels: 64.7 us -> 73.2 us
  starting transfers between devices: 21.9 us -> 29.4 us
  other arithmetic: 13.5 us -> 15.5 us
    ppermute x7 -> x9, waiting for transfers between devices: 40.6 us -> 8.42 us  [both(): near_b = lax.ppermute(block, 'col', pair_b)]
    pallas_call x3 -> x4, Pallas kernels: 20.4 us -> 24.1 us  [coarse_rows(): pl.pallas_call(functools.partial(coarse_kernel, first), grid=(count // st...]
    pallas_call x3 -> x4, Pallas kernels: 7.63 us -> 11 us  [pack_rows(): pl.pallas_call(pack_kernel, grid=(count // step,), in_specs=[pl.BlockSpec...]
    ppermute x8 -> x11, waiting for transfers between devices: 18.6 us -> 15.7 us  [the longest x9 11.1 us: exchange(): even = lax.ppermute(send, axis, route)]
    pallas_call x3 -> x4, Pallas kernels: 27.4 us -> 30.2 us  [prolong_rows(): pl.pallas_call(functools.partial(prolong_kernel, first), grid=(count // s...]
    ppermute x7 -> x9, starting transfers between devices: 7.16 us -> 9.41 us  [both(): near_b = lax.ppermute(block, 'col', pair_b)]
    ppermute x8 -> x11, starting transfers between devices: 8.64 us -> 10.7 us  [the longest x9 8.67 us: exchange(): even = lax.ppermute(send, axis, route)]
    ppermute x3 -> x4, starting transfers between devices: 2.26 us -> 4.19 us  [on_device(): other = lax.ppermute(total, 'row', flip(rows, 1))]
  transfers between devices with their start and end apart: 26 -> 34, of which waited for: 8 -> 7; matrix products, arithmetic and copies ran while one was open for 7% -> 10% of each run, Pallas kernels for 36% -> 46%
where the time goes in v1:
time: 151 us; the launch traced here: 150 us
  Pallas kernels  73.2 us (48%)
  starting transfers between devices  29.4 us (19%)
  waiting for transfers between devices  29.4 us (19%)
  other arithmetic  15.5 us (10%)
  local copies, waits for them, and re-layouts  2.64 us (2%)
    pallas_call x4, Pallas kernels, prolong_rows(): pl.pallas_call(functools.partial(prolong_kernel, first), grid=(count // s...  30.2 us
    pallas_call x4, Pallas kernels, coarse_rows(): pl.pallas_call(functools.partial(coarse_kernel, first), grid=(count // st...  24.1 us
    ppermute x9, waiting for transfers between devices, exchange(): even = lax.ppermute(send, axis, route)  11.1 us
    pallas_call x4, Pallas kernels, pack_rows(): pl.pallas_call(pack_kernel, grid=(count // step,), in_specs=[pl.BlockSpec...  11 us
    ppermute x9, starting transfers between devices, both(): near_b = lax.ppermute(block, 'col', pair_b)  9.41 us
    ppermute x9, starting transfers between devices, exchange(): even = lax.ppermute(send, axis, route)  8.67 us
    ppermute x9, waiting for transfers between devices, both(): near_b = lax.ppermute(block, 'col', pair_b)  8.42 us
    convert_element_type x5, other arithmetic, exchange(): send = (send + odd.astype(jnp.float32)).astype(link)  6.19 us
  transfers between devices with their start and end apart: 34, of which 7 were waited for; matrix products, arithmetic and copies ran while one was open for 10% of the time, Pallas kernels for 46%

profile of v1, /device:TPU:0, one launch (start us, length us, event | category | flops | bytes accessed | tf_op | source)
XLA Modules:
  0.0 150.2 jit_solution(8535118698858746740)
XLA Ops:
  0.0 2.4 %collective-permute-start.1 = (s32[64]{0:T(128)}, s32[64]{0:T(128)}, u32[]{:S(2)}, u32[]{:S(2)}) collective-permute-start(s32[64]{0:T(128)} %param.15), channel_id=1, source_target_pairs={{0,3},{1,2},{2,1},{3,0},{4,7},{5,6},{6,5},{7,4},{8,11},{9,10},{10,... | collective-permute-start | bytes 776 | tf_op jit(solution)/shard_map/ppermute | solution.py:360
  2.4 0.7 collective-permute-start
  3.1 1.7 %shard_map.91 = bf16[2,96,384]{2,1,0:T(8,128)(2,1)} custom-call(bf16[64,96,96]{2,1,0:T(8,128)(2,1)} %own.7), custom_call_target="tpu_custom_call" | custom-call | bytes 368640 | tf_op jit(solution)/shard_map/pallas_call | solution.py:45
  4.9 1.2 bitcast_add_fusion
  6.1 2.1 %collective-permute-start.2 = (s32[32]{0:T(128)}, s32[32]{0:T(128)}, u32[]{:S(2)}, u32[]{:S(2)}) collective-permute-start(s32[32]{0:T(128)} %bitcast_add_fusion), channel_id=1, source_target_pairs={{0,4},{4,0},{8,12},{12,8},{16,20},{20,16},{24,28},{28,24},{1,5},{5... | collective-permute-start | bytes 392 | tf_op jit(solution)/shard_map/ppermute | solution.py:371
  8.2 1.3 fusion.7.table
  9.5 3.7 %shard_map.97 = bf16[5,96,384]{2,1,0:T(8,128)(2,1)} custom-call(bf16[64,96,96]{2,1,0:T(8,128)(2,1)} %own.7), custom_call_target="tpu_custom_call" | custom-call | bytes 921600 | tf_op jit(solution)/shard_map/pallas_call | solution.py:45
  13.2 2.7 %shard_map.101 = bf16[3,96,384]{2,1,0:T(8,128)(2,1)} custom-call(bf16[64,96,96]{2,1,0:T(8,128)(2,1)} %own.7), custom_call_target="tpu_custom_call" | custom-call | bytes 552960 | tf_op jit(solution)/shard_map/pallas_call | solution.py:45
  15.9 1.6 %collective-permute-start.18 = (bf16[5,96,384]{2,1,0:T(8,128)(2,1)}, bf16[5,96,384]{2,1,0:T(8,128)(2,1)}, u32[]{:S(2)}, u32[]{:S(2)}) collective-permute-start(bf16[5,96,384]{2,1,0:T(8,128)(2,1)} %shard_map.97), channel_id=1, source_target_pairs={{0,3},{1,2},{2,1},{3,0},{4,7},{5,6},{6,5},{7,4},{8,11},{9,10},{10,... | collective-permute-start | bytes 1105928 | tf_op jit(solution)/shard_map/ppermute | solution.py:360
  18.1 2.9 %shard_map.94 = bf16[6,96,384]{2,1,0:T(8,128)(2,1)} custom-call(bf16[64,96,96]{2,1,0:T(8,128)(2,1)} %own.7), custom_call_target="tpu_custom_call" | custom-call | bytes 1105920 | tf_op jit(solution)/shard_map/pallas_call | solution.py:45
  21.5 1.2 pad_add_fusion.1.targets
  22.8 1.6 %collective-permute-start.11 = (bf16[6,96,384]{2,1,0:T(8,128)(2,1)}, bf16[6,96,384]{2,1,0:T(8,128)(2,1)}, u32[]{:S(2)}, u32[]{:S(2)}) collective-permute-start(bf16[6,96,384]{2,1,0:T(8,128)(2,1)} %shard_map.94), channel_id=1, source_target_pairs={{0,3},{1,2},{2,1},{3,0},{4,7},{5,6},{6,5},{7,4},{8,11},{9,10},{10,... | collective-permute-start | bytes 1327112 | tf_op jit(solution)/shard_map/ppermute | solution.py:360
  24.4 1.3 pad_add_fusion.labels
  25.6 4.7 %shard_map.92.own = bf16[4,96,384]{2,1,0:T(8,128)(2,1)} custom-call(s32[4,64]{1,0:T(4,128)} %fusion.7.table, s32[3,64]{1,0:T(4,128)} %pad_add_fusion.labels, bf16[64,4,96,96]{3,2,1,0:T(8,128)(2,1)} %off.15, bf16[64,96,96]{2,1,0:T(8,128)(2,1)} %diag.15, bf16[64,96,96]{2,1,0:T(8,128)(2,1)} %inverse.7, bf16[64,96,96]{2,1,0:T(8,128)(2,1)} %own.7, ...), custom_call_target="tpu_custom_call" | custom-call | flops 169869312 | bytes 1622016 | tf_op jit(solution)/shard_map/pallas_call | solution.py:112
  30.4 1.2 collective-permute-done.25.near_b
  31.5 1.1 collective-permute-start.5
  32.6 6.3 %shard_map.102.own = bf16[6,96,384]{2,1,0:T(8,128)(2,1)} custom-call(s32[4,64]{1,0:T(4,128)} %fusion.7.table, s32[3,64]{1,0:T(4,128)} %pad_add_fusion.labels, bf16[64,4,96,96]{3,2,1,0:T(8,128)(2,1)} %off.15, bf16[64,96,96]{2,1,0:T(8,128)(2,1)} %diag.15, bf16[64,96,96]{2,1,0:T(8,128)(2,1)} %inverse.7, bf16[64,96,96]{2,1,0:T(8,128)(2,1)} %own.7, ...), custom_call_target="tpu_custom_call" | custom-call | flops 254803968 | bytes 2433024 | tf_op jit(solution)/shard_map/pallas_call | solution.py:112
  38.9 1.6 %collective-permute-start.27 = (bf16[6,96,384]{2,1,0:T(8,128)(2,1)}, bf16[6,96,384]{2,1,0:T(8,128)(2,1)}, u32[]{:S(2)}, u32[]{:S(2)}) collective-permute-start(bf16[6,96,384]{2,1,0:T(8,128)(2,1)} %shard_map.102.own), channel_id=1, source_target_pairs={{0,3},{1,2},{2,1},{3,0},{4,7},{5,6},{6,5},{7,4},{8,11},{9,10},{10,... | collective-permute-start | bytes 1327112 | tf_op jit(solution)/shard_map/ppermute | solution.py:360
  40.8 9.3 %shard_map.98.own = bf16[10,96,384]{2,1,0:T(8,128)(2,1)} custom-call(s32[4,64]{1,0:T(4,128)} %fusion.7.table, s32[3,64]{1,0:T(4,128)} %pad_add_fusion.labels, bf16[64,4,96,96]{3,2,1,0:T(8,128)(2,1)} %off.15, bf16[64,96,96]{2,1,0:T(8,128)(2,1)} %diag.15, bf16[64,96,96]{2,1,0:T(8,128)(2,1)} %inverse.7, bf16[64,96,96]{2,1,0:T(8,128)(2,1)} %own.7, ...), custom_call_target="tpu_custom_call" | custom-call | flops 424673280 | bytes 4055040 | tf_op jit(solution)/shard_map/pallas_call | solution.py:112
  50.5 1.2 collective-permute-start.20
  51.7 10.0 %shard_map.95.own = bf16[12,96,384]{2,1,0:T(8,128)(2,1)} custom-call(s32[4,64]{1,0:T(4,128)} %fusion.7.table, s32[3,64]{1,0:T(4,128)} %pad_add_fusion.labels, bf16[64,4,96,96]{3,2,1,0:T(8,128)(2,1)} %off.15, bf16[64,96,96]{2,1,0:T(8,128)(2,1)} %diag.15, bf16[64,96,96]{2,1,0:T(8,128)(2,1)} %inverse.7, bf16[64,96,96]{2,1,0:T(8,128)(2,1)} %own.7, ...), custom_call_target="tpu_custom_call" | custom-call | flops 509607936 | bytes 4866048 | tf_op jit(solution)/shard_map/pallas_call | solution.py:112
  62.4 5.2 %shard_map.103 = (f32[2,3,48,384]{3,2,1,0:T(8,128)}, bf16[2,3,48,384]{3,2,1,0:T(8,128)(2,1)}) custom-call(s32[4,64]{1,0:T(4,128)} %fusion.7.table, s32[2]{0:T(128)} %pad_add_fusion.2.place, bf16[64,4,96,96]{3,2,1,0:T(8,128)(2,1)} %off.15, bf16[64,96,96]{2,1,0:T(8,128)(2,1)} %diag.15, bf16[6,96,384]{2,1,0:T(8,128)(2,1)} %shard_map.102.own, ...), custom_call_target="tpu_custom_call" | custom-call | flops 297271296 | bytes 3538944 | tf_op jit(solution)/shard_map/pallas_call | solution.py:189
  68.1 3.9 %shard_map.93 = (f32[2,2,48,384]{3,2,1,0:T(8,128)}, bf16[2,2,48,384]{3,2,1,0:T(8,128)(2,1)}) custom-call(s32[4,64]{1,0:T(4,128)} %fusion.7.table, s32[2]{0:T(128)} %pad_add_fusion.2.place, bf16[64,4,96,96]{3,2,1,0:T(8,128)(2,1)} %off.15, bf16[64,96,96]{2,1,0:T(8,128)(2,1)} %diag.15, bf16[4,96,384]{2,1,0:T(8,128)(2,1)} %shard_map.92.own, ...), custom_call_target="tpu_custom_call" | custom-call | flops 198180864 | bytes 2359296 | tf_op jit(solution)/shard_map/pallas_call | solution.py:189
  72.1 1.7 %add_convert_fusion.6 = bf16[1,3,48,384]{3,2,1,0:T(8,128)(2,1)} fusion(f32[2,3,48,384]{3,2,1,0:T(8,128)} %get-tuple-element.30, bf16[2,3,48,384]{3,2,1,0:T(8,128)(2,1)} %collective-permute-done.28), kind=kLoop, calls=%fused_computation.7 | loop fusion | flops 165888 | bytes 442368 | tf_op jit(solution)/shard_map/convert_element_type | solution.py:331
  73.8 1.5 %collective-permute-start.29 = (bf16[1,3,48,384]{3,2,1,0:T(8,128)(2,1)}, bf16[1,3,48,384]{3,2,1,0:T(8,128)(2,1)}, u32[]{:S(2)}, u32[]{:S(2)}) collective-permute-start(bf16[1,3,48,384]{3,2,1,0:T(8,128)(2,1)} %add_convert_fusion.6), channel_id=1, source_target_pairs={{0,2},{1,3},{2,0},{3,1},{4,6},{5,7},{6,4},{7,5},{8,10},{9,11},{10,... | collective-permute-start | bytes 331784 | tf_op jit(solution)/shard_map/ppermute | solution.py:324
  75.3 7.5 %shard_map.99 = (f32[2,5,48,384]{3,2,1,0:T(8,128)}, bf16[2,5,48,384]{3,2,1,0:T(8,128)(2,1)}) custom-call(s32[4,64]{1,0:T(4,128)} %fusion.7.table, s32[2]{0:T(128)} %pad_add_fusion.2.place, bf16[64,4,96,96]{3,2,1,0:T(8,128)(2,1)} %off.15, bf16[64,96,96]{2,1,0:T(8,128)(2,1)} %diag.15, bf16[10,96,384]{2,1,0:T(8,128)(2,1)} %shard_map.98.own, ...), custom_call_target="tpu_custom_call" | custom-call | flops 495452160 | bytes 5898240 | tf_op jit(solution)/shard_map/pallas_call | solution.py:189
  83.0 1.6 %add_convert_fusion.8 = bf16[1,2,48,384]{3,2,1,0:T(8,128)(2,1)} fusion(f32[2,2,48,384]{3,2,1,0:T(8,128)} %get-tuple-element.24, bf16[2,2,48,384]{3,2,1,0:T(8,128)(2,1)} %collective-permute-done.7), kind=kLoop, calls=%fused_computation.10 | loop fusion | flops 110592 | bytes 294912 | tf_op jit(solution)/shard_map/convert_element_type | solution.py:331
  85.3 7.2 %collective-permute-done.13.near_b = bf16[12,96,384]{2,1,0:T(8,128)(2,1)} collective-permute-done((bf16[12,96,384]{2,1,0:T(8,128)(2,1)}, bf16[12,96,384]{2,1,0:T(8,128)(2,1)}, u32[]{:S(2)}, u32[]{:S(2)}) %collective-permute-start.13) | collective-permute-done | bytes 884768 | tf_op jit(solution)/shard_map/ppermute | solution.py:360
  92.5 7.4 %shard_map.96 = (f32[2,6,48,384]{3,2,1,0:T(8,128)}, bf16[2,6,48,384]{3,2,1,0:T(8,128)(2,1)}) custom-call(s32[4,64]{1,0:T(4,128)} %fusion.7.table, s32[2]{0:T(128)} %pad_add_fusion.2.place, bf16[64,4,96,96]{3,2,1,0:T(8,128)(2,1)} %off.15, bf16[64,96,96]{2,1,0:T(8,128)(2,1)} %diag.15, bf16[12,96,384]{2,1,0:T(8,128)(2,1)} %shard_map.95.own, ...), custom_call_target="tpu_custom_call" | custom-call | flops 594542592 | bytes 7077888 | tf_op jit(solution)/shard_map/pallas_call | solution.py:189
  99.9 0.8 collective-permute-start.14
  100.8 1.7 %fusion.2.mine = bf16[3,48,384]{2,1,0:T(8,128)(2,1)} fusion(bf16[1,3,48,384]{3,2,1,0:T(8,128)(2,1)} %collective-permute-done.29, f32[2,3,48,384]{3,2,1,0:T(8,128)} %get-tuple-element.30, bf16[2,3,48,384]{3,2,1,0:T(8,128)(2,1)} %collective-permute-done.28), kind=kLoop, calls=%fused_computation.11 | loop fusion | flops 276480 | bytes 552960 | tf_op jit(solution)/shard_map/convert_element_type | solution.py:391
  102.7 1.1 add_convert_fusion.3
  103.8 2.0 %collective-permute-start.22 = (bf16[1,5,48,384]{3,2,1,0:T(8,128)(2,1)S(1)}, bf16[1,5,48,384]{3,2,1,0:T(8,128)(2,1)S(1)}, u32[]{:S(2)}, u32[]{:S(2)}) collective-permute-start(bf16[1,5,48,384]{3,2,1,0:T(8,128)(2,1)S(1)} %add_convert_fusion.3), channel_id=1, source_target_pairs={{0,2},{1,3},{2,0},{3,1},{4,6},{5,7},{6,4},{7,5},{8,10},{9,11},{10,... | collective-permute-start | bytes 552968 | tf_op jit(solution)/shard_map/ppermute | solution.py:324
  106.0 5.3 %collective-permute-done.22 = bf16[1,5,48,384]{3,2,1,0:T(8,128)(2,1)S(1)} collective-permute-done((bf16[1,5,48,384]{3,2,1,0:T(8,128)(2,1)S(1)}, bf16[1,5,48,384]{3,2,1,0:T(8,128)(2,1)S(1)}, u32[]{:S(2)}, u32[]{:S(2)}) %collective-permute-start.22) | collective-permute-done | bytes 184352 | tf_op jit(solution)/shard_map/ppermute | solution.py:324
  111.3 1.0 fusion.1.refs_4_
  112.3 1.9 %collective-permute-start.23 = (bf16[5,48,384]{2,1,0:T(8,128)(2,1)S(1)}, bf16[5,48,384]{2,1,0:T(8,128)(2,1)S(1)}, u32[]{:S(2)}, u32[]{:S(2)}) collective-permute-start(bf16[5,48,384]{2,1,0:T(8,128)(2,1)S(1)} %fusion.1.refs_4_), channel_id=1, source_target_pairs={{0,4},{4,0},{8,12},{12,8},{16,20},{20,16},{24,28},{28,24},{1,5},{5... | collective-permute-start | bytes 552968 | tf_op jit(solution)/shard_map/ppermute | solution.py:392
  114.3 0.8 collective-permute-done.15
  115.9 1.7 %collective-permute-start.16 = (bf16[6,48,384]{2,1,0:T(8,128)(2,1)S(1)}, bf16[6,48,384]{2,1,0:T(8,128)(2,1)}, u32[]{:S(2)}, u32[]{:S(2)}) collective-permute-start(bf16[6,48,384]{2,1,0:T(8,128)(2,1)S(1)} %fusion.refs_2_), channel_id=1, source_target_pairs={{0,4},{4,0},{8,12},{12,8},{16,20},{20,16},{24,28},{28,24},{1,5},{5... | collective-permute-start | bytes 663560 | tf_op jit(solution)/shard_map/ppermute | solution.py:392
  117.6 1.0 fusion.3.refs_0_
  119.0 5.3 %collective-permute-done.9.refs_1_ = bf16[2,48,384]{2,1,0:T(8,128)(2,1)S(1)} collective-permute-done((bf16[2,48,384]{2,1,0:T(8,128)(2,1)S(1)}, bf16[2,48,384]{2,1,0:T(8,128)(2,1)S(1)}, u32[]{:S(2)}, u32[]{:S(2)}) %collective-permute-start.9) | collective-permute-done | bytes 73760 | tf_op jit(solution)/shard_map/ppermute | solution.py:392
  125.6 3.2 %shard_map.100.early = f32[33,48,192]{2,1,0:T(8,128)} custom-call(s32[2,32]{1,0:T(2,128)} %pad_add_fusion.1.targets, s32[2]{0:T(128)} %pad_add_fusion.2.place, bf16[2,48,384]{2,1,0:T(8,128)(2,1)} %copy-done.5, bf16[2,48,384]{2,1,0:T(8,128)(2,1)} %copy-done.9, bf16[6,48,384]{2,1,0:T(8,128)(2,1)} %copy-done.1, ...), custom_call_target="tpu_custom_call" | custom-call | flops 479232 | bytes 1916928 | tf_op jit(solution)/shard_map/pallas_call | solution.py:248
  128.7 2.8 %shard_map.104 = (f32[2,4,48,384]{3,2,1,0:T(8,128)}, bf16[1,4,48,384]{3,2,1,0:T(8,128)(2,1)}, bf16[1,4,48,384]{3,2,1,0:T(8,128)(2,1)}) custom-call(s32[2,32]{1,0:T(2,128)} %pad_add_fusion.1.targets, s32[2]{0:T(128)} %pad_add_fusion.2.place, f32[33,48,192]{2,1,0:T(8,128)} %shard_map.100.early, bf16[3,48,384]{2,1,0:T(8,128)(2,1)} %fusion.2.mine, ...), custom_call_target="tpu_custom_call" | custom-call | flops 304128 | bytes 3041280 | tf_op jit(solution)/shard_map/pallas_call | solution.py:276
  131.6 2.0 %collective-permute-start.32 = (bf16[1,4,48,384]{3,2,1,0:T(8,128)(2,1)}, bf16[1,4,48,384]{3,2,1,0:T(8,128)(2,1)S(1)}, u32[]{:S(2)}, u32[]{:S(2)}) collective-permute-start(bf16[1,4,48,384]{3,2,1,0:T(8,128)(2,1)} %get-tuple-element.34), channel_id=1, source_target_pairs={{0,8},{4,12},{8,0},{12,4},{16,24},{20,28},{24,16},{28,20},{1,9},{5... | collective-permute-start | bytes 442376 | tf_op jit(solution)/shard_map/ppermute | solution.py:321
  133.6 4.6 %collective-permute-done.32 = bf16[1,4,48,384]{3,2,1,0:T(8,128)(2,1)S(1)} collective-permute-done((bf16[1,4,48,384]{3,2,1,0:T(8,128)(2,1)}, bf16[1,4,48,384]{3,2,1,0:T(8,128)(2,1)S(1)}, u32[]{:S(2)}, u32[]{:S(2)}) %collective-permute-start.32) | collective-permute-done | bytes 147488 | tf_op jit(solution)/shard_map/ppermute | solution.py:321
  138.2 1.8 %add_convert_fusion.4 = (bf16[1,4,48,384]{3,2,1,0:T(8,128)(2,1)S(1)}, f32[1,4,48,384]{3,2,1,0:T(8,128)}) fusion(bf16[1,4,48,384]{3,2,1,0:T(8,128)(2,1)S(1)} %collective-permute-done.32, f32[2,4,48,384]{3,2,1,0:T(8,128)} %get-tuple-element.32), kind=kLoop, calls=%fused_computation.4 | loop fusion | flops 221184 | bytes 1179648 | tf_op jit(solution)/shard_map/convert_element_type | solution.py:331
  140.0 2.8 %collective-permute-start.33 = (bf16[1,4,48,384]{3,2,1,0:T(8,128)(2,1)S(1)}, bf16[1,4,48,384]{3,2,1,0:T(8,128)(2,1)S(1)}, u32[]{:S(2)}, u32[]{:S(2)}) collective-permute-start(bf16[1,4,48,384]{3,2,1,0:T(8,128)(2,1)S(1)} %get-tuple-element.35), channel_id=1, source_target_pairs={{0,16},{4,20},{8,24},{12,28},{16,0},{20,4},{24,8},{28,12},{1,17},{... | collective-permute-start | bytes 442376 | tf_op jit(solution)/shard_map/ppermute | solution.py:324
  142.8 4.9 %collective-permute-done.33.refs_1_ = bf16[1,4,48,384]{3,2,1,0:T(8,128)(2,1)S(1)} collective-permute-done((bf16[1,4,48,384]{3,2,1,0:T(8,128)(2,1)S(1)}, bf16[1,4,48,384]{3,2,1,0:T(8,128)(2,1)S(1)}, u32[]{:S(2)}, u32[]{:S(2)}) %collective-permute-start.33) | collective-permute-done | bytes 147488 | tf_op jit(solution)/shard_map/ppermute | solution.py:324
  148.3 1.9 %shard_map.105 = f32[8,48,192]{2,1,0:T(8,128)} custom-call(f32[1,4,48,384]{3,2,1,0:T(8,128)} %get-tuple-element.36.keep_ref, bf16[1,4,48,384]{3,2,1,0:T(8,128)(2,1)} %copy-done.7, bf16[1,4,48,384]{3,2,1,0:T(8,128)(2,1)} %copy-done.8), custom_call_target="tpu_custom_call" | custom-call | flops 73728 | bytes 737280 | tf_op jit(solution)/shard_map/pallas_call | solution.py:301
  (69 shorter events, 7.7 us)
Async XLA Ops:
  0.0 15.8 %collective-permute-start.1 = (s32[64]{0:T(128)}, s32[64]{0:T(128)}, u32[]{:S(2)}, u32[]{:S(2)}) collective-permute-start(s32[64]{0:T(128)} %param.15), channel_id=1, source_target_pairs={{0,3},{1,2},{2,1},{3,0},{4,7},{5,6},{6,5},{7,4},{8,11},{9,10},{10,... | collective-permute-start | bytes 776 | tf_op jit(solution)/shard_map/ppermute | solution.py:360
  2.4 15.0 %collective-permute-start = (s32[64]{0:T(128)}, s32[64]{0:T(128)}, u32[]{:S(2)}, u32[]{:S(2)}) collective-permute-start(s32[64]{0:T(128)} %param.15), channel_id=1, source_target_pairs={{0,1},{1,0},{2,3},{3,2},{4,5},{5,4},{6,7},{7,6},{8,9},{9,8},{10,11... | collective-permute-start | bytes 776 | tf_op jit(solution)/shard_map/ppermute | solution.py:361
  4.8 16.2 %collective-permute-start.3 = (bf16[2,96,384]{2,1,0:T(8,128)(2,1)}, bf16[2,96,384]{2,1,0:T(8,128)(2,1)}, u32[]{:S(2)}, u32[]{:S(2)}) collective-permute-start(bf16[2,96,384]{2,1,0:T(8,128)(2,1)} %shard_map.91), channel_id=1, source_target_pairs={{0,1},{1,0},{2,3},{3,2},{4,5},{5,4},{6,7},{7,6},{8,9},{9,8},{10,11... | collective-permute-start | bytes 442376 | tf_op jit(solution)/shard_map/ppermute | solution.py:361
  4.8 17.9 %collective-permute-start.4 = (bf16[2,96,384]{2,1,0:T(8,128)(2,1)}, bf16[2,96,384]{2,1,0:T(8,128)(2,1)}, u32[]{:S(2)}, u32[]{:S(2)}) collective-permute-start(bf16[2,96,384]{2,1,0:T(8,128)(2,1)} %shard_map.91), channel_id=1, source_target_pairs={{0,3},{1,2},{2,1},{3,0},{4,7},{5,6},{6,5},{7,4},{8,11},{9,10},{10,... | collective-permute-start | bytes 442376 | tf_op jit(solution)/shard_map/ppermute | solution.py:360
  6.1 9.8 %collective-permute-start.2 = (s32[32]{0:T(128)}, s32[32]{0:T(128)}, u32[]{:S(2)}, u32[]{:S(2)}) collective-permute-start(s32[32]{0:T(128)} %bitcast_add_fusion), channel_id=1, source_target_pairs={{0,4},{4,0},{8,12},{12,8},{16,20},{20,16},{24,28},{28,24},{1,5},{5... | collective-permute-start | bytes 392 | tf_op jit(solution)/shard_map/ppermute | solution.py:371
  15.8 23.0 %collective-permute-start.17 = (bf16[5,96,384]{2,1,0:T(8,128)(2,1)}, bf16[5,96,384]{2,1,0:T(8,128)(2,1)}, u32[]{:S(2)}, u32[]{:S(2)}) collective-permute-start(bf16[5,96,384]{2,1,0:T(8,128)(2,1)} %shard_map.97), channel_id=1, source_target_pairs={{0,1},{1,0},{2,3},{3,2},{4,5},{5,4},{6,7},{7,6},{8,9},{9,8},{10,11... | collective-permute-start | bytes 1105928 | tf_op jit(solution)/shard_map/ppermute | solution.py:361
  15.9 23.1 %collective-permute-start.18 = (bf16[5,96,384]{2,1,0:T(8,128)(2,1)}, bf16[5,96,384]{2,1,0:T(8,128)(2,1)}, u32[]{:S(2)}, u32[]{:S(2)}) collective-permute-start(bf16[5,96,384]{2,1,0:T(8,128)(2,1)} %shard_map.97), channel_id=1, source_target_pairs={{0,3},{1,2},{2,1},{3,0},{4,7},{5,6},{6,5},{7,4},{8,11},{9,10},{10,... | collective-permute-start | bytes 1105928 | tf_op jit(solution)/shard_map/ppermute | solution.py:360
  17.5 5.3 %collective-permute-start.24 = (bf16[3,96,384]{2,1,0:T(8,128)(2,1)}, bf16[3,96,384]{2,1,0:T(8,128)(2,1)}, u32[]{:S(2)}, u32[]{:S(2)}) collective-permute-start(bf16[3,96,384]{2,1,0:T(8,128)(2,1)} %shard_map.101), channel_id=1, source_target_pairs={{0,1},{1,0},{2,3},{3,2},{4,5},{5,4},{6,7},{7,6},{8,9},{9,8},{10,11... | collective-permute-start | bytes 663560 | tf_op jit(solution)/shard_map/ppermute | solution.py:361
  21.0 10.5 %collective-permute-start.25 = (bf16[3,96,384]{2,1,0:T(8,128)(2,1)}, bf16[3,96,384]{2,1,0:T(8,128)(2,1)}, u32[]{:S(2)}, u32[]{:S(2)}) collective-permute-start(bf16[3,96,384]{2,1,0:T(8,128)(2,1)} %shard_map.101), channel_id=1, source_target_pairs={{0,3},{1,2},{2,1},{3,0},{4,7},{5,6},{6,5},{7,4},{8,11},{9,10},{10,... | collective-permute-start | bytes 663560 | tf_op jit(solution)/shard_map/ppermute | solution.py:360
  22.7 27.3 %collective-permute-start.10 = (bf16[6,96,384]{2,1,0:T(8,128)(2,1)}, bf16[6,96,384]{2,1,0:T(8,128)(2,1)}, u32[]{:S(2)}, u32[]{:S(2)}) collective-permute-start(bf16[6,96,384]{2,1,0:T(8,128)(2,1)} %shard_map.94), channel_id=1, source_target_pairs={{0,1},{1,0},{2,3},{3,2},{4,5},{5,4},{6,7},{7,6},{8,9},{9,8},{10,11... | collective-permute-start | bytes 1327112 | tf_op jit(solution)/shard_map/ppermute | solution.py:361
  22.8 27.7 %collective-permute-start.11 = (bf16[6,96,384]{2,1,0:T(8,128)(2,1)}, bf16[6,96,384]{2,1,0:T(8,128)(2,1)}, u32[]{:S(2)}, u32[]{:S(2)}) collective-permute-start(bf16[6,96,384]{2,1,0:T(8,128)(2,1)} %shard_map.94), channel_id=1, source_target_pairs={{0,3},{1,2},{2,1},{3,0},{4,7},{5,6},{6,5},{7,4},{8,11},{9,10},{10,... | collective-permute-start | bytes 1327112 | tf_op jit(solution)/shard_map/ppermute | solution.py:360
  31.5 9.0 %collective-permute-start.5 = (bf16[4,96,384]{2,1,0:T(8,128)(2,1)}, bf16[4,96,384]{2,1,0:T(8,128)(2,1)}, u32[]{:S(2)}, u32[]{:S(2)}) collective-permute-start(bf16[4,96,384]{2,1,0:T(8,128)(2,1)} %shard_map.92.own), channel_id=1, source_target_pairs={{0,1},{1,0},{2,3},{3,2},{4,5},{5,4},{6,7},{7,6},{8,9},{9,8},{10,11... | collective-permute-start | bytes 884744 | tf_op jit(solution)/shard_map/ppermute | solution.py:361
  38.9 22.9 %collective-permute-start.26 = (bf16[6,96,384]{2,1,0:T(8,128)(2,1)}, bf16[6,96,384]{2,1,0:T(8,128)(2,1)}, u32[]{:S(2)}, u32[]{:S(2)}) collective-permute-start(bf16[6,96,384]{2,1,0:T(8,128)(2,1)} %shard_map.102.own), channel_id=1, source_target_pairs={{0,1},{1,0},{2,3},{3,2},{4,5},{5,4},{6,7},{7,6},{8,9},{9,8},{10,11... | collective-permute-start | bytes 1327112 | tf_op jit(solution)/shard_map/ppermute | solution.py:361
  38.9 23.3 %collective-permute-start.27 = (bf16[6,96,384]{2,1,0:T(8,128)(2,1)}, bf16[6,96,384]{2,1,0:T(8,128)(2,1)}, u32[]{:S(2)}, u32[]{:S(2)}) collective-permute-start(bf16[6,96,384]{2,1,0:T(8,128)(2,1)} %shard_map.102.own), channel_id=1, source_target_pairs={{0,3},{1,2},{2,1},{3,0},{4,7},{5,6},{6,5},{7,4},{8,11},{9,10},{10,... | collective-permute-start | bytes 1327112 | tf_op jit(solution)/shard_map/ppermute | solution.py:360
  40.6 27.1 %collective-permute-start.6 = (bf16[4,96,384]{2,1,0:T(8,128)(2,1)}, bf16[4,96,384]{2,1,0:T(8,128)(2,1)}, u32[]{:S(2)}, u32[]{:S(2)}) collective-permute-start(bf16[4,96,384]{2,1,0:T(8,128)(2,1)} %shard_map.92.own), channel_id=1, source_target_pairs={{0,3},{1,2},{2,1},{3,0},{4,7},{5,6},{6,5},{7,4},{8,11},{9,10},{10,... | collective-permute-start | bytes 884744 | tf_op jit(solution)/shard_map/ppermute | solution.py:360
  50.0 23.8 %collective-permute-start.19 = (bf16[10,96,384]{2,1,0:T(8,128)(2,1)}, bf16[10,96,384]{2,1,0:T(8,128)(2,1)}, u32[]{:S(2)}, u32[]{:S(2)}) collective-permute-start(bf16[10,96,384]{2,1,0:T(8,128)(2,1)} %shard_map.98.own), channel_id=1, source_target_pairs={{0,1},{1,0},{2,3},{3,2},{4,5},{5,4},{6,7},{7,6},{8,9},{9,8},{10,11... | collective-permute-start | bytes 2211848 | tf_op jit(solution)/shard_map/ppermute | solution.py:361
  50.5 24.8 %collective-permute-start.20 = (bf16[10,96,384]{2,1,0:T(8,128)(2,1)}, bf16[10,96,384]{2,1,0:T(8,128)(2,1)}, u32[]{:S(2)}, u32[]{:S(2)}) collective-permute-start(bf16[10,96,384]{2,1,0:T(8,128)(2,1)} %shard_map.98.own), channel_id=1, source_target_pairs={{0,3},{1,2},{2,1},{3,0},{4,7},{5,6},{6,5},{7,4},{8,11},{9,10},{10,... | collective-permute-start | bytes 2211848 | tf_op jit(solution)/shard_map/ppermute | solution.py:360
  61.7 23.5 %collective-permute-start.12 = (bf16[12,96,384]{2,1,0:T(8,128)(2,1)}, bf16[12,96,384]{2,1,0:T(8,128)(2,1)}, u32[]{:S(2)}, u32[]{:S(2)}) collective-permute-start(bf16[12,96,384]{2,1,0:T(8,128)(2,1)} %shard_map.95.own), channel_id=1, source_target_pairs={{0,1},{1,0},{2,3},{3,2},{4,5},{5,4},{6,7},{7,6},{8,9},{9,8},{10,11... | collective-permute-start | bytes 2654216 | tf_op jit(solution)/shard_map/ppermute | solution.py:361
  62.2 30.3 %collective-permute-start.13 = (bf16[12,96,384]{2,1,0:T(8,128)(2,1)}, bf16[12,96,384]{2,1,0:T(8,128)(2,1)}, u32[]{:S(2)}, u32[]{:S(2)}) collective-permute-start(bf16[12,96,384]{2,1,0:T(8,128)(2,1)} %shard_map.95.own), channel_id=1, source_target_pairs={{0,3},{1,2},{2,1},{3,0},{4,7},{5,6},{6,5},{7,4},{8,11},{9,10},{10,... | collective-permute-start | bytes 2654216 | tf_op jit(solution)/shard_map/ppermute | solution.py:360
  67.6 4.4 %collective-permute-start.28 = (bf16[2,3,48,384]{3,2,1,0:T(8,128)(2,1)}, bf16[2,3,48,384]{3,2,1,0:T(8,128)(2,1)}, u32[]{:S(2)}, u32[]{:S(2)}) collective-permute-start(bf16[2,3,48,384]{3,2,1,0:T(8,128)(2,1)} %get-tuple-element.31), channel_id=1, source_target_pairs={{0,1},{1,0},{2,3},{3,2},{4,5},{5,4},{6,7},{7,6},{8,9},{9,8},{10,11... | collective-permute-start | bytes 663560 | tf_op jit(solution)/shard_map/ppermute | solution.py:324
  72.1 11.0 %collective-permute-start.7 = (bf16[2,2,48,384]{3,2,1,0:T(8,128)(2,1)}, bf16[2,2,48,384]{3,2,1,0:T(8,128)(2,1)}, u32[]{:S(2)}, u32[]{:S(2)}) collective-permute-start(bf16[2,2,48,384]{3,2,1,0:T(8,128)(2,1)} %get-tuple-element.25), channel_id=1, source_target_pairs={{0,1},{1,0},{2,3},{3,2},{4,5},{5,4},{6,7},{7,6},{8,9},{9,8},{10,11... | collective-permute-start | bytes 442376 | tf_op jit(solution)/shard_map/ppermute | solution.py:324
  73.8 27.0 %collective-permute-start.29 = (bf16[1,3,48,384]{3,2,1,0:T(8,128)(2,1)}, bf16[1,3,48,384]{3,2,1,0:T(8,128)(2,1)}, u32[]{:S(2)}, u32[]{:S(2)}) collective-permute-start(bf16[1,3,48,384]{3,2,1,0:T(8,128)(2,1)} %add_convert_fusion.6), channel_id=1, source_target_pairs={{0,2},{1,3},{2,0},{3,1},{4,6},{5,7},{6,4},{7,5},{8,10},{9,11},{10,... | collective-permute-start | bytes 331784 | tf_op jit(solution)/shard_map/ppermute | solution.py:324
  82.9 19.8 %collective-permute-start.21 = (bf16[2,5,48,384]{3,2,1,0:T(8,128)(2,1)}, bf16[2,5,48,384]{3,2,1,0:T(8,128)(2,1)}, u32[]{:S(2)}, u32[]{:S(2)}) collective-permute-start(bf16[2,5,48,384]{3,2,1,0:T(8,128)(2,1)} %get-tuple-element.29), channel_id=1, source_target_pairs={{0,1},{1,0},{2,3},{3,2},{4,5},{5,4},{6,7},{7,6},{8,9},{9,8},{10,11... | collective-permute-start | bytes 1105928 | tf_op jit(solution)/shard_map/ppermute | solution.py:324
  84.6 33.0 %collective-permute-start.8 = (bf16[1,2,48,384]{3,2,1,0:T(8,128)(2,1)}, bf16[1,2,48,384]{3,2,1,0:T(8,128)(2,1)}, u32[]{:S(2)}, u32[]{:S(2)}) collective-permute-start(bf16[1,2,48,384]{3,2,1,0:T(8,128)(2,1)} %add_convert_fusion.8), channel_id=1, source_target_pairs={{0,2},{1,3},{2,0},{3,1},{4,6},{5,7},{6,4},{7,5},{8,10},{9,11},{10,... | collective-permute-start | bytes 221192 | tf_op jit(solution)/shard_map/ppermute | solution.py:324
  99.9 5.8 %copy-start = (f32[2,6,48,384]{3,2,1,0:T(8,128)S(1)}, f32[2,6,48,384]{3,2,1,0:T(8,128)}, u32[]{:S(2)}) copy-start(f32[2,6,48,384]{3,2,1,0:T(8,128)} %get-tuple-element.26) | copy-start | bytes 2654212
  99.9 11.4 %copy-start.2 = (f32[2,5,48,384]{3,2,1,0:T(8,128)S(1)}, f32[2,5,48,384]{3,2,1,0:T(8,128)}, u32[]{:S(2)}) copy-start(f32[2,5,48,384]{3,2,1,0:T(8,128)} %get-tuple-element.28) | copy-start | bytes 2211844
  99.9 5.8 %collective-permute-start.14 = (bf16[2,6,48,384]{3,2,1,0:T(8,128)(2,1)}, bf16[2,6,48,384]{3,2,1,0:T(8,128)(2,1)S(1)}, u32[]{:S(2)}, u32[]{:S(2)}) collective-permute-start(bf16[2,6,48,384]{3,2,1,0:T(8,128)(2,1)} %get-tuple-element.27), channel_id=1, source_target_pairs={{0,1},{1,0},{2,3},{3,2},{4,5},{5,4},{6,7},{7,6},{8,9},{9,8},{10,11... | collective-permute-start | bytes 1327112 | tf_op jit(solution)/shard_map/ppermute | solution.py:324
  102.5 26.2 %collective-permute-start.30 = (bf16[3,48,384]{2,1,0:T(8,128)(2,1)}, bf16[3,48,384]{2,1,0:T(8,128)(2,1)}, u32[]{:S(2)}, u32[]{:S(2)}) collective-permute-start(bf16[3,48,384]{2,1,0:T(8,128)(2,1)} %fusion.2.mine), channel_id=1, source_target_pairs={{0,4},{4,0},{8,12},{12,8},{16,20},{20,16},{24,28},{28,24},{1,5},{5... | collective-permute-start | bytes 331784 | tf_op jit(solution)/shard_map/ppermute | solution.py:392
  103.7 13.9 %copy-start.4 = (f32[2,2,48,384]{3,2,1,0:T(8,128)S(1)}, f32[2,2,48,384]{3,2,1,0:T(8,128)}, u32[]{:S(2)}) copy-start(f32[2,2,48,384]{3,2,1,0:T(8,128)} %get-tuple-element.24) | copy-start | bytes 884740
  103.8 7.6 %collective-permute-start.22 = (bf16[1,5,48,384]{3,2,1,0:T(8,128)(2,1)S(1)}, bf16[1,5,48,384]{3,2,1,0:T(8,128)(2,1)S(1)}, u32[]{:S(2)}, u32[]{:S(2)}) collective-permute-start(bf16[1,5,48,384]{3,2,1,0:T(8,128)(2,1)S(1)} %add_convert_fusion.3), channel_id=1, source_target_pairs={{0,2},{1,3},{2,0},{3,1},{4,6},{5,7},{6,4},{7,5},{8,10},{9,11},{10,... | collective-permute-start | bytes 552968 | tf_op jit(solution)/shard_map/ppermute | solution.py:324
  105.8 9.3 %collective-permute-start.15 = (bf16[1,6,48,384]{3,2,1,0:T(8,128)(2,1)S(1)}, bf16[1,6,48,384]{3,2,1,0:T(8,128)(2,1)S(1)}, u32[]{:S(2)}, u32[]{:S(2)}) collective-permute-start(bf16[1,6,48,384]{3,2,1,0:T(8,128)(2,1)S(1)} %add_convert_fusion.1), channel_id=1, source_target_pairs={{0,2},{1,3},{2,0},{3,1},{4,6},{5,7},{6,4},{7,5},{8,10},{9,11},{10,... | collective-permute-start | bytes 663560 | tf_op jit(solution)/shard_map/ppermute | solution.py:324
  112.3 5.3 %copy-start.3 = (bf16[5,48,384]{2,1,0:T(8,128)(2,1)}, bf16[5,48,384]{2,1,0:T(8,128)(2,1)S(1)}, u32[]{:S(2)}) copy-start(bf16[5,48,384]{2,1,0:T(8,128)(2,1)S(1)} %fusion.1.refs_4_) | copy-start | bytes 552964
  112.3 11.9 %collective-permute-start.23 = (bf16[5,48,384]{2,1,0:T(8,128)(2,1)S(1)}, bf16[5,48,384]{2,1,0:T(8,128)(2,1)S(1)}, u32[]{:S(2)}, u32[]{:S(2)}) collective-permute-start(bf16[5,48,384]{2,1,0:T(8,128)(2,1)S(1)} %fusion.1.refs_4_), channel_id=1, source_target_pairs={{0,4},{4,0},{8,12},{12,8},{16,20},{20,16},{24,28},{28,24},{1,5},{5... | collective-permute-start | bytes 552968 | tf_op jit(solution)/shard_map/ppermute | solution.py:392
  115.2 0.7 copy-start.1
  115.9 9.7 %collective-permute-start.16 = (bf16[6,48,384]{2,1,0:T(8,128)(2,1)S(1)}, bf16[6,48,384]{2,1,0:T(8,128)(2,1)}, u32[]{:S(2)}, u32[]{:S(2)}) collective-permute-start(bf16[6,48,384]{2,1,0:T(8,128)(2,1)S(1)} %fusion.refs_2_), channel_id=1, source_target_pairs={{0,4},{4,0},{8,12},{12,8},{16,20},{20,16},{24,28},{28,24},{1,5},{5... | collective-permute-start | bytes 663560 | tf_op jit(solution)/shard_map/ppermute | solution.py:392
  118.6 5.7 %copy-start.5 = (bf16[2,48,384]{2,1,0:T(8,128)(2,1)}, bf16[2,48,384]{2,1,0:T(8,128)(2,1)S(1)}, u32[]{:S(2)}) copy-start(bf16[2,48,384]{2,1,0:T(8,128)(2,1)S(1)} %fusion.3.refs_0_) | copy-start | bytes 221188
  118.6 5.7 %collective-permute-start.9 = (bf16[2,48,384]{2,1,0:T(8,128)(2,1)S(1)}, bf16[2,48,384]{2,1,0:T(8,128)(2,1)S(1)}, u32[]{:S(2)}, u32[]{:S(2)}) collective-permute-start(bf16[2,48,384]{2,1,0:T(8,128)(2,1)S(1)} %fusion.3.refs_0_), channel_id=1, source_target_pairs={{0,4},{4,0},{8,12},{12,8},{16,20},{20,16},{24,28},{28,24},{1,5},{5... | collective-permute-start | bytes 221192 | tf_op jit(solution)/shard_map/ppermute | solution.py:392
  124.3 0.6 copy-start.9
  124.9 0.7 copy-start.6
  131.6 6.7 %collective-permute-start.32 = (bf16[1,4,48,384]{3,2,1,0:T(8,128)(2,1)}, bf16[1,4,48,384]{3,2,1,0:T(8,128)(2,1)S(1)}, u32[]{:S(2)}, u32[]{:S(2)}) collective-permute-start(bf16[1,4,48,384]{3,2,1,0:T(8,128)(2,1)} %get-tuple-element.34), channel_id=1, source_target_pairs={{0,8},{4,12},{8,0},{12,4},{16,24},{20,28},{24,16},{28,20},{1,9},{5... | collective-permute-start | bytes 442376 | tf_op jit(solution)/shard_map/ppermute | solution.py:321
  133.5 9.2 %collective-permute-start.31 = (bf16[1,4,48,384]{3,2,1,0:T(8,128)(2,1)}, bf16[1,4,48,384]{3,2,1,0:T(8,128)(2,1)S(1)}, u32[]{:S(2)}, u32[]{:S(2)}) collective-permute-start(bf16[1,4,48,384]{3,2,1,0:T(8,128)(2,1)} %get-tuple-element.33), channel_id=1, source_target_pairs={{0,8},{4,12},{8,0},{12,4},{16,24},{20,28},{24,16},{28,20},{1,9},{5... | collective-permute-start | bytes 442376 | tf_op jit(solution)/shard_map/ppermute | solution.py:322
  140.0 7.6 %collective-permute-start.33 = (bf16[1,4,48,384]{3,2,1,0:T(8,128)(2,1)S(1)}, bf16[1,4,48,384]{3,2,1,0:T(8,128)(2,1)S(1)}, u32[]{:S(2)}, u32[]{:S(2)}) collective-permute-start(bf16[1,4,48,384]{3,2,1,0:T(8,128)(2,1)S(1)} %get-tuple-element.35), channel_id=1, source_target_pairs={{0,16},{4,20},{8,24},{12,28},{16,0},{20,4},{24,8},{28,12},{1,17},{... | collective-permute-start | bytes 442376 | tf_op jit(solution)/shard_map/ppermute | solution.py:324
  142.8 4.9 %copy-start.7 = (bf16[1,4,48,384]{3,2,1,0:T(8,128)(2,1)}, bf16[1,4,48,384]{3,2,1,0:T(8,128)(2,1)S(1)}, u32[]{:S(2)}) copy-start(bf16[1,4,48,384]{3,2,1,0:T(8,128)(2,1)S(1)} %collective-permute-done.31.refs_0_) | copy-start | bytes 442372
  147.6 0.6 copy-start.8

commit v2 on v1

--- a/solution.py
+++ b/solution.py
@@ -13,7 +13,7 @@
 G_DEV = 8
 OMEGA = 0.6
 
-EDGES = (0, 2, 8, 13, 16)
+EDGES = (0, 6, 12, 16)
 STEP = 2
 
 
@@ -30,71 +30,82 @@
     return pl.CostEstimate(flops=int(flops), bytes_accessed=int(moved), transcendentals=0)
 
 
-def pack_kernel(rows_ref, out_ref):
-    per = rows_ref.shape[0] // out_ref.shape[0]
+def pack_kernel(first, rows_ref, *outs):
+    per = 2 * RQ
     width = rows_ref.shape[2]
-    for m in range(out_ref.shape[0]):
-        for j in range(per):
-            out_ref[m, :, j * width : (j + 1) * width] = rows_ref[per * m + j]
-
-
-def pack_rows(tentative, first, count):
+    base = per * first
+    for out in outs:
+        for m in range(out.shape[0]):
+            for j in range(per):
+                out[m, :, j * width : (j + 1) * width] = rows_ref[base + per * m + j]
+        base += per * out.shape[0]
+
+
+def pack_rows(tentative, spans):
     per = 2 * RQ
     _, high, width = tentative.shape
-    step = step_of(first, count)
-    return pl.pallas_call(
-        pack_kernel,
-        grid=(count // step,),
-        in_specs=[pl.BlockSpec((per * step, high, width), lambda i: (i + first // step, 0, 0))],
-        out_specs=pl.BlockSpec((step, high, per * width), lambda i: (i, 0, 0)),
-        out_shape=jax.ShapeDtypeStruct((count, high, per * width), tentative.dtype),
-        compiler_params=PARAMS,
-        cost_estimate=cost(0, 5 * count * per * high * width),
+    first, last = spans[0][0], spans[-1][1]
+    whole = first % (last - first) == 0
+    block = per * (last - first if whole else last)
+    at = first // (last - first) if whole else 0
+    counts = [stop - start for start, stop in spans]
+    return pl.pallas_call(
+        functools.partial(pack_kernel, 0 if whole else first),
+        grid=(1,),
+        in_specs=[pl.BlockSpec((block, high, width), lambda i: (at, 0, 0))],
+        out_specs=[
+            pl.BlockSpec((count, high, per * width), lambda i: (0, 0, 0)) for count in counts
+        ],
+        out_shape=[
+            jax.ShapeDtypeStruct((count, high, per * width), tentative.dtype) for count in counts
+        ],
+        compiler_params=PARAMS,
+        cost_estimate=cost(0, 5 * sum(counts) * per * high * width),
     )(tentative)
 
 
-def prolong_kernel(
-    first, table, labels, off, diag, inverse, own, near_a, near_b, out, wide
-):
+def prolong_kernel(first, table, labels, off, diag, inverse, own, near_a, near_b, out, *wides):
     step = near_a.shape[0]
     slots, size = off.shape[1], off.shape[2]
     window = CW * size
+    start = 2 * RQ * (first + pl.program_id(0) * step)
 
     @pl.when(pl.program_id(0) == 0)
     def _():
-        wide[3 * RQ] = jnp.zeros((size, window), wide.dtype)
-
-    for m in range(step):
-        for u in range(2):
-            for k in range(RQ):
-                j = u * RQ + k
-                local = 2 * RQ * m + j
-                row = 2 * RQ * (first + pl.program_id(0) * step + m) + j
-                lanes = slice(j * size, (j + 1) * size)
-                for side, block in enumerate(
-                    (near_a[m, :, lanes], own[local], near_b[m, :, lanes])
-                ):
-                    label = labels[side, row]
-                    for w in range(CW):
-                        wide[side * RQ + k, :, w * size : (w + 1) * size] = jnp.where(
-                            label == w, block, jnp.zeros_like(block)
-                        )
-            for k in range(RQ):
-                j = u * RQ + k
-                local = 2 * RQ * m + j
-                row = 2 * RQ * (first + pl.program_id(0) * step + m) + j
-                mine = wide[RQ + k]
-                total = jnp.dot(diag[local], mine, preferred_element_type=jnp.float32)
-                for s in range(slots):
-                    total += jnp.dot(
-                        off[local, s], wide[table[s, row]], preferred_element_type=jnp.float32
+        for wide in wides:
+            wide[3 * RQ] = jnp.zeros((size, window), wide.dtype)
+
+    for c, wide in enumerate(wides):
+        m = c // 2
+        for k in range(RQ):
+            local = RQ * c + k
+            j = local % (2 * RQ)
+            lanes = slice(j * size, (j + 1) * size)
+            for side, block in enumerate((near_a[m, :, lanes], own[local], near_b[m, :, lanes])):
+                label = labels[side, start + local]
+                for w in range(CW):
+                    wide[side * RQ + k, :, w * size : (w + 1) * size] = jnp.where(
+                        label == w, block, jnp.zeros_like(block)
                     )
-                change = jnp.dot(
-                    inverse[local], total.astype(out.dtype), preferred_element_type=jnp.float32
+    sums = []
+    for c, wide in enumerate(wides):
+        for k in range(RQ):
+            local = RQ * c + k
+            total = jnp.dot(diag[local], wide[RQ + k], preferred_element_type=jnp.float32)
+            for s in range(slots):
+                total += jnp.dot(
+                    off[local, s],
+                    wide[table[s, start + local]],
+                    preferred_element_type=jnp.float32,
                 )
-                out[2 * m + u, :, k * window : (k + 1) * window] = (
-                    mine.astype(jnp.float32) - OMEGA * change
-                ).astype(out.dtype)
+            sums.append(total.astype(out.dtype))
+    for c, wide in enumerate(wides):
+        for k in range(RQ):
+            local = RQ * c + k
+            change = jnp.dot(inverse[local], sums[local], preferred_element_type=jnp.float32)
+            out[c, :, k * window : (k + 1) * window] = (
+                wide[RQ + k].astype(jnp.float32) - OMEGA * change
+            ).astype(out.dtype)
 
 
 def prolong_rows(table, labels, off, diag, inverse, tentative, near_a, near_b, first):
@@ -124,7 +135,7 @@
         ],
         out_specs=pl.BlockSpec((2 * step, size, RQ * window), lambda i: (i, 0, 0)),
         out_shape=jax.ShapeDtypeStruct((2 * count, size, RQ * window), tentative.dtype),
-        scratch_shapes=[pltpu.VMEM((3 * RQ + 1, size, window), tentative.dtype)],
+        scratch_shapes=[pltpu.VMEM((3 * RQ + 1, size, window), tentative.dtype)] * (2 * step),
         compiler_params=PARAMS,
         cost_estimate=cost(
             2 * count * per * (slots + 2) * size * size * window,
@@ -133,43 +144,48 @@
     )(table, labels, off, diag, inverse, tentative, near_a, near_b)
 
 
-def coarse_kernel(first, table, place, off, diag, own, near_a, near_b, keep, send, field, stiff, whole):
+def coarse_kernel(first, table, place, off, diag, own, near_a, near_b, keep, send, *scratch):
     step = keep.shape[1]
     slots, size = off.shape[1], off.shape[2]
     window = CW * size
     halves, high = keep.shape[0], keep.shape[2]
     col = place[0]
+    start = 2 * RQ * (first + pl.program_id(0) * step)
+    fields, stiffs, wholes = (scratch[2 * step * i : 2 * step * (i + 1)] for i in range(3))
 
     @pl.when(pl.program_id(0) == 0)
     def _():
-        field[3 * RQ] = jnp.zeros((size, window), field.dtype)
-
-    for m in range(step):
-        for u in range(2):
-            for k in range(RQ):
-                lanes = slice(k * window, (k + 1) * window)
-                for side, source in enumerate((near_a, own, near_b)):
-                    field[side * RQ + k] = source[2 * m + u, :, lanes]
-            for k in range(RQ):
-                j = u * RQ + k
-                local = 2 * RQ * m + j
-                row = 2 * RQ * (first + pl.program_id(0) * step + m) + j
-                total = jnp.dot(diag[local], field[RQ + k], preferred_element_type=jnp.float32)
-                for s in range(slots):
-                    total += jnp.dot(
-                        off[local, s], field[table[s, row]], preferred_element_type=jnp.float32
-                    )
-                stiff[k * size : (k + 1) * size, :] = total.astype(stiff.dtype)
-            left = field[RQ : 2 * RQ].reshape(RQ * size, window)
-            block = lax.dot_general(
-                left, stiff[...], (((0,), (0,)), ((), ())), preferred_element_type=jnp.float32
-            )
-            for piece in range(2 * halves):
-                whole[piece] = block[piece * high : (piece + 1) * high]
-            lanes = slice(u * window, (u + 1) * window)
-            for h in range(halves):
-                keep[h, m, :, lanes] = whole[col ^ (2 * h)]
-                send[h, m, :, lanes] = whole[col ^ (2 * h + 1)].astype(send.dtype)
+        for field in fields:
+            field[3 * RQ] = jnp.zeros((size, window), field.dtype)
+
+    for c, field in enumerate(fields):
+        for k in range(RQ):
+            lanes = slice(k * window, (k + 1) * window)
+            for side, source in enumerate((near_a, own, near_b)):
+                field[side * RQ + k] = source[c, :, lanes]
+    for c, (field, stiff) in enumerate(zip(fields, stiffs)):
+        for k in range(RQ):
+            local = RQ * c + k
+            total = jnp.dot(diag[local], field[RQ + k], preferred_element_type=jnp.float32)
+            for s in range(slots):
+                total += jnp.dot(
+                    off[local, s],
+                    field[table[s, start + local]],
+                    preferred_element_type=jnp.float32,
+                )
+            stiff[k * size : (k + 1) * size, :] = total.astype(stiff.dtype)
+    for field, stiff, whole in zip(fields, stiffs, wholes):
+        left = field[RQ : 2 * RQ].reshape(RQ * size, window)
+        block = lax.dot_general(
+            left, stiff[...], (((0,), (0,)), ((), ())), preferred_element_type=jnp.float32
+        )
+        for piece in range(2 * halves):
+            whole[piece] = block[piece * high : (piece + 1) * high]
+    for c, whole in enumerate(wholes):
+        lanes = slice(c % 2 * window, (c % 2 + 1) * window)
+        for h in range(halves):
+            keep[h, c // 2, :, lanes] = whole[col ^ (2 * h)]
+            send[h, c // 2, :, lanes] = whole[col ^ (2 * h + 1)].astype(send.dtype)
 
 
 def coarse_rows(table, place, off, diag, own, near_a, near_b, first, columns):
@@ -203,11 +219,9 @@
             jax.ShapeDtypeStruct(shape, jnp.float32),
             jax.ShapeDtypeStruct(shape, own.dtype),
         ],
-        scratch_shapes=[
-            pltpu.VMEM((3 * RQ + 1, size, window), own.dtype),
-            pltpu.VMEM((RQ * size, window), own.dtype),
-            pltpu.VMEM((columns, high, window), jnp.float32),
-        ],
+        scratch_shapes=[pltpu.VMEM((3 * RQ + 1, size, window), own.dtype)] * (2 * step)
+        + [pltpu.VMEM((RQ * size, window), own.dtype)] * (2 * step)
+        + [pltpu.VMEM((columns, high, window), jnp.float32)] * (2 * step),
         compiler_params=PARAMS,
         cost_estimate=cost(
             2 * count * per * (slots + 3) * size * size * window,
@@ -361,10 +375,9 @@
         near_a = lax.ppermute(block, "col", pair_a)
         return near_a, near_b
 
-    halos = []
-    for low, high in spans:
-        packed = pack_rows(tentative, low, high - low)
-        halos.append(both(packed))
+    packed = list(pack_rows(tentative, spans[:1]))
+    packed += pack_rows(tentative, spans[1:])
+    halos = [both(block) for block in packed]
     label_a, label_b = both(aggregate)
     labels = jnp.stack([label_a, aggregate, label_b])
     targets = owner_row[:, 0] * G_DEV + owner_group

time: 151 us -> 153 us (1.013)
  waiting for transfers between devices: 29.4 us -> 68.3 us
  Pallas kernels: 73.2 us -> 45.7 us
  starting transfers between devices: 29.4 us -> 24.7 us
  other arithmetic: 15.5 us -> 12.1 us
    ppermute x9 -> x7, waiting for transfers between devices: 8.42 us -> 47.4 us  [both(): near_b = lax.ppermute(block, 'col', pair_b)]
    pallas_call x4 -> x3, Pallas kernels: 30.2 us -> 16.2 us  [prolong_rows(): pl.pallas_call(functools.partial(prolong_kernel, first), grid=(count // s...]
    pallas_call x4 -> x3, Pallas kernels: 24.1 us -> 16.8 us  [coarse_rows(): pl.pallas_call(functools.partial(coarse_kernel, first), grid=(count // st...]
    pallas_call x4 -> x2, Pallas kernels: 11 us -> 4.7 us  [pack_rows(): pl.pallas_call(functools.partial(pack_kernel, 0 if whole else first), gri...]
    ppermute x9 -> x7, starting transfers between devices: 9.41 us -> 6.49 us  [both(): near_b = lax.ppermute(block, 'col', pair_b)]
    ppermute x9 -> x7, starting transfers between devices: 8.67 us -> 6.45 us  [exchange(): even = lax.ppermute(send, axis, route)]
    ppermute x9 -> x7, waiting for transfers between devices: 11.1 us -> 12.8 us  [exchange(): even = lax.ppermute(send, axis, route)]
    convert_element_type x5 -> x4, other arithmetic: 6.19 us -> 5.01 us  [exchange(): send = (send + odd.astype(jnp.float32)).astype(link)]
  transfers between devices with their start and end apart: 34 -> 27, of which waited for: 7 -> 10; matrix products, arithmetic and copies ran while one was open for 10% -> 8% of each run, Pallas kernels for 46% -> 27%
where the time goes in v2:
time: 153 us; the launch traced here: 152 us
  waiting for transfers between devices  68.3 us (45%)
  Pallas kernels  45.7 us (30%)
  starting transfers between devices  24.7 us (16%)
  other arithmetic  12.1 us (8%)
    ppermute x7, waiting for transfers between devices, both(): near_b = lax.ppermute(block, 'col', pair_b)  47.4 us
    pallas_call x3, Pallas kernels, coarse_rows(): pl.pallas_call(functools.partial(coarse_kernel, first), grid=(count // st...  16.8 us
    pallas_call x3, Pallas kernels, prolong_rows(): pl.pallas_call(functools.partial(prolong_kernel, first), grid=(count // s...  16.2 us
    ppermute x7, waiting for transfers between devices, exchange(): even = lax.ppermute(send, axis, route)  12.8 us
    ppermute x7, starting transfers between devices, both(): near_b = lax.ppermute(block, 'col', pair_b)  6.49 us
    ppermute x7, starting transfers between devices, exchange(): even = lax.ppermute(send, axis, route)  6.45 us
    convert_element_type x4, other arithmetic, exchange(): send = (send + odd.astype(jnp.float32)).astype(link)  5.01 us
    pallas_call x2, Pallas kernels, pack_rows(): pl.pallas_call(functools.partial(pack_kernel, 0 if whole else first), gri...  4.7 us
  transfers between devices with their start and end apart: 27, of which 10 were waited for; matrix products, arithmetic and copies ran while one was open for 8% of the time, Pallas kernels for 27%

profile of v2, /device:TPU:0, one launch (start us, length us, event | category | flops | bytes accessed | tf_op | source)
XLA Modules:
  0.0 152.3 jit_solution(17962561823269536401)
XLA Ops:
  0.5 2.6 %collective-permute-start.1 = (s32[64]{0:T(128)}, s32[64]{0:T(128)}, u32[]{:S(2)}, u32[]{:S(2)}) collective-permute-start(s32[64]{0:T(128)} %param.15), channel_id=1, source_target_pairs={{0,3},{1,2},{2,1},{3,0},{4,7},{5,6},{6,5},{7,4},{8,11},{9,10},{10,... | collective-permute-start | bytes 776 | tf_op jit(solution)/shard_map/ppermute | solution.py:374
  3.1 2.6 %shard_map.94 = (bf16[6,96,384]{2,1,0:T(8,128)(2,1)}, bf16[4,96,384]{2,1,0:T(8,128)(2,1)}) custom-call(bf16[64,96,96]{2,1,0:T(8,128)(2,1)} %own.5), custom_call_target="tpu_custom_call" | custom-call | bytes 1843200 | tf_op jit(solution)/shard_map/pallas_call | solution.py:52
  5.7 0.7 bitcast_add_fusion
  6.4 2.1 %collective-permute-start.2 = (s32[32]{0:T(128)S(1)}, s32[32]{0:T(128)S(1)}, u32[]{:S(2)}, u32[]{:S(2)}) collective-permute-start(s32[32]{0:T(128)S(1)} %bitcast_add_fusion), channel_id=1, source_target_pairs={{0,4},{4,0},{8,12},{12,8},{16,20},{20,16},{24,28},{28,24},{1,5},{5... | collective-permute-start | bytes 392 | tf_op jit(solution)/shard_map/ppermute | solution.py:384
  8.5 1.3 fusion.6.table
  9.8 0.6 pad_add_fusion.2.place
  10.9 1.8 %collective-permute-start.11 = (bf16[6,96,384]{2,1,0:T(8,128)(2,1)}, bf16[6,96,384]{2,1,0:T(8,128)(2,1)}, u32[]{:S(2)}, u32[]{:S(2)}) collective-permute-start(bf16[6,96,384]{2,1,0:T(8,128)(2,1)} %get-tuple-element.26), channel_id=1, source_target_pairs={{0,3},{1,2},{2,1},{3,0},{4,7},{5,6},{6,5},{7,4},{8,11},{9,10},{10,... | collective-permute-start | bytes 1327112 | tf_op jit(solution)/shard_map/ppermute | solution.py:374
  12.7 1.3 pad_add_fusion.labels
  14.0 0.6 collective-permute-done.18.near_b
  14.6 4.4 %shard_map.98.own = bf16[8,96,384]{2,1,0:T(8,128)(2,1)} custom-call(s32[4,64]{1,0:T(4,128)} %fusion.6.table, s32[3,64]{1,0:T(4,128)} %pad_add_fusion.labels, bf16[64,4,96,96]{3,2,1,0:T(8,128)(2,1)} %off.11, bf16[64,96,96]{2,1,0:T(8,128)(2,1)} %diag.11, bf16[64,96,96]{2,1,0:T(8,128)(2,1)} %inverse.5, bf16[64,96,96]{2,1,0:T(8,128)(2,1)} %own.5, ...), custom_call_target="tpu_custom_call" | custom-call | flops 339738624 | bytes 3244032 | tf_op jit(solution)/shard_map/pallas_call | solution.py:123
  19.0 1.5 collective-permute-start.19
  20.5 2.1 %shard_map.91 = bf16[6,96,384]{2,1,0:T(8,128)(2,1)} custom-call(bf16[64,96,96]{2,1,0:T(8,128)(2,1)} %own.5), custom_call_target="tpu_custom_call" | custom-call | bytes 1105920 | tf_op jit(solution)/shard_map/pallas_call | solution.py:52
  22.7 1.4 collective-permute-done.11.near_b
  24.1 5.9 %shard_map.95.own = bf16[12,96,384]{2,1,0:T(8,128)(2,1)} custom-call(s32[4,64]{1,0:T(4,128)} %fusion.6.table, s32[3,64]{1,0:T(4,128)} %pad_add_fusion.labels, bf16[64,4,96,96]{3,2,1,0:T(8,128)(2,1)} %off.11, bf16[64,96,96]{2,1,0:T(8,128)(2,1)} %diag.11, bf16[64,96,96]{2,1,0:T(8,128)(2,1)} %inverse.5, bf16[64,96,96]{2,1,0:T(8,128)(2,1)} %own.5, ...), custom_call_target="tpu_custom_call" | custom-call | flops 509607936 | bytes 4866048 | tf_op jit(solution)/shard_map/pallas_call | solution.py:123
  30.0 0.5 collective-permute-start.12
  30.8 3.9 %collective-permute-done.4.near_b = bf16[6,96,384]{2,1,0:T(8,128)(2,1)} collective-permute-done((bf16[6,96,384]{2,1,0:T(8,128)(2,1)}, bf16[6,96,384]{2,1,0:T(8,128)(2,1)}, u32[]{:S(2)}, u32[]{:S(2)}) %collective-permute-start.4) | collective-permute-done | bytes 442400 | tf_op jit(solution)/shard_map/ppermute | solution.py:374
  34.8 5.9 %shard_map.92.own = bf16[12,96,384]{2,1,0:T(8,128)(2,1)} custom-call(s32[4,64]{1,0:T(4,128)} %fusion.6.table, s32[3,64]{1,0:T(4,128)} %pad_add_fusion.labels, bf16[64,4,96,96]{3,2,1,0:T(8,128)(2,1)} %off.11, bf16[64,96,96]{2,1,0:T(8,128)(2,1)} %diag.11, bf16[64,96,96]{2,1,0:T(8,128)(2,1)} %inverse.5, bf16[64,96,96]{2,1,0:T(8,128)(2,1)} %own.5, ...), custom_call_target="tpu_custom_call" | custom-call | flops 509607936 | bytes 4866048 | tf_op jit(solution)/shard_map/pallas_call | solution.py:123
  40.7 1.5 collective-permute-start.5
  42.1 1.7 %collective-permute-start.20 = (bf16[8,96,384]{2,1,0:T(8,128)(2,1)}, bf16[8,96,384]{2,1,0:T(8,128)(2,1)}, u32[]{:S(2)}, u32[]{:S(2)}) collective-permute-start(bf16[8,96,384]{2,1,0:T(8,128)(2,1)} %shard_map.98.own), channel_id=1, source_target_pairs={{0,3},{1,2},{2,1},{3,0},{4,7},{5,6},{6,5},{7,4},{8,11},{9,10},{10,... | collective-permute-start | bytes 1769480 | tf_op jit(solution)/shard_map/ppermute | solution.py:374
  43.9 41.4 %collective-permute-done.20.near_b = bf16[8,96,384]{2,1,0:T(8,128)(2,1)} collective-permute-done((bf16[8,96,384]{2,1,0:T(8,128)(2,1)}, bf16[8,96,384]{2,1,0:T(8,128)(2,1)}, u32[]{:S(2)}, u32[]{:S(2)}) %collective-permute-start.20) | collective-permute-done | bytes 589856 | tf_op jit(solution)/shard_map/ppermute | solution.py:374
  85.3 4.5 %shard_map.99 = (f32[2,4,48,384]{3,2,1,0:T(8,128)}, bf16[2,4,48,384]{3,2,1,0:T(8,128)(2,1)}) custom-call(s32[4,64]{1,0:T(4,128)} %fusion.6.table, s32[2]{0:T(128)} %pad_add_fusion.2.place, bf16[64,4,96,96]{3,2,1,0:T(8,128)(2,1)} %off.11, bf16[64,96,96]{2,1,0:T(8,128)(2,1)} %diag.11, bf16[8,96,384]{2,1,0:T(8,128)(2,1)} %shard_map.98.own, ...), custom_call_target="tpu_custom_call" | custom-call | flops 396361728 | bytes 4718592 | tf_op jit(solution)/shard_map/pallas_call | solution.py:205
  90.4 6.1 %shard_map.96 = (f32[2,6,48,384]{3,2,1,0:T(8,128)}, bf16[2,6,48,384]{3,2,1,0:T(8,128)(2,1)}) custom-call(s32[4,64]{1,0:T(4,128)} %fusion.6.table, s32[2]{0:T(128)} %pad_add_fusion.2.place, bf16[64,4,96,96]{3,2,1,0:T(8,128)(2,1)} %off.11, bf16[64,96,96]{2,1,0:T(8,128)(2,1)} %diag.11, bf16[12,96,384]{2,1,0:T(8,128)(2,1)} %shard_map.95.own, ...), custom_call_target="tpu_custom_call" | custom-call | flops 594542592 | bytes 7077888 | tf_op jit(solution)/shard_map/pallas_call | solution.py:205
  96.5 6.1 %shard_map.93 = (f32[2,6,48,384]{3,2,1,0:T(8,128)}, bf16[2,6,48,384]{3,2,1,0:T(8,128)(2,1)}) custom-call(s32[4,64]{1,0:T(4,128)} %fusion.6.table, s32[2]{0:T(128)} %pad_add_fusion.2.place, bf16[64,4,96,96]{3,2,1,0:T(8,128)(2,1)} %off.11, bf16[64,96,96]{2,1,0:T(8,128)(2,1)} %diag.11, bf16[12,96,384]{2,1,0:T(8,128)(2,1)} %shard_map.92.own, ...), custom_call_target="tpu_custom_call" | custom-call | flops 594542592 | bytes 7077888 | tf_op jit(solution)/shard_map/pallas_call | solution.py:205
  102.7 0.5 collective-permute-start.7
  103.2 1.0 add_convert_fusion.6
  104.3 0.6 collective-permute-start.22
  104.9 1.1 add_convert_fusion.1
  106.0 1.5 collective-permute-start.15
  107.6 1.1 add_convert_fusion.3
  108.6 0.6 collective-permute-start.8
  109.3 6.5 %collective-permute-done.15 = bf16[1,6,48,384]{3,2,1,0:T(8,128)(2,1)S(1)} collective-permute-done((bf16[1,6,48,384]{3,2,1,0:T(8,128)(2,1)S(1)}, bf16[1,6,48,384]{3,2,1,0:T(8,128)(2,1)S(1)}, u32[]{:S(2)}, u32[]{:S(2)}) %collective-permute-start.15) | collective-permute-done | bytes 221216 | tf_op jit(solution)/shard_map/ppermute | solution.py:338
  115.8 1.0 fusion.1.refs_2_
  116.8 1.5 %collective-permute-start.16 = (bf16[6,48,384]{2,1,0:T(8,128)(2,1)S(1)}, bf16[6,48,384]{2,1,0:T(8,128)(2,1)S(1)}, u32[]{:S(2)}, u32[]{:S(2)}) collective-permute-start(bf16[6,48,384]{2,1,0:T(8,128)(2,1)S(1)} %fusion.1.refs_2_), channel_id=1, source_target_pairs={{0,4},{4,0},{8,12},{12,8},{16,20},{20,16},{24,28},{28,24},{1,5},{5... | collective-permute-start | bytes 663560 | tf_op jit(solution)/shard_map/ppermute | solution.py:405
  118.4 1.3 collective-permute-done.8
  119.8 1.6 %collective-permute-start.9 = (bf16[6,48,384]{2,1,0:T(8,128)(2,1)S(1)}, bf16[6,48,384]{2,1,0:T(8,128)(2,1)}, u32[]{:S(2)}, u32[]{:S(2)}) collective-permute-start(bf16[6,48,384]{2,1,0:T(8,128)(2,1)S(1)} %fusion.refs_0_), channel_id=1, source_target_pairs={{0,4},{4,0},{8,12},{12,8},{16,20},{20,16},{24,28},{28,24},{1,5},{5... | collective-permute-start | bytes 663560 | tf_op jit(solution)/shard_map/ppermute | solution.py:405
  121.3 1.6 %fusion.2.mine = bf16[4,48,384]{2,1,0:T(8,128)(2,1)} fusion(bf16[1,4,48,384]{3,2,1,0:T(8,128)(2,1)S(1)} %collective-permute-done.22, f32[2,4,48,384]{3,2,1,0:T(8,128)S(1)} %copy-done.4, bf16[2,4,48,384]{3,2,1,0:T(8,128)(2,1)} %collective-permute-done.21), kind=kLoop, calls=%fused_computation.9 | loop fusion | flops 368640 | bytes 737280 | tf_op jit(solution)/shard_map/convert_element_type | solution.py:404
  123.0 0.5 collective-permute-start.23
  124.0 0.7 copy-done.5
  124.7 4.1 %collective-permute-done.9.refs_1_ = bf16[6,48,384]{2,1,0:T(8,128)(2,1)} collective-permute-done((bf16[6,48,384]{2,1,0:T(8,128)(2,1)S(1)}, bf16[6,48,384]{2,1,0:T(8,128)(2,1)}, u32[]{:S(2)}, u32[]{:S(2)}) %collective-permute-start.9) | collective-permute-done | bytes 221216 | tf_op jit(solution)/shard_map/ppermute | solution.py:405
  128.9 3.1 %shard_map.97.early = f32[33,48,192]{2,1,0:T(8,128)} custom-call(s32[2,32]{1,0:T(2,128)} %pad_add_fusion.1.targets, s32[2]{0:T(128)} %pad_add_fusion.2.place, bf16[6,48,384]{2,1,0:T(8,128)(2,1)} %copy-done.3, bf16[6,48,384]{2,1,0:T(8,128)(2,1)} %collective-permute-done.9.refs_1_, bf16[6,48,384]{2,1,0:T(8,128)(2,1)} %copy-done.2, bf16[6,48,384]{2,1,0:T(8,128)(2,1)} %copy-done.5), custom_call_target="tpu_custom_call" | custom-call | flops 442368 | bytes 1769472 | tf_op jit(solution)/shard_map/pallas_call | solution.py:262
  132.0 2.9 %shard_map.100 = (f32[2,4,48,384]{3,2,1,0:T(8,128)}, bf16[1,4,48,384]{3,2,1,0:T(8,128)(2,1)}, bf16[1,4,48,384]{3,2,1,0:T(8,128)(2,1)}) custom-call(s32[2,32]{1,0:T(2,128)} %pad_add_fusion.1.targets, s32[2]{0:T(128)} %pad_add_fusion.2.place, f32[33,48,192]{2,1,0:T(8,128)} %shard_map.97.early, bf16[4,48,384]{2,1,0:T(8,128)(2,1)} %fusion.2.mine, ...), custom_call_target="tpu_custom_call" | custom-call | flops 304128 | bytes 3041280 | tf_op jit(solution)/shard_map/pallas_call | solution.py:290
  134.9 1.6 %collective-permute-start.25 = (bf16[1,4,48,384]{3,2,1,0:T(8,128)(2,1)}, bf16[1,4,48,384]{3,2,1,0:T(8,128)(2,1)S(1)}, u32[]{:S(2)}, u32[]{:S(2)}) collective-permute-start(bf16[1,4,48,384]{3,2,1,0:T(8,128)(2,1)} %get-tuple-element.34), channel_id=1, source_target_pairs={{0,8},{4,12},{8,0},{12,4},{16,24},{20,28},{24,16},{28,20},{1,9},{5... | collective-permute-start | bytes 442376 | tf_op jit(solution)/shard_map/ppermute | solution.py:335
  136.9 3.3 %collective-permute-done.25 = bf16[1,4,48,384]{3,2,1,0:T(8,128)(2,1)S(1)} collective-permute-done((bf16[1,4,48,384]{3,2,1,0:T(8,128)(2,1)}, bf16[1,4,48,384]{3,2,1,0:T(8,128)(2,1)S(1)}, u32[]{:S(2)}, u32[]{:S(2)}) %collective-permute-start.25) | collective-permute-done | bytes 147488 | tf_op jit(solution)/shard_map/ppermute | solution.py:335
  140.3 1.8 %add_convert_fusion.4 = (bf16[1,4,48,384]{3,2,1,0:T(8,128)(2,1)S(1)}, f32[1,4,48,384]{3,2,1,0:T(8,128)}) fusion(bf16[1,4,48,384]{3,2,1,0:T(8,128)(2,1)S(1)} %collective-permute-done.25, f32[2,4,48,384]{3,2,1,0:T(8,128)} %get-tuple-element.32), kind=kLoop, calls=%fused_computation.4 | loop fusion | flops 221184 | bytes 1179648 | tf_op jit(solution)/shard_map/convert_element_type | solution.py:345
  142.1 2.6 %collective-permute-start.26 = (bf16[1,4,48,384]{3,2,1,0:T(8,128)(2,1)S(1)}, bf16[1,4,48,384]{3,2,1,0:T(8,128)(2,1)S(1)}, u32[]{:S(2)}, u32[]{:S(2)}) collective-permute-start(bf16[1,4,48,384]{3,2,1,0:T(8,128)(2,1)S(1)} %get-tuple-element.35), channel_id=1, source_target_pairs={{0,16},{4,20},{8,24},{12,28},{16,0},{20,4},{24,8},{28,12},{1,17},{... | collective-permute-start | bytes 442376 | tf_op jit(solution)/shard_map/ppermute | solution.py:338
  144.6 5.0 %collective-permute-done.26.refs_1_ = bf16[1,4,48,384]{3,2,1,0:T(8,128)(2,1)S(1)} collective-permute-done((bf16[1,4,48,384]{3,2,1,0:T(8,128)(2,1)S(1)}, bf16[1,4,48,384]{3,2,1,0:T(8,128)(2,1)S(1)}, u32[]{:S(2)}, u32[]{:S(2)}) %collective-permute-start.26) | collective-permute-done | bytes 147488 | tf_op jit(solution)/shard_map/ppermute | solution.py:338
  149.7 0.7 copy-done.7
  150.4 1.9 %shard_map.101 = f32[8,48,192]{2,1,0:T(8,128)} custom-call(f32[1,4,48,384]{3,2,1,0:T(8,128)} %get-tuple-element.36.keep_ref, bf16[1,4,48,384]{3,2,1,0:T(8,128)(2,1)} %copy-done.6, bf16[1,4,48,384]{3,2,1,0:T(8,128)(2,1)} %copy-done.7), custom_call_target="tpu_custom_call" | custom-call | flops 73728 | bytes 737280 | tf_op jit(solution)/shard_map/pallas_call | solution.py:315
  (45 shorter events, 3.0 us)
Async XLA Ops:
  0.0 10.9 %collective-permute-start = (s32[64]{0:T(128)}, s32[64]{0:T(128)}, u32[]{:S(2)}, u32[]{:S(2)}) collective-permute-start(s32[64]{0:T(128)} %param.15), channel_id=1, source_target_pairs={{0,1},{1,0},{2,3},{3,2},{4,5},{5,4},{6,7},{7,6},{8,9},{9,8},{10,11... | collective-permute-start | bytes 776 | tf_op jit(solution)/shard_map/ppermute | solution.py:375
  0.5 12.2 %collective-permute-start.1 = (s32[64]{0:T(128)}, s32[64]{0:T(128)}, u32[]{:S(2)}, u32[]{:S(2)}) collective-permute-start(s32[64]{0:T(128)} %param.15), channel_id=1, source_target_pairs={{0,3},{1,2},{2,1},{3,0},{4,7},{5,6},{6,5},{7,4},{8,11},{9,10},{10,... | collective-permute-start | bytes 776 | tf_op jit(solution)/shard_map/ppermute | solution.py:374
  5.7 8.3 %collective-permute-start.17 = (bf16[4,96,384]{2,1,0:T(8,128)(2,1)}, bf16[4,96,384]{2,1,0:T(8,128)(2,1)}, u32[]{:S(2)}, u32[]{:S(2)}) collective-permute-start(bf16[4,96,384]{2,1,0:T(8,128)(2,1)} %get-tuple-element.29), channel_id=1, source_target_pairs={{0,1},{1,0},{2,3},{3,2},{4,5},{5,4},{6,7},{7,6},{8,9},{9,8},{10,11... | collective-permute-start | bytes 884744 | tf_op jit(solution)/shard_map/ppermute | solution.py:375
  5.7 8.9 %collective-permute-start.18 = (bf16[4,96,384]{2,1,0:T(8,128)(2,1)}, bf16[4,96,384]{2,1,0:T(8,128)(2,1)}, u32[]{:S(2)}, u32[]{:S(2)}) collective-permute-start(bf16[4,96,384]{2,1,0:T(8,128)(2,1)} %get-tuple-element.29), channel_id=1, source_target_pairs={{0,3},{1,2},{2,1},{3,0},{4,7},{5,6},{6,5},{7,4},{8,11},{9,10},{10,... | collective-permute-start | bytes 884744 | tf_op jit(solution)/shard_map/ppermute | solution.py:374
  6.4 4.0 %collective-permute-start.2 = (s32[32]{0:T(128)S(1)}, s32[32]{0:T(128)S(1)}, u32[]{:S(2)}, u32[]{:S(2)}) collective-permute-start(s32[32]{0:T(128)S(1)} %bitcast_add_fusion), channel_id=1, source_target_pairs={{0,4},{4,0},{8,12},{12,8},{16,20},{20,16},{24,28},{28,24},{1,5},{5... | collective-permute-start | bytes 392 | tf_op jit(solution)/shard_map/ppermute | solution.py:384
  10.3 12.3 %collective-permute-start.10 = (bf16[6,96,384]{2,1,0:T(8,128)(2,1)}, bf16[6,96,384]{2,1,0:T(8,128)(2,1)}, u32[]{:S(2)}, u32[]{:S(2)}) collective-permute-start(bf16[6,96,384]{2,1,0:T(8,128)(2,1)} %get-tuple-element.26), channel_id=1, source_target_pairs={{0,1},{1,0},{2,3},{3,2},{4,5},{5,4},{6,7},{7,6},{8,9},{9,8},{10,11... | collective-permute-start | bytes 1327112 | tf_op jit(solution)/shard_map/ppermute | solution.py:375
  10.9 13.2 %collective-permute-start.11 = (bf16[6,96,384]{2,1,0:T(8,128)(2,1)}, bf16[6,96,384]{2,1,0:T(8,128)(2,1)}, u32[]{:S(2)}, u32[]{:S(2)}) collective-permute-start(bf16[6,96,384]{2,1,0:T(8,128)(2,1)} %get-tuple-element.26), channel_id=1, source_target_pairs={{0,3},{1,2},{2,1},{3,0},{4,7},{5,6},{6,5},{7,4},{8,11},{9,10},{10,... | collective-permute-start | bytes 1327112 | tf_op jit(solution)/shard_map/ppermute | solution.py:374
  19.0 23.1 %collective-permute-start.19 = (bf16[8,96,384]{2,1,0:T(8,128)(2,1)}, bf16[8,96,384]{2,1,0:T(8,128)(2,1)}, u32[]{:S(2)}, u32[]{:S(2)}) collective-permute-start(bf16[8,96,384]{2,1,0:T(8,128)(2,1)} %shard_map.98.own), channel_id=1, source_target_pairs={{0,1},{1,0},{2,3},{3,2},{4,5},{5,4},{6,7},{7,6},{8,9},{9,8},{10,11... | collective-permute-start | bytes 1769480 | tf_op jit(solution)/shard_map/ppermute | solution.py:375
  22.6 8.2 %collective-permute-start.3 = (bf16[6,96,384]{2,1,0:T(8,128)(2,1)}, bf16[6,96,384]{2,1,0:T(8,128)(2,1)}, u32[]{:S(2)}, u32[]{:S(2)}) collective-permute-start(bf16[6,96,384]{2,1,0:T(8,128)(2,1)} %shard_map.91), channel_id=1, source_target_pairs={{0,1},{1,0},{2,3},{3,2},{4,5},{5,4},{6,7},{7,6},{8,9},{9,8},{10,11... | collective-permute-start | bytes 1327112 | tf_op jit(solution)/shard_map/ppermute | solution.py:375
  22.7 12.1 %collective-permute-start.4 = (bf16[6,96,384]{2,1,0:T(8,128)(2,1)}, bf16[6,96,384]{2,1,0:T(8,128)(2,1)}, u32[]{:S(2)}, u32[]{:S(2)}) collective-permute-start(bf16[6,96,384]{2,1,0:T(8,128)(2,1)} %shard_map.91), channel_id=1, source_target_pairs={{0,3},{1,2},{2,1},{3,0},{4,7},{5,6},{6,5},{7,4},{8,11},{9,10},{10,... | collective-permute-start | bytes 1327112 | tf_op jit(solution)/shard_map/ppermute | solution.py:374
  30.0 60.4 %collective-permute-start.12 = (bf16[12,96,384]{2,1,0:T(8,128)(2,1)}, bf16[12,96,384]{2,1,0:T(8,128)(2,1)}, u32[]{:S(2)}, u32[]{:S(2)}) collective-permute-start(bf16[12,96,384]{2,1,0:T(8,128)(2,1)} %shard_map.95.own), channel_id=1, source_target_pairs={{0,1},{1,0},{2,3},{3,2},{4,5},{5,4},{6,7},{7,6},{8,9},{9,8},{10,11... | collective-permute-start | bytes 2654216 | tf_op jit(solution)/shard_map/ppermute | solution.py:375
  30.5 59.8 %collective-permute-start.13 = (bf16[12,96,384]{2,1,0:T(8,128)(2,1)}, bf16[12,96,384]{2,1,0:T(8,128)(2,1)}, u32[]{:S(2)}, u32[]{:S(2)}) collective-permute-start(bf16[12,96,384]{2,1,0:T(8,128)(2,1)} %shard_map.95.own), channel_id=1, source_target_pairs={{0,3},{1,2},{2,1},{3,0},{4,7},{5,6},{6,5},{7,4},{8,11},{9,10},{10,... | collective-permute-start | bytes 2654216 | tf_op jit(solution)/shard_map/ppermute | solution.py:374
  40.7 55.9 %collective-permute-start.5 = (bf16[12,96,384]{2,1,0:T(8,128)(2,1)}, bf16[12,96,384]{2,1,0:T(8,128)(2,1)}, u32[]{:S(2)}, u32[]{:S(2)}) collective-permute-start(bf16[12,96,384]{2,1,0:T(8,128)(2,1)} %shard_map.92.own), channel_id=1, source_target_pairs={{0,1},{1,0},{2,3},{3,2},{4,5},{5,4},{6,7},{7,6},{8,9},{9,8},{10,11... | collective-permute-start | bytes 2654216 | tf_op jit(solution)/shard_map/ppermute | solution.py:375
  42.1 54.4 %collective-permute-start.6 = (bf16[12,96,384]{2,1,0:T(8,128)(2,1)}, bf16[12,96,384]{2,1,0:T(8,128)(2,1)}, u32[]{:S(2)}, u32[]{:S(2)}) collective-permute-start(bf16[12,96,384]{2,1,0:T(8,128)(2,1)} %shard_map.92.own), channel_id=1, source_target_pairs={{0,3},{1,2},{2,1},{3,0},{4,7},{5,6},{6,5},{7,4},{8,11},{9,10},{10,... | collective-permute-start | bytes 2654216 | tf_op jit(solution)/shard_map/ppermute | solution.py:374
  42.1 43.2 %collective-permute-start.20 = (bf16[8,96,384]{2,1,0:T(8,128)(2,1)}, bf16[8,96,384]{2,1,0:T(8,128)(2,1)}, u32[]{:S(2)}, u32[]{:S(2)}) collective-permute-start(bf16[8,96,384]{2,1,0:T(8,128)(2,1)} %shard_map.98.own), channel_id=1, source_target_pairs={{0,3},{1,2},{2,1},{3,0},{4,7},{5,6},{6,5},{7,4},{8,11},{9,10},{10,... | collective-permute-start | bytes 1769480 | tf_op jit(solution)/shard_map/ppermute | solution.py:374
  89.8 13.4 %collective-permute-start.21 = (bf16[2,4,48,384]{3,2,1,0:T(8,128)(2,1)}, bf16[2,4,48,384]{3,2,1,0:T(8,128)(2,1)}, u32[]{:S(2)}, u32[]{:S(2)}) collective-permute-start(bf16[2,4,48,384]{3,2,1,0:T(8,128)(2,1)} %get-tuple-element.31), channel_id=1, source_target_pairs={{0,1},{1,0},{2,3},{3,2},{4,5},{5,4},{6,7},{7,6},{8,9},{9,8},{10,11... | collective-permute-start | bytes 884744 | tf_op jit(solution)/shard_map/ppermute | solution.py:338
  96.5 8.4 %collective-permute-start.14 = (bf16[2,6,48,384]{3,2,1,0:T(8,128)(2,1)}, bf16[2,6,48,384]{3,2,1,0:T(8,128)(2,1)}, u32[]{:S(2)}, u32[]{:S(2)}) collective-permute-start(bf16[2,6,48,384]{3,2,1,0:T(8,128)(2,1)} %get-tuple-element.28), channel_id=1, source_target_pairs={{0,1},{1,0},{2,3},{3,2},{4,5},{5,4},{6,7},{7,6},{8,9},{9,8},{10,11... | collective-permute-start | bytes 1327112 | tf_op jit(solution)/shard_map/ppermute | solution.py:338
  102.7 13.1 %copy-start = (f32[2,6,48,384]{3,2,1,0:T(8,128)S(1)}, f32[2,6,48,384]{3,2,1,0:T(8,128)}, u32[]{:S(2)}) copy-start(f32[2,6,48,384]{3,2,1,0:T(8,128)} %get-tuple-element.27) | copy-start | bytes 2654212
  102.7 4.9 %collective-permute-start.7 = (bf16[2,6,48,384]{3,2,1,0:T(8,128)(2,1)}, bf16[2,6,48,384]{3,2,1,0:T(8,128)(2,1)S(1)}, u32[]{:S(2)}, u32[]{:S(2)}) collective-permute-start(bf16[2,6,48,384]{3,2,1,0:T(8,128)(2,1)} %get-tuple-element.25), channel_id=1, source_target_pairs={{0,1},{1,0},{2,3},{3,2},{4,5},{5,4},{6,7},{7,6},{8,9},{9,8},{10,11... | collective-permute-start | bytes 1327112 | tf_op jit(solution)/shard_map/ppermute | solution.py:338
  104.3 15.4 %copy-start.1 = (f32[2,6,48,384]{3,2,1,0:T(8,128)S(1)}, f32[2,6,48,384]{3,2,1,0:T(8,128)}, u32[]{:S(2)}) copy-start(f32[2,6,48,384]{3,2,1,0:T(8,128)} %get-tuple-element.24) | copy-start | bytes 2654212
  104.3 17.1 %collective-permute-start.22 = (bf16[1,4,48,384]{3,2,1,0:T(8,128)(2,1)S(1)}, bf16[1,4,48,384]{3,2,1,0:T(8,128)(2,1)S(1)}, u32[]{:S(2)}, u32[]{:S(2)}) collective-permute-start(bf16[1,4,48,384]{3,2,1,0:T(8,128)(2,1)S(1)} %add_convert_fusion.6), channel_id=1, source_target_pairs={{0,2},{1,3},{2,0},{3,1},{4,6},{5,7},{6,4},{7,5},{8,10},{9,11},{10,... | collective-permute-start | bytes 442376 | tf_op jit(solution)/shard_map/ppermute | solution.py:338
  106.0 15.3 %copy-start.4 = (f32[2,4,48,384]{3,2,1,0:T(8,128)S(1)}, f32[2,4,48,384]{3,2,1,0:T(8,128)}, u32[]{:S(2)}) copy-start(f32[2,4,48,384]{3,2,1,0:T(8,128)} %get-tuple-element.30) | copy-start | bytes 1769476
  106.0 9.8 %collective-permute-start.15 = (bf16[1,6,48,384]{3,2,1,0:T(8,128)(2,1)S(1)}, bf16[1,6,48,384]{3,2,1,0:T(8,128)(2,1)S(1)}, u32[]{:S(2)}, u32[]{:S(2)}) collective-permute-start(bf16[1,6,48,384]{3,2,1,0:T(8,128)(2,1)S(1)} %add_convert_fusion.1), channel_id=1, source_target_pairs={{0,2},{1,3},{2,0},{3,1},{4,6},{5,7},{6,4},{7,5},{8,10},{9,11},{10,... | collective-permute-start | bytes 663560 | tf_op jit(solution)/shard_map/ppermute | solution.py:338
  108.6 11.0 %collective-permute-start.8 = (bf16[1,6,48,384]{3,2,1,0:T(8,128)(2,1)S(1)}, bf16[1,6,48,384]{3,2,1,0:T(8,128)(2,1)S(1)}, u32[]{:S(2)}, u32[]{:S(2)}) collective-permute-start(bf16[1,6,48,384]{3,2,1,0:T(8,128)(2,1)S(1)} %add_convert_fusion.3), channel_id=1, source_target_pairs={{0,2},{1,3},{2,0},{3,1},{4,6},{5,7},{6,4},{7,5},{8,10},{9,11},{10,... | collective-permute-start | bytes 663560 | tf_op jit(solution)/shard_map/ppermute | solution.py:338
  116.8 2.9 %copy-start.2 = (bf16[6,48,384]{2,1,0:T(8,128)(2,1)}, bf16[6,48,384]{2,1,0:T(8,128)(2,1)S(1)}, u32[]{:S(2)}) copy-start(bf16[6,48,384]{2,1,0:T(8,128)(2,1)S(1)} %fusion.1.refs_2_) | copy-start | bytes 663556
  116.8 7.2 %collective-permute-start.16 = (bf16[6,48,384]{2,1,0:T(8,128)(2,1)S(1)}, bf16[6,48,384]{2,1,0:T(8,128)(2,1)S(1)}, u32[]{:S(2)}, u32[]{:S(2)}) collective-permute-start(bf16[6,48,384]{2,1,0:T(8,128)(2,1)S(1)} %fusion.1.refs_2_), channel_id=1, source_target_pairs={{0,4},{4,0},{8,12},{12,8},{16,20},{20,16},{24,28},{28,24},{1,5},{5... | collective-permute-start | bytes 663560 | tf_op jit(solution)/shard_map/ppermute | solution.py:405
  119.8 4.3 %copy-start.3 = (bf16[6,48,384]{2,1,0:T(8,128)(2,1)}, bf16[6,48,384]{2,1,0:T(8,128)(2,1)S(1)}, u32[]{:S(2)}) copy-start(bf16[6,48,384]{2,1,0:T(8,128)(2,1)S(1)} %fusion.refs_0_) | copy-start | bytes 663556
  119.8 9.1 %collective-permute-start.9 = (bf16[6,48,384]{2,1,0:T(8,128)(2,1)S(1)}, bf16[6,48,384]{2,1,0:T(8,128)(2,1)}, u32[]{:S(2)}, u32[]{:S(2)}) collective-permute-start(bf16[6,48,384]{2,1,0:T(8,128)(2,1)S(1)} %fusion.refs_0_), channel_id=1, source_target_pairs={{0,4},{4,0},{8,12},{12,8},{16,20},{20,16},{24,28},{28,24},{1,5},{5... | collective-permute-start | bytes 663560 | tf_op jit(solution)/shard_map/ppermute | solution.py:405
  123.0 9.0 %collective-permute-start.23 = (bf16[4,48,384]{2,1,0:T(8,128)(2,1)}, bf16[4,48,384]{2,1,0:T(8,128)(2,1)}, u32[]{:S(2)}, u32[]{:S(2)}) collective-permute-start(bf16[4,48,384]{2,1,0:T(8,128)(2,1)} %fusion.2.mine), channel_id=1, source_target_pairs={{0,4},{4,0},{8,12},{12,8},{16,20},{20,16},{24,28},{28,24},{1,5},{5... | collective-permute-start | bytes 442376 | tf_op jit(solution)/shard_map/ppermute | solution.py:405
  124.0 0.7 copy-start.5
  134.9 5.4 %collective-permute-start.25 = (bf16[1,4,48,384]{3,2,1,0:T(8,128)(2,1)}, bf16[1,4,48,384]{3,2,1,0:T(8,128)(2,1)S(1)}, u32[]{:S(2)}, u32[]{:S(2)}) collective-permute-start(bf16[1,4,48,384]{3,2,1,0:T(8,128)(2,1)} %get-tuple-element.34), channel_id=1, source_target_pairs={{0,8},{4,12},{8,0},{12,4},{16,24},{20,28},{24,16},{28,20},{1,9},{5... | collective-permute-start | bytes 442376 | tf_op jit(solution)/shard_map/ppermute | solution.py:335
  136.5 8.2 %collective-permute-start.24 = (bf16[1,4,48,384]{3,2,1,0:T(8,128)(2,1)}, bf16[1,4,48,384]{3,2,1,0:T(8,128)(2,1)S(1)}, u32[]{:S(2)}, u32[]{:S(2)}) collective-permute-start(bf16[1,4,48,384]{3,2,1,0:T(8,128)(2,1)} %get-tuple-element.33), channel_id=1, source_target_pairs={{0,8},{4,12},{8,0},{12,4},{16,24},{20,28},{24,16},{28,20},{1,9},{5... | collective-permute-start | bytes 442376 | tf_op jit(solution)/shard_map/ppermute | solution.py:336
  142.1 7.6 %collective-permute-start.26 = (bf16[1,4,48,384]{3,2,1,0:T(8,128)(2,1)S(1)}, bf16[1,4,48,384]{3,2,1,0:T(8,128)(2,1)S(1)}, u32[]{:S(2)}, u32[]{:S(2)}) collective-permute-start(bf16[1,4,48,384]{3,2,1,0:T(8,128)(2,1)S(1)} %get-tuple-element.35), channel_id=1, source_target_pairs={{0,16},{4,20},{8,24},{12,28},{16,0},{20,4},{24,8},{28,12},{1,17},{... | collective-permute-start | bytes 442376 | tf_op jit(solution)/shard_map/ppermute | solution.py:338
  144.6 5.0 %copy-start.6 = (bf16[1,4,48,384]{3,2,1,0:T(8,128)(2,1)}, bf16[1,4,48,384]{3,2,1,0:T(8,128)(2,1)S(1)}, u32[]{:S(2)}) copy-start(bf16[1,4,48,384]{3,2,1,0:T(8,128)(2,1)S(1)} %collective-permute-done.24.refs_0_) | copy-start | bytes 442372
  149.7 0.7 copy-start.7

commit v3 on v2

--- a/solution.py
+++ b/solution.py
@@ -13,7 +13,7 @@
 G_DEV = 8
 OMEGA = 0.6
 
-EDGES = (0, 6, 12, 16)
+EDGES = (0, 8, 12, 16)
 STEP = 2
 
 
@@ -328,22 +328,21 @@
 
 
 def exchange(keep, send, axis, count, bit, link):
-    terms = [keep]
+    terms = [(keep, 1)]
     while True:
         route = flip(count, bit)
         if isinstance(send, tuple):
             odd = lax.ppermute(send[0], axis, route)
-            even = lax.ppermute(send[1], axis, route)
+            arrived = (lax.ppermute(send[1], axis, route), 1)
         else:
-            even = lax.ppermute(send, axis, route)
-            if 2 * bit < count:
-                even, odd = even[0::2], even[1::2]
+            arrived = (lax.ppermute(send, axis, route), 2)
+            odd = arrived[0][1::2]
         bit *= 2
         if bit == count:
-            return terms + [even]
-        send = sum(term[1::2].astype(jnp.float32) for term in terms)
-        send = (send + odd.astype(jnp.float32)).astype(link)
-        terms = [term[0::2] for term in terms] + [even]
+            return [term for term, _ in terms] + [arrived[0]]
+        leave = sum(term[stride :: 2 * stride].astype(jnp.float32) for term, stride in terms)
+        send = (leave + odd.astype(jnp.float32)).astype(link)
+        terms = [(term, 2 * stride) for term, stride in terms] + [arrived]
 
 
 def on_device(

time: 153 us -> 150 us (0.980)
    ppermute x8, waiting for transfers between devices: 12.8 us -> 11 us  [the longest x7 11 us: exchange(): arrived = (lax.ppermute(send, axis, route), 2)]
    convert_element_type x4, other arithmetic: 5.01 us -> 3.41 us  [exchange(): send = (leave + odd.astype(jnp.float32)).astype(link)]
    ppermute x7, starting transfers between devices: 4.01 us -> 2.48 us  [both(): near_a = lax.ppermute(block, 'col', pair_a)]
  transfers between devices with their start and end apart: 27 -> 27, of which waited for: 10 -> 11; matrix products, arithmetic and copies ran while one was open for 8% -> 7% of each run, Pallas kernels for 27% -> 22%
where the time goes in v3:
time: 150 us; the launch traced here: 149 us
  waiting for transfers between devices  67.7 us (45%)
  Pallas kernels  44.7 us (30%)
  starting transfers between devices  24.7 us (16%)
  other arithmetic  10.6 us (7%)
    ppermute x7, waiting for transfers between devices, both(): near_b = lax.ppermute(block, 'col', pair_b)  47.3 us
    pallas_call x3, Pallas kernels, coarse_rows(): pl.pallas_call(functools.partial(coarse_kernel, first), grid=(count // st...  16.5 us
    pallas_call x3, Pallas kernels, prolong_rows(): pl.pallas_call(functools.partial(prolong_kernel, first), grid=(count // s...  15.8 us
    ppermute x7, waiting for transfers between devices, exchange(): arrived = (lax.ppermute(send, axis, route), 2)  11 us
    ppermute x7, starting transfers between devices, exchange(): arrived = (lax.ppermute(send, axis, route), 2)  7.91 us
    ppermute x7, starting transfers between devices, both(): near_b = lax.ppermute(block, 'col', pair_b)  6.29 us
    ppermute x3, waiting for transfers between devices, on_device(): other = lax.ppermute(total, 'row', flip(rows, 1))  5.88 us
    pallas_call x2, Pallas kernels, pack_rows(): pl.pallas_call(functools.partial(pack_kernel, 0 if whole else first), gri...  4.53 us
  transfers between devices with their start and end apart: 27, of which 11 were waited for; matrix products, arithmetic and copies ran while one was open for 7% of the time, Pallas kernels for 22%

profile of v3, /device:TPU:0, one launch (start us, length us, event | category | flops | bytes accessed | tf_op | source)
XLA Modules:
  0.0 149.1 jit_solution(9066126317684755966)
XLA Ops:
  0.0 2.4 %collective-permute-start.1 = (s32[64]{0:T(128)}, s32[64]{0:T(128)}, u32[]{:S(2)}, u32[]{:S(2)}) collective-permute-start(s32[64]{0:T(128)} %param.15), channel_id=1, source_target_pairs={{0,3},{1,2},{2,1},{3,0},{4,7},{5,6},{6,5},{7,4},{8,11},{9,10},{10,... | collective-permute-start | bytes 776 | tf_op jit(solution)/shard_map/ppermute | solution.py:373
  2.4 0.7 collective-permute-start
  3.1 2.3 %shard_map.91 = bf16[8,96,384]{2,1,0:T(8,128)(2,1)} custom-call(bf16[64,96,96]{2,1,0:T(8,128)(2,1)} %own.5), custom_call_target="tpu_custom_call" | custom-call | bytes 1474560 | tf_op jit(solution)/shard_map/pallas_call | solution.py:52
  5.4 0.7 bitcast_add_fusion
  6.1 2.1 %collective-permute-start.2 = (s32[32]{0:T(128)S(1)}, s32[32]{0:T(128)S(1)}, u32[]{:S(2)}, u32[]{:S(2)}) collective-permute-start(s32[32]{0:T(128)S(1)} %bitcast_add_fusion), channel_id=1, source_target_pairs={{0,4},{4,0},{8,12},{12,8},{16,20},{20,16},{24,28},{28,24},{1,5},{5... | collective-permute-start | bytes 392 | tf_op jit(solution)/shard_map/ppermute | solution.py:383
  8.2 1.3 fusion.6.table
  9.5 0.6 pad_add_fusion.2.place
  10.8 1.3 pad_add_fusion.labels
  12.0 8.7 %collective-permute-done.4.near_b = bf16[8,96,384]{2,1,0:T(8,128)(2,1)} collective-permute-done((bf16[8,96,384]{2,1,0:T(8,128)(2,1)}, bf16[8,96,384]{2,1,0:T(8,128)(2,1)}, u32[]{:S(2)}, u32[]{:S(2)}) %collective-permute-start.4) | collective-permute-done | bytes 589856 | tf_op jit(solution)/shard_map/ppermute | solution.py:373
  20.7 7.0 %shard_map.92.own = bf16[16,96,384]{2,1,0:T(8,128)(2,1)} custom-call(s32[4,64]{1,0:T(4,128)} %fusion.6.table, s32[3,64]{1,0:T(4,128)} %pad_add_fusion.labels, bf16[64,4,96,96]{3,2,1,0:T(8,128)(2,1)} %off.11, bf16[64,96,96]{2,1,0:T(8,128)(2,1)} %diag.11, bf16[64,96,96]{2,1,0:T(8,128)(2,1)} %inverse.5, bf16[64,96,96]{2,1,0:T(8,128)(2,1)} %own.5, ...), custom_call_target="tpu_custom_call" | custom-call | flops 679477248 | bytes 6488064 | tf_op jit(solution)/shard_map/pallas_call | solution.py:123
  28.7 2.2 %shard_map.94 = (bf16[4,96,384]{2,1,0:T(8,128)(2,1)}, bf16[4,96,384]{2,1,0:T(8,128)(2,1)}) custom-call(bf16[64,96,96]{2,1,0:T(8,128)(2,1)} %own.5), custom_call_target="tpu_custom_call" | custom-call | bytes 1474560 | tf_op jit(solution)/shard_map/pallas_call | solution.py:52
  31.1 1.2 collective-permute-start.11
  32.9 1.3 collective-permute-start.18
  34.1 28.8 %collective-permute-done.11.near_b = bf16[4,96,384]{2,1,0:T(8,128)(2,1)} collective-permute-done((bf16[4,96,384]{2,1,0:T(8,128)(2,1)}, bf16[4,96,384]{2,1,0:T(8,128)(2,1)}, u32[]{:S(2)}, u32[]{:S(2)}) %collective-permute-start.11) | collective-permute-done | bytes 294944 | tf_op jit(solution)/shard_map/ppermute | solution.py:373
  62.9 4.4 %shard_map.95.own = bf16[8,96,384]{2,1,0:T(8,128)(2,1)} custom-call(s32[4,64]{1,0:T(4,128)} %fusion.6.table, s32[3,64]{1,0:T(4,128)} %pad_add_fusion.labels, bf16[64,4,96,96]{3,2,1,0:T(8,128)(2,1)} %off.11, bf16[64,96,96]{2,1,0:T(8,128)(2,1)} %diag.11, bf16[64,96,96]{2,1,0:T(8,128)(2,1)} %inverse.5, bf16[64,96,96]{2,1,0:T(8,128)(2,1)} %own.5, ...), custom_call_target="tpu_custom_call" | custom-call | flops 339738624 | bytes 3244032 | tf_op jit(solution)/shard_map/pallas_call | solution.py:123
  67.3 0.6 collective-permute-start.12
  68.4 0.8 collective-permute-done.18.near_b
  69.2 4.4 %shard_map.98.own = bf16[8,96,384]{2,1,0:T(8,128)(2,1)} custom-call(s32[4,64]{1,0:T(4,128)} %fusion.6.table, s32[3,64]{1,0:T(4,128)} %pad_add_fusion.labels, bf16[64,4,96,96]{3,2,1,0:T(8,128)(2,1)} %off.11, bf16[64,96,96]{2,1,0:T(8,128)(2,1)} %diag.11, bf16[64,96,96]{2,1,0:T(8,128)(2,1)} %inverse.5, bf16[64,96,96]{2,1,0:T(8,128)(2,1)} %own.5, ...), custom_call_target="tpu_custom_call" | custom-call | flops 339738624 | bytes 3244032 | tf_op jit(solution)/shard_map/pallas_call | solution.py:123
  74.1 7.4 %shard_map.93 = (f32[2,8,48,384]{3,2,1,0:T(8,128)}, bf16[2,8,48,384]{3,2,1,0:T(8,128)(2,1)}) custom-call(s32[4,64]{1,0:T(4,128)} %fusion.6.table, s32[2]{0:T(128)} %pad_add_fusion.2.place, bf16[64,4,96,96]{3,2,1,0:T(8,128)(2,1)} %off.11, bf16[64,96,96]{2,1,0:T(8,128)(2,1)} %diag.11, bf16[16,96,384]{2,1,0:T(8,128)(2,1)} %shard_map.92.own, ...), custom_call_target="tpu_custom_call" | custom-call | flops 792723456 | bytes 9437184 | tf_op jit(solution)/shard_map/pallas_call | solution.py:205
  82.0 1.6 %collective-permute-done.13.near_b = bf16[8,96,384]{2,1,0:T(8,128)(2,1)} collective-permute-done((bf16[8,96,384]{2,1,0:T(8,128)(2,1)}, bf16[8,96,384]{2,1,0:T(8,128)(2,1)}, u32[]{:S(2)}, u32[]{:S(2)}) %collective-permute-start.13) | collective-permute-done | bytes 589856 | tf_op jit(solution)/shard_map/ppermute | solution.py:373
  83.6 4.5 %shard_map.96 = (f32[2,4,48,384]{3,2,1,0:T(8,128)}, bf16[2,4,48,384]{3,2,1,0:T(8,128)(2,1)}) custom-call(s32[4,64]{1,0:T(4,128)} %fusion.6.table, s32[2]{0:T(128)} %pad_add_fusion.2.place, bf16[64,4,96,96]{3,2,1,0:T(8,128)(2,1)} %off.11, bf16[64,96,96]{2,1,0:T(8,128)(2,1)} %diag.11, bf16[8,96,384]{2,1,0:T(8,128)(2,1)} %shard_map.95.own, ...), custom_call_target="tpu_custom_call" | custom-call | flops 396361728 | bytes 4718592 | tf_op jit(solution)/shard_map/pallas_call | solution.py:205
  88.1 0.6 collective-permute-start.14
  88.7 7.5 %collective-permute-done.20.near_b = bf16[8,96,384]{2,1,0:T(8,128)(2,1)} collective-permute-done((bf16[8,96,384]{2,1,0:T(8,128)(2,1)}, bf16[8,96,384]{2,1,0:T(8,128)(2,1)}, u32[]{:S(2)}, u32[]{:S(2)}) %collective-permute-start.20) | collective-permute-done | bytes 589856 | tf_op jit(solution)/shard_map/ppermute | solution.py:373
  96.2 4.6 %shard_map.99 = (f32[2,4,48,384]{3,2,1,0:T(8,128)}, bf16[2,4,48,384]{3,2,1,0:T(8,128)(2,1)}) custom-call(s32[4,64]{1,0:T(4,128)} %fusion.6.table, s32[2]{0:T(128)} %pad_add_fusion.2.place, bf16[64,4,96,96]{3,2,1,0:T(8,128)(2,1)} %off.11, bf16[64,96,96]{2,1,0:T(8,128)(2,1)} %diag.11, bf16[8,96,384]{2,1,0:T(8,128)(2,1)} %shard_map.98.own, ...), custom_call_target="tpu_custom_call" | custom-call | flops 396361728 | bytes 4718592 | tf_op jit(solution)/shard_map/pallas_call | solution.py:205
  101.0 1.1 add_convert_fusion.6
  102.0 0.9 collective-permute-start.15
  103.0 1.3 add_convert_fusion.1
  104.3 1.3 collective-permute-start.8
  105.6 0.9 collective-permute-start.22
  106.4 2.4 %collective-permute-done.15 = bf16[1,4,48,384]{3,2,1,0:T(8,128)(2,1)S(1)} collective-permute-done((bf16[1,4,48,384]{3,2,1,0:T(8,128)(2,1)S(1)}, bf16[1,4,48,384]{3,2,1,0:T(8,128)(2,1)S(1)}, u32[]{:S(2)}, u32[]{:S(2)}) %collective-permute-start.15) | collective-permute-done | bytes 147488 | tf_op jit(solution)/shard_map/ppermute | solution.py:338
  108.8 1.0 fusion.1.refs_2_
  109.8 1.6 %collective-permute-start.16 = (bf16[4,48,384]{2,1,0:T(8,128)(2,1)S(1)}, bf16[4,48,384]{2,1,0:T(8,128)(2,1)S(1)}, u32[]{:S(2)}, u32[]{:S(2)}) collective-permute-start(bf16[4,48,384]{2,1,0:T(8,128)(2,1)S(1)} %fusion.1.refs_2_), channel_id=1, source_target_pairs={{0,4},{4,0},{8,12},{12,8},{16,20},{20,16},{24,28},{28,24},{1,5},{5... | collective-permute-start | bytes 442376 | tf_op jit(solution)/shard_map/ppermute | solution.py:404
  111.4 3.8 %collective-permute-done.8 = bf16[1,8,48,384]{3,2,1,0:T(8,128)(2,1)S(1)} collective-permute-done((bf16[1,8,48,384]{3,2,1,0:T(8,128)(2,1)S(1)}, bf16[1,8,48,384]{3,2,1,0:T(8,128)(2,1)S(1)}, u32[]{:S(2)}, u32[]{:S(2)}) %collective-permute-start.8) | collective-permute-done | bytes 294944 | tf_op jit(solution)/shard_map/ppermute | solution.py:338
  115.2 1.1 fusion.refs_0_
  116.2 0.7 copy-done
  116.9 1.5 %collective-permute-start.9 = (bf16[8,48,384]{2,1,0:T(8,128)(2,1)S(1)}, bf16[8,48,384]{2,1,0:T(8,128)(2,1)}, u32[]{:S(2)}, u32[]{:S(2)}) collective-permute-start(bf16[8,48,384]{2,1,0:T(8,128)(2,1)S(1)} %fusion.refs_0_), channel_id=1, source_target_pairs={{0,4},{4,0},{8,12},{12,8},{16,20},{20,16},{24,28},{28,24},{1,5},{5... | collective-permute-start | bytes 884744 | tf_op jit(solution)/shard_map/ppermute | solution.py:404
  118.4 0.7 fusion.2.mine
  119.1 0.8 collective-permute-start.23
  120.0 0.7 copy-done.5
  120.6 5.9 %collective-permute-done.9.refs_1_ = bf16[8,48,384]{2,1,0:T(8,128)(2,1)} collective-permute-done((bf16[8,48,384]{2,1,0:T(8,128)(2,1)S(1)}, bf16[8,48,384]{2,1,0:T(8,128)(2,1)}, u32[]{:S(2)}, u32[]{:S(2)}) %collective-permute-start.9) | collective-permute-done | bytes 294944 | tf_op jit(solution)/shard_map/ppermute | solution.py:404
  126.5 3.0 %shard_map.97.early = f32[33,48,192]{2,1,0:T(8,128)} custom-call(s32[2,32]{1,0:T(2,128)} %pad_add_fusion.1.targets, s32[2]{0:T(128)} %pad_add_fusion.2.place, bf16[8,48,384]{2,1,0:T(8,128)(2,1)} %copy-done, bf16[8,48,384]{2,1,0:T(8,128)(2,1)} %collective-permute-done.9.refs_1_, bf16[4,48,384]{2,1,0:T(8,128)(2,1)} %copy-done.2, bf16[4,48,384]{2,1,0:T(8,128)(2,1)} %copy-done.5), custom_call_target="tpu_custom_call" | custom-call | flops 442368 | bytes 1769472 | tf_op jit(solution)/shard_map/pallas_call | solution.py:262
  129.5 2.9 %shard_map.100 = (f32[2,4,48,384]{3,2,1,0:T(8,128)}, bf16[1,4,48,384]{3,2,1,0:T(8,128)(2,1)}, bf16[1,4,48,384]{3,2,1,0:T(8,128)(2,1)}) custom-call(s32[2,32]{1,0:T(2,128)} %pad_add_fusion.1.targets, s32[2]{0:T(128)} %pad_add_fusion.2.place, f32[33,48,192]{2,1,0:T(8,128)} %shard_map.97.early, bf16[4,48,384]{2,1,0:T(8,128)(2,1)} %fusion.2.mine, ...), custom_call_target="tpu_custom_call" | custom-call | flops 304128 | bytes 3041280 | tf_op jit(solution)/shard_map/pallas_call | solution.py:290
  132.4 1.6 %collective-permute-start.25 = (bf16[1,4,48,384]{3,2,1,0:T(8,128)(2,1)}, bf16[1,4,48,384]{3,2,1,0:T(8,128)(2,1)S(1)}, u32[]{:S(2)}, u32[]{:S(2)}) collective-permute-start(bf16[1,4,48,384]{3,2,1,0:T(8,128)(2,1)} %get-tuple-element.34), channel_id=1, source_target_pairs={{0,8},{4,12},{8,0},{12,4},{16,24},{20,28},{24,16},{28,20},{1,9},{5... | collective-permute-start | bytes 442376 | tf_op jit(solution)/shard_map/ppermute | solution.py:335
  134.4 3.3 %collective-permute-done.25 = bf16[1,4,48,384]{3,2,1,0:T(8,128)(2,1)S(1)} collective-permute-done((bf16[1,4,48,384]{3,2,1,0:T(8,128)(2,1)}, bf16[1,4,48,384]{3,2,1,0:T(8,128)(2,1)S(1)}, u32[]{:S(2)}, u32[]{:S(2)}) %collective-permute-start.25) | collective-permute-done | bytes 147488 | tf_op jit(solution)/shard_map/ppermute | solution.py:335
  137.8 1.0 add_convert_fusion.2
  138.8 3.6 %collective-permute-start.26 = (bf16[1,4,48,384]{3,2,1,0:T(8,128)(2,1)S(1)}, bf16[1,4,48,384]{3,2,1,0:T(8,128)(2,1)}, u32[]{:S(2)}, u32[]{:S(2)}) collective-permute-start(bf16[1,4,48,384]{3,2,1,0:T(8,128)(2,1)S(1)} %add_convert_fusion.2), channel_id=1, source_target_pairs={{0,16},{4,20},{8,24},{12,28},{16,0},{20,4},{24,8},{28,12},{1,17},{... | collective-permute-start | bytes 442376 | tf_op jit(solution)/shard_map/ppermute | solution.py:338
  142.4 4.8 %collective-permute-done.26.refs_1_ = bf16[1,4,48,384]{3,2,1,0:T(8,128)(2,1)} collective-permute-done((bf16[1,4,48,384]{3,2,1,0:T(8,128)(2,1)S(1)}, bf16[1,4,48,384]{3,2,1,0:T(8,128)(2,1)}, u32[]{:S(2)}, u32[]{:S(2)}) %collective-permute-start.26) | collective-permute-done | bytes 147488 | tf_op jit(solution)/shard_map/ppermute | solution.py:338
  147.2 1.9 %shard_map.101 = f32[8,48,192]{2,1,0:T(8,128)} custom-call(f32[2,4,48,384]{3,2,1,0:T(8,128)} %get-tuple-element.32.keep_ref, bf16[1,4,48,384]{3,2,1,0:T(8,128)(2,1)} %collective-permute-done.24.refs_0_, bf16[1,4,48,384]{3,2,1,0:T(8,128)(2,1)} %collective-permute-done.26.refs_1_), custom_call_target="tpu_custom_call" | custom-call | flops 73728 | bytes 737280 | tf_op jit(solution)/shard_map/pallas_call | solution.py:315
  (41 shorter events, 4.5 us)
Async XLA Ops:
  0.0 10.7 %collective-permute-start.1 = (s32[64]{0:T(128)}, s32[64]{0:T(128)}, u32[]{:S(2)}, u32[]{:S(2)}) collective-permute-start(s32[64]{0:T(128)} %param.15), channel_id=1, source_target_pairs={{0,3},{1,2},{2,1},{3,0},{4,7},{5,6},{6,5},{7,4},{8,11},{9,10},{10,... | collective-permute-start | bytes 776 | tf_op jit(solution)/shard_map/ppermute | solution.py:373
  2.4 8.3 %collective-permute-start = (s32[64]{0:T(128)}, s32[64]{0:T(128)}, u32[]{:S(2)}, u32[]{:S(2)}) collective-permute-start(s32[64]{0:T(128)} %param.15), channel_id=1, source_target_pairs={{0,1},{1,0},{2,3},{3,2},{4,5},{5,4},{6,7},{7,6},{8,9},{9,8},{10,11... | collective-permute-start | bytes 776 | tf_op jit(solution)/shard_map/ppermute | solution.py:374
  5.4 6.6 %collective-permute-start.3 = (bf16[8,96,384]{2,1,0:T(8,128)(2,1)}, bf16[8,96,384]{2,1,0:T(8,128)(2,1)}, u32[]{:S(2)}, u32[]{:S(2)}) collective-permute-start(bf16[8,96,384]{2,1,0:T(8,128)(2,1)} %shard_map.91), channel_id=1, source_target_pairs={{0,1},{1,0},{2,3},{3,2},{4,5},{5,4},{6,7},{7,6},{8,9},{9,8},{10,11... | collective-permute-start | bytes 1769480 | tf_op jit(solution)/shard_map/ppermute | solution.py:374
  5.4 15.3 %collective-permute-start.4 = (bf16[8,96,384]{2,1,0:T(8,128)(2,1)}, bf16[8,96,384]{2,1,0:T(8,128)(2,1)}, u32[]{:S(2)}, u32[]{:S(2)}) collective-permute-start(bf16[8,96,384]{2,1,0:T(8,128)(2,1)} %shard_map.91), channel_id=1, source_target_pairs={{0,3},{1,2},{2,1},{3,0},{4,7},{5,6},{6,5},{7,4},{8,11},{9,10},{10,... | collective-permute-start | bytes 1769480 | tf_op jit(solution)/shard_map/ppermute | solution.py:373
  6.1 4.0 %collective-permute-start.2 = (s32[32]{0:T(128)S(1)}, s32[32]{0:T(128)S(1)}, u32[]{:S(2)}, u32[]{:S(2)}) collective-permute-start(s32[32]{0:T(128)S(1)} %bitcast_add_fusion), channel_id=1, source_target_pairs={{0,4},{4,0},{8,12},{12,8},{16,20},{20,16},{24,28},{28,24},{1,5},{5... | collective-permute-start | bytes 392 | tf_op jit(solution)/shard_map/ppermute | solution.py:383
  27.7 46.0 %collective-permute-start.5 = (bf16[16,96,384]{2,1,0:T(8,128)(2,1)}, bf16[16,96,384]{2,1,0:T(8,128)(2,1)}, u32[]{:S(2)}, u32[]{:S(2)}) collective-permute-start(bf16[16,96,384]{2,1,0:T(8,128)(2,1)} %shard_map.92.own), channel_id=1, source_target_pairs={{0,1},{1,0},{2,3},{3,2},{4,5},{5,4},{6,7},{7,6},{8,9},{9,8},{10,11... | collective-permute-start | bytes 3538952 | tf_op jit(solution)/shard_map/ppermute | solution.py:374
  28.2 45.9 %collective-permute-start.6 = (bf16[16,96,384]{2,1,0:T(8,128)(2,1)}, bf16[16,96,384]{2,1,0:T(8,128)(2,1)}, u32[]{:S(2)}, u32[]{:S(2)}) collective-permute-start(bf16[16,96,384]{2,1,0:T(8,128)(2,1)} %shard_map.92.own), channel_id=1, source_target_pairs={{0,3},{1,2},{2,1},{3,0},{4,7},{5,6},{6,5},{7,4},{8,11},{9,10},{10,... | collective-permute-start | bytes 3538952 | tf_op jit(solution)/shard_map/ppermute | solution.py:373
  30.9 1.9 %collective-permute-start.10 = (bf16[4,96,384]{2,1,0:T(8,128)(2,1)}, bf16[4,96,384]{2,1,0:T(8,128)(2,1)}, u32[]{:S(2)}, u32[]{:S(2)}) collective-permute-start(bf16[4,96,384]{2,1,0:T(8,128)(2,1)} %get-tuple-element.26), channel_id=1, source_target_pairs={{0,1},{1,0},{2,3},{3,2},{4,5},{5,4},{6,7},{7,6},{8,9},{9,8},{10,11... | collective-permute-start | bytes 884744 | tf_op jit(solution)/shard_map/ppermute | solution.py:374
  31.1 31.8 %collective-permute-start.11 = (bf16[4,96,384]{2,1,0:T(8,128)(2,1)}, bf16[4,96,384]{2,1,0:T(8,128)(2,1)}, u32[]{:S(2)}, u32[]{:S(2)}) collective-permute-start(bf16[4,96,384]{2,1,0:T(8,128)(2,1)} %get-tuple-element.26), channel_id=1, source_target_pairs={{0,3},{1,2},{2,1},{3,0},{4,7},{5,6},{6,5},{7,4},{8,11},{9,10},{10,... | collective-permute-start | bytes 884744 | tf_op jit(solution)/shard_map/ppermute | solution.py:373
  32.3 35.6 %collective-permute-start.17 = (bf16[4,96,384]{2,1,0:T(8,128)(2,1)}, bf16[4,96,384]{2,1,0:T(8,128)(2,1)}, u32[]{:S(2)}, u32[]{:S(2)}) collective-permute-start(bf16[4,96,384]{2,1,0:T(8,128)(2,1)} %get-tuple-element.29), channel_id=1, source_target_pairs={{0,1},{1,0},{2,3},{3,2},{4,5},{5,4},{6,7},{7,6},{8,9},{9,8},{10,11... | collective-permute-start | bytes 884744 | tf_op jit(solution)/shard_map/ppermute | solution.py:374
  32.9 36.3 %collective-permute-start.18 = (bf16[4,96,384]{2,1,0:T(8,128)(2,1)}, bf16[4,96,384]{2,1,0:T(8,128)(2,1)}, u32[]{:S(2)}, u32[]{:S(2)}) collective-permute-start(bf16[4,96,384]{2,1,0:T(8,128)(2,1)} %get-tuple-element.29), channel_id=1, source_target_pairs={{0,3},{1,2},{2,1},{3,0},{4,7},{5,6},{6,5},{7,4},{8,11},{9,10},{10,... | collective-permute-start | bytes 884744 | tf_op jit(solution)/shard_map/ppermute | solution.py:373
  67.3 14.7 %collective-permute-start.12 = (bf16[8,96,384]{2,1,0:T(8,128)(2,1)}, bf16[8,96,384]{2,1,0:T(8,128)(2,1)}, u32[]{:S(2)}, u32[]{:S(2)}) collective-permute-start(bf16[8,96,384]{2,1,0:T(8,128)(2,1)} %shard_map.95.own), channel_id=1, source_target_pairs={{0,1},{1,0},{2,3},{3,2},{4,5},{5,4},{6,7},{7,6},{8,9},{9,8},{10,11... | collective-permute-start | bytes 1769480 | tf_op jit(solution)/shard_map/ppermute | solution.py:374
  67.9 15.7 %collective-permute-start.13 = (bf16[8,96,384]{2,1,0:T(8,128)(2,1)}, bf16[8,96,384]{2,1,0:T(8,128)(2,1)}, u32[]{:S(2)}, u32[]{:S(2)}) collective-permute-start(bf16[8,96,384]{2,1,0:T(8,128)(2,1)} %shard_map.95.own), channel_id=1, source_target_pairs={{0,3},{1,2},{2,1},{3,0},{4,7},{5,6},{6,5},{7,4},{8,11},{9,10},{10,... | collective-permute-start | bytes 1769480 | tf_op jit(solution)/shard_map/ppermute | solution.py:373
  73.6 15.1 %collective-permute-start.19 = (bf16[8,96,384]{2,1,0:T(8,128)(2,1)}, bf16[8,96,384]{2,1,0:T(8,128)(2,1)}, u32[]{:S(2)}, u32[]{:S(2)}) collective-permute-start(bf16[8,96,384]{2,1,0:T(8,128)(2,1)} %shard_map.98.own), channel_id=1, source_target_pairs={{0,1},{1,0},{2,3},{3,2},{4,5},{5,4},{6,7},{7,6},{8,9},{9,8},{10,11... | collective-permute-start | bytes 1769480 | tf_op jit(solution)/shard_map/ppermute | solution.py:374
  73.7 22.5 %collective-permute-start.20 = (bf16[8,96,384]{2,1,0:T(8,128)(2,1)}, bf16[8,96,384]{2,1,0:T(8,128)(2,1)}, u32[]{:S(2)}, u32[]{:S(2)}) collective-permute-start(bf16[8,96,384]{2,1,0:T(8,128)(2,1)} %shard_map.98.own), channel_id=1, source_target_pairs={{0,3},{1,2},{2,1},{3,0},{4,7},{5,6},{6,5},{7,4},{8,11},{9,10},{10,... | collective-permute-start | bytes 1769480 | tf_op jit(solution)/shard_map/ppermute | solution.py:373
  81.5 21.4 %collective-permute-start.7 = (bf16[2,8,48,384]{3,2,1,0:T(8,128)(2,1)}, bf16[2,8,48,384]{3,2,1,0:T(8,128)(2,1)}, u32[]{:S(2)}, u32[]{:S(2)}) collective-permute-start(bf16[2,8,48,384]{3,2,1,0:T(8,128)(2,1)} %get-tuple-element.25), channel_id=1, source_target_pairs={{0,1},{1,0},{2,3},{3,2},{4,5},{5,4},{6,7},{7,6},{8,9},{9,8},{10,11... | collective-permute-start | bytes 1769480 | tf_op jit(solution)/shard_map/ppermute | solution.py:338
  88.1 12.9 %collective-permute-start.14 = (bf16[2,4,48,384]{3,2,1,0:T(8,128)(2,1)}, bf16[2,4,48,384]{3,2,1,0:T(8,128)(2,1)}, u32[]{:S(2)}, u32[]{:S(2)}) collective-permute-start(bf16[2,4,48,384]{3,2,1,0:T(8,128)(2,1)} %get-tuple-element.28), channel_id=1, source_target_pairs={{0,1},{1,0},{2,3},{3,2},{4,5},{5,4},{6,7},{7,6},{8,9},{9,8},{10,11... | collective-permute-start | bytes 884744 | tf_op jit(solution)/shard_map/ppermute | solution.py:338
  100.8 4.7 %copy-start.3 = (f32[2,4,48,384]{3,2,1,0:T(8,128)S(1)}, f32[2,4,48,384]{3,2,1,0:T(8,128)}, u32[]{:S(2)}) copy-start(f32[2,4,48,384]{3,2,1,0:T(8,128)} %get-tuple-element.30) | copy-start | bytes 1769476
  100.8 4.7 %collective-permute-start.21 = (bf16[2,4,48,384]{3,2,1,0:T(8,128)(2,1)}, bf16[2,4,48,384]{3,2,1,0:T(8,128)(2,1)S(1)}, u32[]{:S(2)}, u32[]{:S(2)}) collective-permute-start(bf16[2,4,48,384]{3,2,1,0:T(8,128)(2,1)} %get-tuple-element.31), channel_id=1, source_target_pairs={{0,1},{1,0},{2,3},{3,2},{4,5},{5,4},{6,7},{7,6},{8,9},{9,8},{10,11... | collective-permute-start | bytes 884744 | tf_op jit(solution)/shard_map/ppermute | solution.py:338
  101.0 7.9 %copy-start.4 = (f32[2,4,48,384]{3,2,1,0:T(8,128)S(1)}, f32[2,4,48,384]{3,2,1,0:T(8,128)}, u32[]{:S(2)}) copy-start(f32[2,4,48,384]{3,2,1,0:T(8,128)} %get-tuple-element.27) | copy-start | bytes 1769476
  102.0 6.8 %collective-permute-start.15 = (bf16[1,4,48,384]{3,2,1,0:T(8,128)(2,1)S(1)}, bf16[1,4,48,384]{3,2,1,0:T(8,128)(2,1)S(1)}, u32[]{:S(2)}, u32[]{:S(2)}) collective-permute-start(bf16[1,4,48,384]{3,2,1,0:T(8,128)(2,1)S(1)} %add_convert_fusion.6), channel_id=1, source_target_pairs={{0,2},{1,3},{2,0},{3,1},{4,6},{5,7},{6,4},{7,5},{8,10},{9,11},{10,... | collective-permute-start | bytes 442376 | tf_op jit(solution)/shard_map/ppermute | solution.py:338
  103.0 12.2 %copy-start.1 = (f32[2,8,48,384]{3,2,1,0:T(8,128)S(1)}, f32[2,8,48,384]{3,2,1,0:T(8,128)}, u32[]{:S(2)}) copy-start(f32[2,8,48,384]{3,2,1,0:T(8,128)} %get-tuple-element.24) | copy-start | bytes 3538948
  104.3 10.9 %collective-permute-start.8 = (bf16[1,8,48,384]{3,2,1,0:T(8,128)(2,1)S(1)}, bf16[1,8,48,384]{3,2,1,0:T(8,128)(2,1)S(1)}, u32[]{:S(2)}, u32[]{:S(2)}) collective-permute-start(bf16[1,8,48,384]{3,2,1,0:T(8,128)(2,1)S(1)} %add_convert_fusion.1), channel_id=1, source_target_pairs={{0,2},{1,3},{2,0},{3,1},{4,6},{5,7},{6,4},{7,5},{8,10},{9,11},{10,... | collective-permute-start | bytes 884744 | tf_op jit(solution)/shard_map/ppermute | solution.py:338
  105.6 12.9 %collective-permute-start.22 = (bf16[1,4,48,384]{3,2,1,0:T(8,128)(2,1)S(1)}, bf16[1,4,48,384]{3,2,1,0:T(8,128)(2,1)S(1)}, u32[]{:S(2)}, u32[]{:S(2)}) collective-permute-start(bf16[1,4,48,384]{3,2,1,0:T(8,128)(2,1)S(1)} %add_convert_fusion.4), channel_id=1, source_target_pairs={{0,2},{1,3},{2,0},{3,1},{4,6},{5,7},{6,4},{7,5},{8,10},{9,11},{10,... | collective-permute-start | bytes 442376 | tf_op jit(solution)/shard_map/ppermute | solution.py:338
  109.8 8.6 %copy-start.2 = (bf16[4,48,384]{2,1,0:T(8,128)(2,1)}, bf16[4,48,384]{2,1,0:T(8,128)(2,1)S(1)}, u32[]{:S(2)}) copy-start(bf16[4,48,384]{2,1,0:T(8,128)(2,1)S(1)} %fusion.1.refs_2_) | copy-start | bytes 442372
  109.8 10.1 %collective-permute-start.16 = (bf16[4,48,384]{2,1,0:T(8,128)(2,1)S(1)}, bf16[4,48,384]{2,1,0:T(8,128)(2,1)S(1)}, u32[]{:S(2)}, u32[]{:S(2)}) collective-permute-start(bf16[4,48,384]{2,1,0:T(8,128)(2,1)S(1)} %fusion.1.refs_2_), channel_id=1, source_target_pairs={{0,4},{4,0},{8,12},{12,8},{16,20},{20,16},{24,28},{28,24},{1,5},{5... | collective-permute-start | bytes 442376 | tf_op jit(solution)/shard_map/ppermute | solution.py:404
  116.2 0.7 copy-start
  116.9 9.6 %collective-permute-start.9 = (bf16[8,48,384]{2,1,0:T(8,128)(2,1)S(1)}, bf16[8,48,384]{2,1,0:T(8,128)(2,1)}, u32[]{:S(2)}, u32[]{:S(2)}) collective-permute-start(bf16[8,48,384]{2,1,0:T(8,128)(2,1)S(1)} %fusion.refs_0_), channel_id=1, source_target_pairs={{0,4},{4,0},{8,12},{12,8},{16,20},{20,16},{24,28},{28,24},{1,5},{5... | collective-permute-start | bytes 884744 | tf_op jit(solution)/shard_map/ppermute | solution.py:404
  119.1 10.4 %collective-permute-start.23 = (bf16[4,48,384]{2,1,0:T(8,128)(2,1)}, bf16[4,48,384]{2,1,0:T(8,128)(2,1)}, u32[]{:S(2)}, u32[]{:S(2)}) collective-permute-start(bf16[4,48,384]{2,1,0:T(8,128)(2,1)} %fusion.2.mine), channel_id=1, source_target_pairs={{0,4},{4,0},{8,12},{12,8},{16,20},{20,16},{24,28},{28,24},{1,5},{5... | collective-permute-start | bytes 442376 | tf_op jit(solution)/shard_map/ppermute | solution.py:404
  120.0 0.7 copy-start.5
  132.4 5.4 %collective-permute-start.25 = (bf16[1,4,48,384]{3,2,1,0:T(8,128)(2,1)}, bf16[1,4,48,384]{3,2,1,0:T(8,128)(2,1)S(1)}, u32[]{:S(2)}, u32[]{:S(2)}) collective-permute-start(bf16[1,4,48,384]{3,2,1,0:T(8,128)(2,1)} %get-tuple-element.34), channel_id=1, source_target_pairs={{0,8},{4,12},{8,0},{12,4},{16,24},{20,28},{24,16},{28,20},{1,9},{5... | collective-permute-start | bytes 442376 | tf_op jit(solution)/shard_map/ppermute | solution.py:335
  134.0 8.4 %collective-permute-start.24 = (bf16[1,4,48,384]{3,2,1,0:T(8,128)(2,1)}, bf16[1,4,48,384]{3,2,1,0:T(8,128)(2,1)}, u32[]{:S(2)}, u32[]{:S(2)}) collective-permute-start(bf16[1,4,48,384]{3,2,1,0:T(8,128)(2,1)} %get-tuple-element.33), channel_id=1, source_target_pairs={{0,8},{4,12},{8,0},{12,4},{16,24},{20,28},{24,16},{28,20},{1,9},{5... | collective-permute-start | bytes 442376 | tf_op jit(solution)/shard_map/ppermute | solution.py:336
  138.8 8.4 %collective-permute-start.26 = (bf16[1,4,48,384]{3,2,1,0:T(8,128)(2,1)S(1)}, bf16[1,4,48,384]{3,2,1,0:T(8,128)(2,1)}, u32[]{:S(2)}, u32[]{:S(2)}) collective-permute-start(bf16[1,4,48,384]{3,2,1,0:T(8,128)(2,1)S(1)} %add_convert_fusion.2), channel_id=1, source_target_pairs={{0,16},{4,20},{8,24},{12,28},{16,0},{20,4},{24,8},{28,12},{1,17},{... | collective-permute-start | bytes 442376 | tf_op jit(solution)/shard_map/ppermute | solution.py:338

commit v4 on v3

--- a/solution.py
+++ b/solution.py
@@ -13,12 +13,14 @@
 G_DEV = 8
 OMEGA = 0.6
 
-EDGES = (0, 8, 12, 16)
+EDGES = (0, 4, 12, 16)
 STEP = 2
 
 
 VMEM = pl.BlockSpec(memory_space=pltpu.VMEM)
 SMEM = pl.BlockSpec(memory_space=pltpu.SMEM)
+ANY = pl.BlockSpec(memory_space=pl.ANY)
+SMALL = pltpu.CompilerParams(vmem_limit_bytes=50331648)
 PARAMS = pltpu.CompilerParams(vmem_limit_bytes=67043328)
 
 
@@ -247,11 +249,25 @@
             one(m)
 
 
+def bring(sources, buffers, sems):
+    copies = [
+        pltpu.make_async_copy(source, buffer, sems.at[i])
+        for i, (source, buffer) in enumerate(zip(sources, buffers))
+    ]
+    for copy in copies:
+        copy.start()
+    return copies
+
+
 def gather_kernel(starts, targets, place, *refs):
-    sums = refs[-1]
+    count = 2 * len(starts)
+    sources, sums, buffers, sems = refs[:count], refs[count], refs[count + 1 : -1], refs[-1]
+    copies = bring(sources, buffers, sems)
     sums[...] = jnp.zeros_like(sums)
     for part, first in enumerate(starts):
-        add_groups(targets, place, refs[2 * part : 2 * part + 2], first, sums)
+        for copy in copies[2 * part : 2 * part + 2]:
+            copy.wait()
+        add_groups(targets, place, buffers[2 * part : 2 * part + 2], first, sums)
 
 
 def gather_groups(targets, place, parts, starts, rows):
@@ -261,17 +277,21 @@
     total = sum(array.size for array in flat)
     return pl.pallas_call(
         functools.partial(gather_kernel, starts),
-        in_specs=[SMEM, SMEM] + [VMEM] * len(flat),
+        in_specs=[SMEM, SMEM] + [ANY] * len(flat),
         out_specs=VMEM,
         out_shape=jax.ShapeDtypeStruct(shape, jnp.float32),
-        compiler_params=PARAMS,
+        scratch_shapes=[pltpu.VMEM(array.shape, array.dtype) for array in flat]
+        + [pltpu.SemaphoreType.DMA((len(flat),))],
+        compiler_params=SMALL,
         cost_estimate=cost(total, 4 * total),
     )(targets, place, *flat)
 
 
-def split_kernel(first, targets, place, early, mine, theirs, keep, odd, even, sums):
-    sums[...] = early[...]
-    add_groups(targets, place, (mine, theirs), first, sums)
+def split_kernel(first, targets, place, early, mine, theirs, keep, odd, even, sums, *scratch):
+    buffers, sems = scratch[:-1], scratch[-1]
+    for copy in bring((early, mine, theirs), (sums,) + buffers, sems):
+        copy.wait()
+    add_groups(targets, place, buffers, first, sums)
     window = sums.shape[2]
     for h in range(keep.shape[0]):
         send = odd if h % 2 else even
@@ -289,11 +309,16 @@
     half = jax.ShapeDtypeStruct((rows // 8,) + shape[1:], mine.dtype)
     return pl.pallas_call(
         functools.partial(split_kernel, first),
-        in_specs=[SMEM, SMEM, VMEM, VMEM, VMEM],
+        in_specs=[SMEM, SMEM, ANY, ANY, ANY],
         out_specs=[VMEM, VMEM, VMEM],
         out_shape=[jax.ShapeDtypeStruct(shape, jnp.float32), half, half],
-        scratch_shapes=[pltpu.VMEM(early.shape, jnp.float32)],
-        compiler_params=PARAMS,
+        scratch_shapes=[
+            pltpu.VMEM(early.shape, jnp.float32),
+            pltpu.VMEM(mine.shape, mine.dtype),
+            pltpu.VMEM(theirs.shape, theirs.dtype),
+            pltpu.SemaphoreType.DMA((3,)),
+        ],
+        compiler_params=SMALL,
         cost_estimate=cost(early.size, 10 * early.size),
     )(targets, place, early, mine, theirs)
 

time: 150 us -> 146 us (0.973)
  Pallas kernels: 44.7 us -> 42.3 us
  other arithmetic: 10.6 us -> 8.92 us
  transfers between devices with their start and end apart: 27 -> 27, of which waited for: 11 -> 11; matrix products, arithmetic and copies ran while one was open for 7% -> 6% of each run, Pallas kernels for 22% -> 22%
where the time goes in v4:
time: 146 us; the launch traced here: 145 us
  waiting for transfers between devices  67.7 us (46%)
  Pallas kernels  42.3 us (29%)
  starting transfers between devices  25.3 us (17%)
  other arithmetic  8.92 us (6%)
    ppermute x7, waiting for transfers between devices, both(): near_b = lax.ppermute(block, 'col', pair_b)  47.7 us
    pallas_call x3, Pallas kernels, coarse_rows(): pl.pallas_call(functools.partial(coarse_kernel, first), grid=(count // st...  16.5 us
    pallas_call x3, Pallas kernels, prolong_rows(): pl.pallas_call(functools.partial(prolong_kernel, first), grid=(count // s...  15.8 us
    ppermute x7, waiting for transfers between devices, exchange(): arrived = (lax.ppermute(send, axis, route), 2)  10.3 us
    ppermute x7, starting transfers between devices, exchange(): arrived = (lax.ppermute(send, axis, route), 2)  7.74 us
    ppermute x7, starting transfers between devices, both(): near_b = lax.ppermute(block, 'col', pair_b)  6.46 us
    ppermute x3, waiting for transfers between devices, on_device(): other = lax.ppermute(total, 'row', flip(rows, 1))  6.39 us
    ppermute x3, starting transfers between devices, on_device(): other = lax.ppermute(total, 'row', flip(rows, 1))  4.64 us
  transfers between devices with their start and end apart: 27, of which 11 were waited for; matrix products, arithmetic and copies ran while one was open for 6% of the time, Pallas kernels for 22%

profile of v4, /device:TPU:0, one launch (start us, length us, event | category | flops | bytes accessed | tf_op | source)
XLA Modules:
  0.0 145.0 jit_solution(464641934708731084)
XLA Ops:
  0.5 2.6 %collective-permute-start.1 = (s32[64]{0:T(128)}, s32[64]{0:T(128)}, u32[]{:S(2)}, u32[]{:S(2)}) collective-permute-start(s32[64]{0:T(128)} %param.15), channel_id=1, source_target_pairs={{0,3},{1,2},{2,1},{3,0},{4,7},{5,6},{6,5},{7,4},{8,11},{9,10},{10,... | collective-permute-start | bytes 776 | tf_op jit(solution)/shard_map/ppermute | solution.py:398
  3.1 2.7 %shard_map.94 = (bf16[8,96,384]{2,1,0:T(8,128)(2,1)}, bf16[4,96,384]{2,1,0:T(8,128)(2,1)}) custom-call(bf16[64,96,96]{2,1,0:T(8,128)(2,1)} %own.5), custom_call_target="tpu_custom_call" | custom-call | bytes 2211840 | tf_op jit(solution)/shard_map/pallas_call | solution.py:54
  5.8 0.7 bitcast_add_fusion
  6.5 2.1 %collective-permute-start.2 = (s32[32]{0:T(128)S(1)}, s32[32]{0:T(128)S(1)}, u32[]{:S(2)}, u32[]{:S(2)}) collective-permute-start(s32[32]{0:T(128)S(1)} %bitcast_add_fusion), channel_id=1, source_target_pairs={{0,4},{4,0},{8,12},{12,8},{16,20},{20,16},{24,28},{28,24},{1,5},{5... | collective-permute-start | bytes 392 | tf_op jit(solution)/shard_map/ppermute | solution.py:408
  8.6 1.3 fusion.6.table
  9.9 0.6 pad_add_fusion.2.place
  10.5 0.6 pad_add_fusion.1.targets
  11.1 1.3 pad_add_fusion.labels
  12.3 8.7 %collective-permute-done.11.near_b = bf16[8,96,384]{2,1,0:T(8,128)(2,1)} collective-permute-done((bf16[8,96,384]{2,1,0:T(8,128)(2,1)}, bf16[8,96,384]{2,1,0:T(8,128)(2,1)}, u32[]{:S(2)}, u32[]{:S(2)}) %collective-permute-start.11) | collective-permute-done | bytes 589856 | tf_op jit(solution)/shard_map/ppermute | solution.py:398
  21.1 7.0 %shard_map.95.own = bf16[16,96,384]{2,1,0:T(8,128)(2,1)} custom-call(s32[4,64]{1,0:T(4,128)} %fusion.6.table, s32[3,64]{1,0:T(4,128)} %pad_add_fusion.labels, bf16[64,4,96,96]{3,2,1,0:T(8,128)(2,1)} %off.11, bf16[64,96,96]{2,1,0:T(8,128)(2,1)} %diag.11, bf16[64,96,96]{2,1,0:T(8,128)(2,1)} %inverse.5, bf16[64,96,96]{2,1,0:T(8,128)(2,1)} %own.5, ...), custom_call_target="tpu_custom_call" | custom-call | flops 679477248 | bytes 6488064 | tf_op jit(solution)/shard_map/pallas_call | solution.py:125
  28.1 0.5 collective-permute-start.12
  28.6 0.5 collective-permute-start.13
  29.1 1.9 %shard_map.91 = bf16[4,96,384]{2,1,0:T(8,128)(2,1)} custom-call(bf16[64,96,96]{2,1,0:T(8,128)(2,1)} %own.5), custom_call_target="tpu_custom_call" | custom-call | bytes 737280 | tf_op jit(solution)/shard_map/pallas_call | solution.py:54
  31.1 1.2 collective-permute-start.4
  33.0 1.2 collective-permute-start.18
  34.2 29.1 %collective-permute-done.4.near_b = bf16[4,96,384]{2,1,0:T(8,128)(2,1)} collective-permute-done((bf16[4,96,384]{2,1,0:T(8,128)(2,1)}, bf16[4,96,384]{2,1,0:T(8,128)(2,1)}, u32[]{:S(2)}, u32[]{:S(2)}) %collective-permute-start.4) | collective-permute-done | bytes 294944 | tf_op jit(solution)/shard_map/ppermute | solution.py:398
  63.2 4.4 %shard_map.92.own = bf16[8,96,384]{2,1,0:T(8,128)(2,1)} custom-call(s32[4,64]{1,0:T(4,128)} %fusion.6.table, s32[3,64]{1,0:T(4,128)} %pad_add_fusion.labels, bf16[64,4,96,96]{3,2,1,0:T(8,128)(2,1)} %off.11, bf16[64,96,96]{2,1,0:T(8,128)(2,1)} %diag.11, bf16[64,96,96]{2,1,0:T(8,128)(2,1)} %inverse.5, bf16[64,96,96]{2,1,0:T(8,128)(2,1)} %own.5, ...), custom_call_target="tpu_custom_call" | custom-call | flops 339738624 | bytes 3244032 | tf_op jit(solution)/shard_map/pallas_call | solution.py:125
  67.6 0.6 collective-permute-start.5
  68.2 0.5 collective-permute-start.6
  68.8 0.8 collective-permute-done.18.near_b
  69.6 4.4 %shard_map.98.own = bf16[8,96,384]{2,1,0:T(8,128)(2,1)} custom-call(s32[4,64]{1,0:T(4,128)} %fusion.6.table, s32[3,64]{1,0:T(4,128)} %pad_add_fusion.labels, bf16[64,4,96,96]{3,2,1,0:T(8,128)(2,1)} %off.11, bf16[64,96,96]{2,1,0:T(8,128)(2,1)} %diag.11, bf16[64,96,96]{2,1,0:T(8,128)(2,1)} %inverse.5, bf16[64,96,96]{2,1,0:T(8,128)(2,1)} %own.5, ...), custom_call_target="tpu_custom_call" | custom-call | flops 339738624 | bytes 3244032 | tf_op jit(solution)/shard_map/pallas_call | solution.py:125
  74.5 7.4 %shard_map.96 = (f32[2,8,48,384]{3,2,1,0:T(8,128)}, bf16[2,8,48,384]{3,2,1,0:T(8,128)(2,1)}) custom-call(s32[4,64]{1,0:T(4,128)} %fusion.6.table, s32[2]{0:T(128)} %pad_add_fusion.2.place, bf16[64,4,96,96]{3,2,1,0:T(8,128)(2,1)} %off.11, bf16[64,96,96]{2,1,0:T(8,128)(2,1)} %diag.11, bf16[16,96,384]{2,1,0:T(8,128)(2,1)} %shard_map.95.own, ...), custom_call_target="tpu_custom_call" | custom-call | flops 792723456 | bytes 9437184 | tf_op jit(solution)/shard_map/pallas_call | solution.py:207
  82.3 1.6 %collective-permute-done.6.near_b = bf16[8,96,384]{2,1,0:T(8,128)(2,1)} collective-permute-done((bf16[8,96,384]{2,1,0:T(8,128)(2,1)}, bf16[8,96,384]{2,1,0:T(8,128)(2,1)}, u32[]{:S(2)}, u32[]{:S(2)}) %collective-permute-start.6) | collective-permute-done | bytes 589856 | tf_op jit(solution)/shard_map/ppermute | solution.py:398
  83.9 4.5 %shard_map.93 = (f32[2,4,48,384]{3,2,1,0:T(8,128)}, bf16[2,4,48,384]{3,2,1,0:T(8,128)(2,1)}) custom-call(s32[4,64]{1,0:T(4,128)} %fusion.6.table, s32[2]{0:T(128)} %pad_add_fusion.2.place, bf16[64,4,96,96]{3,2,1,0:T(8,128)(2,1)} %off.11, bf16[64,96,96]{2,1,0:T(8,128)(2,1)} %diag.11, bf16[8,96,384]{2,1,0:T(8,128)(2,1)} %shard_map.92.own, ...), custom_call_target="tpu_custom_call" | custom-call | flops 396361728 | bytes 4718592 | tf_op jit(solution)/shard_map/pallas_call | solution.py:207
  88.4 0.6 collective-permute-start.7
  89.1 7.5 %collective-permute-done.20.near_b = bf16[8,96,384]{2,1,0:T(8,128)(2,1)} collective-permute-done((bf16[8,96,384]{2,1,0:T(8,128)(2,1)}, bf16[8,96,384]{2,1,0:T(8,128)(2,1)}, u32[]{:S(2)}, u32[]{:S(2)}) %collective-permute-start.20) | collective-permute-done | bytes 589856 | tf_op jit(solution)/shard_map/ppermute | solution.py:398
  96.6 4.6 %shard_map.99 = (f32[2,4,48,384]{3,2,1,0:T(8,128)}, bf16[2,4,48,384]{3,2,1,0:T(8,128)(2,1)}) custom-call(s32[4,64]{1,0:T(4,128)} %fusion.6.table, s32[2]{0:T(128)} %pad_add_fusion.2.place, bf16[64,4,96,96]{3,2,1,0:T(8,128)(2,1)} %off.11, bf16[64,96,96]{2,1,0:T(8,128)(2,1)} %diag.11, bf16[8,96,384]{2,1,0:T(8,128)(2,1)} %shard_map.98.own, ...), custom_call_target="tpu_custom_call" | custom-call | flops 396361728 | bytes 4718592 | tf_op jit(solution)/shard_map/pallas_call | solution.py:207
  101.3 1.1 add_convert_fusion.6
  102.4 0.9 collective-permute-start.8
  103.3 1.3 add_convert_fusion.1
  104.6 1.3 collective-permute-start.15
  105.9 0.9 collective-permute-start.22
  106.8 2.4 %collective-permute-done.8 = bf16[1,4,48,384]{3,2,1,0:T(8,128)(2,1)S(1)} collective-permute-done((bf16[1,4,48,384]{3,2,1,0:T(8,128)(2,1)S(1)}, bf16[1,4,48,384]{3,2,1,0:T(8,128)(2,1)S(1)}, u32[]{:S(2)}, u32[]{:S(2)}) %collective-permute-start.8) | collective-permute-done | bytes 147488 | tf_op jit(solution)/shard_map/ppermute | solution.py:363
  109.2 1.0 fusion.1.refs_0_
  110.2 1.6 %collective-permute-start.9 = (bf16[4,48,384]{2,1,0:T(8,128)(2,1)S(1)}, bf16[4,48,384]{2,1,0:T(8,128)(2,1)S(1)}, u32[]{:S(2)}, u32[]{:S(2)}) collective-permute-start(bf16[4,48,384]{2,1,0:T(8,128)(2,1)S(1)} %fusion.1.refs_0_), channel_id=1, source_target_pairs={{0,4},{4,0},{8,12},{12,8},{16,20},{20,16},{24,28},{28,24},{1,5},{5... | collective-permute-start | bytes 442376 | tf_op jit(solution)/shard_map/ppermute | solution.py:429
  111.8 3.8 %collective-permute-done.15 = bf16[1,8,48,384]{3,2,1,0:T(8,128)(2,1)S(1)} collective-permute-done((bf16[1,8,48,384]{3,2,1,0:T(8,128)(2,1)S(1)}, bf16[1,8,48,384]{3,2,1,0:T(8,128)(2,1)S(1)}, u32[]{:S(2)}, u32[]{:S(2)}) %collective-permute-start.15) | collective-permute-done | bytes 294944 | tf_op jit(solution)/shard_map/ppermute | solution.py:363
  115.5 1.1 fusion.refs_2_
  116.6 1.6 %collective-permute-start.16 = (bf16[8,48,384]{2,1,0:T(8,128)(2,1)S(1)}, bf16[8,48,384]{2,1,0:T(8,128)(2,1)S(1)}, u32[]{:S(2)}, u32[]{:S(2)}) collective-permute-start(bf16[8,48,384]{2,1,0:T(8,128)(2,1)S(1)} %fusion.refs_2_), channel_id=1, source_target_pairs={{0,4},{4,0},{8,12},{12,8},{16,20},{20,16},{24,28},{28,24},{1,5},{5... | collective-permute-start | bytes 884744 | tf_op jit(solution)/shard_map/ppermute | solution.py:429
  118.2 1.5 %collective-permute-start.23 = (bf16[4,48,384]{2,1,0:T(8,128)(2,1)S(1)}, bf16[4,48,384]{2,1,0:T(8,128)(2,1)S(1)}, u32[]{:S(2)}, u32[]{:S(2)}) collective-permute-start(bf16[4,48,384]{2,1,0:T(8,128)(2,1)S(1)} %fusion.2.mine), channel_id=1, source_target_pairs={{0,4},{4,0},{8,12},{12,8},{16,20},{20,16},{24,28},{28,24},{1,5},{5... | collective-permute-start | bytes 442376 | tf_op jit(solution)/shard_map/ppermute | solution.py:429
  119.7 6.4 %collective-permute-done.16.refs_3_ = bf16[8,48,384]{2,1,0:T(8,128)(2,1)S(1)} collective-permute-done((bf16[8,48,384]{2,1,0:T(8,128)(2,1)S(1)}, bf16[8,48,384]{2,1,0:T(8,128)(2,1)S(1)}, u32[]{:S(2)}, u32[]{:S(2)}) %collective-permute-start.16) | collective-permute-done | bytes 294944 | tf_op jit(solution)/shard_map/ppermute | solution.py:429
  126.1 1.9 %shard_map.97.early = f32[33,48,192]{2,1,0:T(8,128)S(1)} custom-call(s32[2,32]{1,0:T(2,128)S(1)} %copy-done.2, s32[2]{0:T(128)S(1)} %copy-done.1, bf16[4,48,384]{2,1,0:T(8,128)(2,1)S(1)} %fusion.1.refs_0_, bf16[4,48,384]{2,1,0:T(8,128)(2,1)S(1)} %collective-permute-done.9.refs_1_, bf16[8,48,384]{2,1,0:T(8,128)(2,1)S(1)} %fusion.refs_2_, ...), custom_call_target="tpu_custom_call" | custom-call | flops 442368 | bytes 1769472 | tf_op jit(solution)/shard_map/pallas_call | solution.py:278
  128.0 1.6 %shard_map.100 = (f32[2,4,48,384]{3,2,1,0:T(8,128)S(1)}, bf16[1,4,48,384]{3,2,1,0:T(8,128)(2,1)S(1)}, bf16[1,4,48,384]{3,2,1,0:T(8,128)(2,1)S(1)}) custom-call(s32[2,32]{1,0:T(2,128)S(1)} %copy-done.2, s32[2]{0:T(128)S(1)} %copy-done.1, f32[33,48,192]{2,1,0:T(8,128)S(1)} %shard_map.97.early, bf16[4,48,384]{2,1,0:T(8,128)(2,1)S(1)} %fusion.2.mine, ...), custom_call_target="tpu_custom_call" | custom-call | flops 304128 | bytes 3041280 | tf_op jit(solution)/shard_map/pallas_call | solution.py:310
  129.6 1.7 %collective-permute-start.25 = (bf16[1,4,48,384]{3,2,1,0:T(8,128)(2,1)S(1)}, bf16[1,4,48,384]{3,2,1,0:T(8,128)(2,1)S(1)}, u32[]{:S(2)}, u32[]{:S(2)}) collective-permute-start(bf16[1,4,48,384]{3,2,1,0:T(8,128)(2,1)S(1)} %get-tuple-element.34), channel_id=1, source_target_pairs={{0,8},{4,12},{8,0},{12,4},{16,24},{20,28},{24,16},{28,20},{1,9},{5... | collective-permute-start | bytes 442376 | tf_op jit(solution)/shard_map/ppermute | solution.py:360
  131.7 3.1 %collective-permute-done.25 = bf16[1,4,48,384]{3,2,1,0:T(8,128)(2,1)S(1)} collective-permute-done((bf16[1,4,48,384]{3,2,1,0:T(8,128)(2,1)S(1)}, bf16[1,4,48,384]{3,2,1,0:T(8,128)(2,1)S(1)}, u32[]{:S(2)}, u32[]{:S(2)}) %collective-permute-start.25) | collective-permute-done | bytes 147488 | tf_op jit(solution)/shard_map/ppermute | solution.py:360
  134.8 3.4 %collective-permute-start.26 = (bf16[1,4,48,384]{3,2,1,0:T(8,128)(2,1)S(1)}, bf16[1,4,48,384]{3,2,1,0:T(8,128)(2,1)}, u32[]{:S(2)}, u32[]{:S(2)}) collective-permute-start(bf16[1,4,48,384]{3,2,1,0:T(8,128)(2,1)S(1)} %add_convert_fusion.2), channel_id=1, source_target_pairs={{0,16},{4,20},{8,24},{12,28},{16,0},{20,4},{24,8},{28,12},{1,17},{... | collective-permute-start | bytes 442376 | tf_op jit(solution)/shard_map/ppermute | solution.py:363
  138.3 0.7 copy-done.6
  138.9 4.1 %collective-permute-done.26.refs_1_ = bf16[1,4,48,384]{3,2,1,0:T(8,128)(2,1)} collective-permute-done((bf16[1,4,48,384]{3,2,1,0:T(8,128)(2,1)S(1)}, bf16[1,4,48,384]{3,2,1,0:T(8,128)(2,1)}, u32[]{:S(2)}, u32[]{:S(2)}) %collective-permute-start.26) | collective-permute-done | bytes 147488 | tf_op jit(solution)/shard_map/ppermute | solution.py:363
  143.1 1.9 %shard_map.101 = f32[8,48,192]{2,1,0:T(8,128)} custom-call(f32[2,4,48,384]{3,2,1,0:T(8,128)} %copy-done, bf16[1,4,48,384]{3,2,1,0:T(8,128)(2,1)} %copy-done.6, bf16[1,4,48,384]{3,2,1,0:T(8,128)(2,1)} %collective-permute-done.26.refs_1_), custom_call_target="tpu_custom_call" | custom-call | flops 73728 | bytes 737280 | tf_op jit(solution)/shard_map/pallas_call | solution.py:340
  (43 shorter events, 3.0 us)
Async XLA Ops:
  0.0 11.1 %collective-permute-start = (s32[64]{0:T(128)}, s32[64]{0:T(128)}, u32[]{:S(2)}, u32[]{:S(2)}) collective-permute-start(s32[64]{0:T(128)} %param.15), channel_id=1, source_target_pairs={{0,1},{1,0},{2,3},{3,2},{4,5},{5,4},{6,7},{7,6},{8,9},{9,8},{10,11... | collective-permute-start | bytes 776 | tf_op jit(solution)/shard_map/ppermute | solution.py:399
  0.5 10.6 %collective-permute-start.1 = (s32[64]{0:T(128)}, s32[64]{0:T(128)}, u32[]{:S(2)}, u32[]{:S(2)}) collective-permute-start(s32[64]{0:T(128)} %param.15), channel_id=1, source_target_pairs={{0,3},{1,2},{2,1},{3,0},{4,7},{5,6},{6,5},{7,4},{8,11},{9,10},{10,... | collective-permute-start | bytes 776 | tf_op jit(solution)/shard_map/ppermute | solution.py:398
  5.8 6.5 %collective-permute-start.10 = (bf16[8,96,384]{2,1,0:T(8,128)(2,1)}, bf16[8,96,384]{2,1,0:T(8,128)(2,1)}, u32[]{:S(2)}, u32[]{:S(2)}) collective-permute-start(bf16[8,96,384]{2,1,0:T(8,128)(2,1)} %get-tuple-element.26), channel_id=1, source_target_pairs={{0,1},{1,0},{2,3},{3,2},{4,5},{5,4},{6,7},{7,6},{8,9},{9,8},{10,11... | collective-permute-start | bytes 1769480 | tf_op jit(solution)/shard_map/ppermute | solution.py:399
  5.8 15.3 %collective-permute-start.11 = (bf16[8,96,384]{2,1,0:T(8,128)(2,1)}, bf16[8,96,384]{2,1,0:T(8,128)(2,1)}, u32[]{:S(2)}, u32[]{:S(2)}) collective-permute-start(bf16[8,96,384]{2,1,0:T(8,128)(2,1)} %get-tuple-element.26), channel_id=1, source_target_pairs={{0,3},{1,2},{2,1},{3,0},{4,7},{5,6},{6,5},{7,4},{8,11},{9,10},{10,... | collective-permute-start | bytes 1769480 | tf_op jit(solution)/shard_map/ppermute | solution.py:398
  6.5 4.0 %collective-permute-start.2 = (s32[32]{0:T(128)S(1)}, s32[32]{0:T(128)S(1)}, u32[]{:S(2)}, u32[]{:S(2)}) collective-permute-start(s32[32]{0:T(128)S(1)} %bitcast_add_fusion), channel_id=1, source_target_pairs={{0,4},{4,0},{8,12},{12,8},{16,20},{20,16},{24,28},{28,24},{1,5},{5... | collective-permute-start | bytes 392 | tf_op jit(solution)/shard_map/ppermute | solution.py:408
  28.1 46.0 %collective-permute-start.12 = (bf16[16,96,384]{2,1,0:T(8,128)(2,1)}, bf16[16,96,384]{2,1,0:T(8,128)(2,1)}, u32[]{:S(2)}, u32[]{:S(2)}) collective-permute-start(bf16[16,96,384]{2,1,0:T(8,128)(2,1)} %shard_map.95.own), channel_id=1, source_target_pairs={{0,1},{1,0},{2,3},{3,2},{4,5},{5,4},{6,7},{7,6},{8,9},{9,8},{10,11... | collective-permute-start | bytes 3538952 | tf_op jit(solution)/shard_map/ppermute | solution.py:399
  28.6 45.9 %collective-permute-start.13 = (bf16[16,96,384]{2,1,0:T(8,128)(2,1)}, bf16[16,96,384]{2,1,0:T(8,128)(2,1)}, u32[]{:S(2)}, u32[]{:S(2)}) collective-permute-start(bf16[16,96,384]{2,1,0:T(8,128)(2,1)} %shard_map.95.own), channel_id=1, source_target_pairs={{0,3},{1,2},{2,1},{3,0},{4,7},{5,6},{6,5},{7,4},{8,11},{9,10},{10,... | collective-permute-start | bytes 3538952 | tf_op jit(solution)/shard_map/ppermute | solution.py:398
  31.0 1.9 %collective-permute-start.3 = (bf16[4,96,384]{2,1,0:T(8,128)(2,1)}, bf16[4,96,384]{2,1,0:T(8,128)(2,1)}, u32[]{:S(2)}, u32[]{:S(2)}) collective-permute-start(bf16[4,96,384]{2,1,0:T(8,128)(2,1)} %shard_map.91), channel_id=1, source_target_pairs={{0,1},{1,0},{2,3},{3,2},{4,5},{5,4},{6,7},{7,6},{8,9},{9,8},{10,11... | collective-permute-start | bytes 884744 | tf_op jit(solution)/shard_map/ppermute | solution.py:399
  31.1 32.1 %collective-permute-start.4 = (bf16[4,96,384]{2,1,0:T(8,128)(2,1)}, bf16[4,96,384]{2,1,0:T(8,128)(2,1)}, u32[]{:S(2)}, u32[]{:S(2)}) collective-permute-start(bf16[4,96,384]{2,1,0:T(8,128)(2,1)} %shard_map.91), channel_id=1, source_target_pairs={{0,3},{1,2},{2,1},{3,0},{4,7},{5,6},{6,5},{7,4},{8,11},{9,10},{10,... | collective-permute-start | bytes 884744 | tf_op jit(solution)/shard_map/ppermute | solution.py:398
  32.3 35.9 %collective-permute-start.17 = (bf16[4,96,384]{2,1,0:T(8,128)(2,1)}, bf16[4,96,384]{2,1,0:T(8,128)(2,1)}, u32[]{:S(2)}, u32[]{:S(2)}) collective-permute-start(bf16[4,96,384]{2,1,0:T(8,128)(2,1)} %get-tuple-element.29), channel_id=1, source_target_pairs={{0,1},{1,0},{2,3},{3,2},{4,5},{5,4},{6,7},{7,6},{8,9},{9,8},{10,11... | collective-permute-start | bytes 884744 | tf_op jit(solution)/shard_map/ppermute | solution.py:399
  33.0 36.6 %collective-permute-start.18 = (bf16[4,96,384]{2,1,0:T(8,128)(2,1)}, bf16[4,96,384]{2,1,0:T(8,128)(2,1)}, u32[]{:S(2)}, u32[]{:S(2)}) collective-permute-start(bf16[4,96,384]{2,1,0:T(8,128)(2,1)} %get-tuple-element.29), channel_id=1, source_target_pairs={{0,3},{1,2},{2,1},{3,0},{4,7},{5,6},{6,5},{7,4},{8,11},{9,10},{10,... | collective-permute-start | bytes 884744 | tf_op jit(solution)/shard_map/ppermute | solution.py:398
  67.6 14.7 %collective-permute-start.5 = (bf16[8,96,384]{2,1,0:T(8,128)(2,1)}, bf16[8,96,384]{2,1,0:T(8,128)(2,1)}, u32[]{:S(2)}, u32[]{:S(2)}) collective-permute-start(bf16[8,96,384]{2,1,0:T(8,128)(2,1)} %shard_map.92.own), channel_id=1, source_target_pairs={{0,1},{1,0},{2,3},{3,2},{4,5},{5,4},{6,7},{7,6},{8,9},{9,8},{10,11... | collective-permute-start | bytes 1769480 | tf_op jit(solution)/shard_map/ppermute | solution.py:399
  68.2 15.7 %collective-permute-start.6 = (bf16[8,96,384]{2,1,0:T(8,128)(2,1)}, bf16[8,96,384]{2,1,0:T(8,128)(2,1)}, u32[]{:S(2)}, u32[]{:S(2)}) collective-permute-start(bf16[8,96,384]{2,1,0:T(8,128)(2,1)} %shard_map.92.own), channel_id=1, source_target_pairs={{0,3},{1,2},{2,1},{3,0},{4,7},{5,6},{6,5},{7,4},{8,11},{9,10},{10,... | collective-permute-start | bytes 1769480 | tf_op jit(solution)/shard_map/ppermute | solution.py:398
  74.0 15.1 %collective-permute-start.19 = (bf16[8,96,384]{2,1,0:T(8,128)(2,1)}, bf16[8,96,384]{2,1,0:T(8,128)(2,1)}, u32[]{:S(2)}, u32[]{:S(2)}) collective-permute-start(bf16[8,96,384]{2,1,0:T(8,128)(2,1)} %shard_map.98.own), channel_id=1, source_target_pairs={{0,1},{1,0},{2,3},{3,2},{4,5},{5,4},{6,7},{7,6},{8,9},{9,8},{10,11... | collective-permute-start | bytes 1769480 | tf_op jit(solution)/shard_map/ppermute | solution.py:399
  74.1 22.5 %collective-permute-start.20 = (bf16[8,96,384]{2,1,0:T(8,128)(2,1)}, bf16[8,96,384]{2,1,0:T(8,128)(2,1)}, u32[]{:S(2)}, u32[]{:S(2)}) collective-permute-start(bf16[8,96,384]{2,1,0:T(8,128)(2,1)} %shard_map.98.own), channel_id=1, source_target_pairs={{0,3},{1,2},{2,1},{3,0},{4,7},{5,6},{6,5},{7,4},{8,11},{9,10},{10,... | collective-permute-start | bytes 1769480 | tf_op jit(solution)/shard_map/ppermute | solution.py:398
  81.9 21.5 %collective-permute-start.14 = (bf16[2,8,48,384]{3,2,1,0:T(8,128)(2,1)}, bf16[2,8,48,384]{3,2,1,0:T(8,128)(2,1)}, u32[]{:S(2)}, u32[]{:S(2)}) collective-permute-start(bf16[2,8,48,384]{3,2,1,0:T(8,128)(2,1)} %get-tuple-element.28), channel_id=1, source_target_pairs={{0,1},{1,0},{2,3},{3,2},{4,5},{5,4},{6,7},{7,6},{8,9},{9,8},{10,11... | collective-permute-start | bytes 1769480 | tf_op jit(solution)/shard_map/ppermute | solution.py:363
  88.4 12.9 %collective-permute-start.7 = (bf16[2,4,48,384]{3,2,1,0:T(8,128)(2,1)}, bf16[2,4,48,384]{3,2,1,0:T(8,128)(2,1)}, u32[]{:S(2)}, u32[]{:S(2)}) collective-permute-start(bf16[2,4,48,384]{3,2,1,0:T(8,128)(2,1)} %get-tuple-element.25), channel_id=1, source_target_pairs={{0,1},{1,0},{2,3},{3,2},{4,5},{5,4},{6,7},{7,6},{8,9},{9,8},{10,11... | collective-permute-start | bytes 884744 | tf_op jit(solution)/shard_map/ppermute | solution.py:363
  101.2 4.7 %copy-start.4 = (f32[2,4,48,384]{3,2,1,0:T(8,128)S(1)}, f32[2,4,48,384]{3,2,1,0:T(8,128)}, u32[]{:S(2)}) copy-start(f32[2,4,48,384]{3,2,1,0:T(8,128)} %get-tuple-element.30) | copy-start | bytes 1769476
  101.2 4.7 %collective-permute-start.21 = (bf16[2,4,48,384]{3,2,1,0:T(8,128)(2,1)}, bf16[2,4,48,384]{3,2,1,0:T(8,128)(2,1)S(1)}, u32[]{:S(2)}, u32[]{:S(2)}) collective-permute-start(bf16[2,4,48,384]{3,2,1,0:T(8,128)(2,1)} %get-tuple-element.31), channel_id=1, source_target_pairs={{0,1},{1,0},{2,3},{3,2},{4,5},{5,4},{6,7},{7,6},{8,9},{9,8},{10,11... | collective-permute-start | bytes 884744 | tf_op jit(solution)/shard_map/ppermute | solution.py:363
  101.3 7.9 %copy-start.5 = (f32[2,4,48,384]{3,2,1,0:T(8,128)S(1)}, f32[2,4,48,384]{3,2,1,0:T(8,128)}, u32[]{:S(2)}) copy-start(f32[2,4,48,384]{3,2,1,0:T(8,128)} %get-tuple-element.24) | copy-start | bytes 1769476
  102.4 6.8 %collective-permute-start.8 = (bf16[1,4,48,384]{3,2,1,0:T(8,128)(2,1)S(1)}, bf16[1,4,48,384]{3,2,1,0:T(8,128)(2,1)S(1)}, u32[]{:S(2)}, u32[]{:S(2)}) collective-permute-start(bf16[1,4,48,384]{3,2,1,0:T(8,128)(2,1)S(1)} %add_convert_fusion.6), channel_id=1, source_target_pairs={{0,2},{1,3},{2,0},{3,1},{4,6},{5,7},{6,4},{7,5},{8,10},{9,11},{10,... | collective-permute-start | bytes 442376 | tf_op jit(solution)/shard_map/ppermute | solution.py:363
  103.3 12.2 %copy-start.3 = (f32[2,8,48,384]{3,2,1,0:T(8,128)S(1)}, f32[2,8,48,384]{3,2,1,0:T(8,128)}, u32[]{:S(2)}) copy-start(f32[2,8,48,384]{3,2,1,0:T(8,128)} %get-tuple-element.27) | copy-start | bytes 3538948
  104.6 10.9 %collective-permute-start.15 = (bf16[1,8,48,384]{3,2,1,0:T(8,128)(2,1)S(1)}, bf16[1,8,48,384]{3,2,1,0:T(8,128)(2,1)S(1)}, u32[]{:S(2)}, u32[]{:S(2)}) collective-permute-start(bf16[1,8,48,384]{3,2,1,0:T(8,128)(2,1)S(1)} %add_convert_fusion.1), channel_id=1, source_target_pairs={{0,2},{1,3},{2,0},{3,1},{4,6},{5,7},{6,4},{7,5},{8,10},{9,11},{10,... | collective-permute-start | bytes 884744 | tf_op jit(solution)/shard_map/ppermute | solution.py:363
  105.9 12.2 %collective-permute-start.22 = (bf16[1,4,48,384]{3,2,1,0:T(8,128)(2,1)S(1)}, bf16[1,4,48,384]{3,2,1,0:T(8,128)(2,1)S(1)}, u32[]{:S(2)}, u32[]{:S(2)}) collective-permute-start(bf16[1,4,48,384]{3,2,1,0:T(8,128)(2,1)S(1)} %add_convert_fusion.4), channel_id=1, source_target_pairs={{0,2},{1,3},{2,0},{3,1},{4,6},{5,7},{6,4},{7,5},{8,10},{9,11},{10,... | collective-permute-start | bytes 442376 | tf_op jit(solution)/shard_map/ppermute | solution.py:363
  110.2 15.9 %copy-start.1 = (s32[2]{0:T(128)S(1)}, s32[2]{0:T(128)}, u32[]{:S(2)}) copy-start(s32[2]{0:T(128)} %pad_add_fusion.2.place) | copy-start | bytes 28
  110.2 15.9 %copy-start.2 = (s32[2,32]{1,0:T(2,128)S(1)}, s32[2,32]{1,0:T(2,128)}, u32[]{:S(2)}) copy-start(s32[2,32]{1,0:T(2,128)} %pad_add_fusion.1.targets) | copy-start | bytes 772
  110.2 9.5 %collective-permute-start.9 = (bf16[4,48,384]{2,1,0:T(8,128)(2,1)S(1)}, bf16[4,48,384]{2,1,0:T(8,128)(2,1)S(1)}, u32[]{:S(2)}, u32[]{:S(2)}) collective-permute-start(bf16[4,48,384]{2,1,0:T(8,128)(2,1)S(1)} %fusion.1.refs_0_), channel_id=1, source_target_pairs={{0,4},{4,0},{8,12},{12,8},{16,20},{20,16},{24,28},{28,24},{1,5},{5... | collective-permute-start | bytes 442376 | tf_op jit(solution)/shard_map/ppermute | solution.py:429
  116.6 9.5 %collective-permute-start.16 = (bf16[8,48,384]{2,1,0:T(8,128)(2,1)S(1)}, bf16[8,48,384]{2,1,0:T(8,128)(2,1)S(1)}, u32[]{:S(2)}, u32[]{:S(2)}) collective-permute-start(bf16[8,48,384]{2,1,0:T(8,128)(2,1)S(1)} %fusion.refs_2_), channel_id=1, source_target_pairs={{0,4},{4,0},{8,12},{12,8},{16,20},{20,16},{24,28},{28,24},{1,5},{5... | collective-permute-start | bytes 884744 | tf_op jit(solution)/shard_map/ppermute | solution.py:429
  118.2 9.8 %collective-permute-start.23 = (bf16[4,48,384]{2,1,0:T(8,128)(2,1)S(1)}, bf16[4,48,384]{2,1,0:T(8,128)(2,1)S(1)}, u32[]{:S(2)}, u32[]{:S(2)}) collective-permute-start(bf16[4,48,384]{2,1,0:T(8,128)(2,1)S(1)} %fusion.2.mine), channel_id=1, source_target_pairs={{0,4},{4,0},{8,12},{12,8},{16,20},{20,16},{24,28},{28,24},{1,5},{5... | collective-permute-start | bytes 442376 | tf_op jit(solution)/shard_map/ppermute | solution.py:429
  129.6 5.2 %copy-start = (f32[2,4,48,384]{3,2,1,0:T(8,128)}, f32[2,4,48,384]{3,2,1,0:T(8,128)S(1)}, u32[]{:S(2)}) copy-start(f32[2,4,48,384]{3,2,1,0:T(8,128)S(1)} %get-tuple-element.32.keep_ref) | copy-start | bytes 1769476
  129.6 5.2 %collective-permute-start.25 = (bf16[1,4,48,384]{3,2,1,0:T(8,128)(2,1)S(1)}, bf16[1,4,48,384]{3,2,1,0:T(8,128)(2,1)S(1)}, u32[]{:S(2)}, u32[]{:S(2)}) collective-permute-start(bf16[1,4,48,384]{3,2,1,0:T(8,128)(2,1)S(1)} %get-tuple-element.34), channel_id=1, source_target_pairs={{0,8},{4,12},{8,0},{12,4},{16,24},{20,28},{24,16},{28,20},{1,9},{5... | collective-permute-start | bytes 442376 | tf_op jit(solution)/shard_map/ppermute | solution.py:360
  131.2 7.0 %collective-permute-start.24 = (bf16[1,4,48,384]{3,2,1,0:T(8,128)(2,1)S(1)}, bf16[1,4,48,384]{3,2,1,0:T(8,128)(2,1)S(1)}, u32[]{:S(2)}, u32[]{:S(2)}) collective-permute-start(bf16[1,4,48,384]{3,2,1,0:T(8,128)(2,1)S(1)} %get-tuple-element.33), channel_id=1, source_target_pairs={{0,8},{4,12},{8,0},{12,4},{16,24},{20,28},{24,16},{28,20},{1,9},{5... | collective-permute-start | bytes 442376 | tf_op jit(solution)/shard_map/ppermute | solution.py:361
  134.8 8.3 %collective-permute-start.26 = (bf16[1,4,48,384]{3,2,1,0:T(8,128)(2,1)S(1)}, bf16[1,4,48,384]{3,2,1,0:T(8,128)(2,1)}, u32[]{:S(2)}, u32[]{:S(2)}) collective-permute-start(bf16[1,4,48,384]{3,2,1,0:T(8,128)(2,1)S(1)} %add_convert_fusion.2), channel_id=1, source_target_pairs={{0,16},{4,20},{8,24},{12,28},{16,0},{20,4},{24,8},{28,12},{1,17},{... | collective-permute-start | bytes 442376 | tf_op jit(solution)/shard_map/ppermute | solution.py:363
  138.3 0.7 copy-start.6

commit v5 on v4

--- a/solution.py
+++ b/solution.py
@@ -13,15 +13,15 @@
 G_DEV = 8
 OMEGA = 0.6
 
-EDGES = (0, 4, 12, 16)
+EDGES = (0, 6, 10, 14, 16)
 STEP = 2
 
 
 VMEM = pl.BlockSpec(memory_space=pltpu.VMEM)
 SMEM = pl.BlockSpec(memory_space=pltpu.SMEM)
 ANY = pl.BlockSpec(memory_space=pl.ANY)
-SMALL = pltpu.CompilerParams(vmem_limit_bytes=50331648)
-PARAMS = pltpu.CompilerParams(vmem_limit_bytes=67043328)
+PARAMS = pltpu.CompilerParams(vmem_limit_bytes=25165824)
+ALONE = pltpu.CompilerParams(vmem_limit_bytes=67043328)
 
 
 def step_of(first, count):
@@ -61,16 +61,17 @@
         out_shape=[
             jax.ShapeDtypeStruct((count, high, per * width), tentative.dtype) for count in counts
         ],
-        compiler_params=PARAMS,
+        compiler_params=PARAMS if first else ALONE,
         cost_estimate=cost(0, 5 * sum(counts) * per * high * width),
     )(tentative)
 
 
 def prolong_kernel(first, table, labels, off, diag, inverse, own, near_a, near_b, out, *wides):
-    step = near_a.shape[0]
+    step = len(wides) // 2
     slots, size = off.shape[1], off.shape[2]
     window = CW * size
-    start = 2 * RQ * (first + pl.program_id(0) * step)
+    base = pl.program_id(0) * step
+    start = 2 * RQ * (first + base)
 
     @pl.when(pl.program_id(0) == 0)
     def _():
@@ -83,7 +84,9 @@
             local = RQ * c + k
             j = local % (2 * RQ)
             lanes = slice(j * size, (j + 1) * size)
-            for side, block in enumerate((near_a[m, :, lanes], own[local], near_b[m, :, lanes])):
+            for side, block in enumerate(
+                (near_a[base + m, :, lanes], own[local], near_b[base + m, :, lanes])
+            ):
                 label = labels[side, start + local]
                 for w in range(CW):
                     wide[side * RQ + k, :, w * size : (w + 1) * size] = jnp.where(
@@ -105,14 +108,14 @@
         for k in range(RQ):
             local = RQ * c + k
             change = jnp.dot(inverse[local], sums[local], preferred_element_type=jnp.float32)
-            out[c, :, k * window : (k + 1) * window] = (
+            out[2 * base + c, :, k * window : (k + 1) * window] = (
                 wide[RQ + k].astype(jnp.float32) - OMEGA * change
             ).astype(out.dtype)
 
 
 def prolong_rows(table, labels, off, diag, inverse, tentative, near_a, near_b, first):
     per = 2 * RQ
-    count, high, _ = near_a.shape
+    count = near_a.shape[0]
     slots, size = off.shape[1], off.shape[2]
     window = CW * size
     step = step_of(first, count)
@@ -121,7 +124,6 @@
         return (i + first // step, 0, 0)
 
     square = pl.BlockSpec((per * step, size, size), rows)
-    packed = pl.BlockSpec((step, high, per * size), lambda i: (i, 0, 0))
     return pl.pallas_call(
         functools.partial(prolong_kernel, first),
         grid=(count // step,),
@@ -132,10 +134,10 @@
             square,
             square,
             square,
-            packed,
-            packed,
-        ],
-        out_specs=pl.BlockSpec((2 * step, size, RQ * window), lambda i: (i, 0, 0)),
+            VMEM,
+            VMEM,
+        ],
+        out_specs=VMEM,
         out_shape=jax.ShapeDtypeStruct((2 * count, size, RQ * window), tentative.dtype),
         scratch_shapes=[pltpu.VMEM((3 * RQ + 1, size, window), tentative.dtype)] * (2 * step),
         compiler_params=PARAMS,
@@ -147,12 +149,13 @@
 
 
 def coarse_kernel(first, table, place, off, diag, own, near_a, near_b, keep, send, *scratch):
-    step = keep.shape[1]
+    step = len(scratch) // 6
     slots, size = off.shape[1], off.shape[2]
     window = CW * size
     halves, high = keep.shape[0], keep.shape[2]
     col = place[0]
-    start = 2 * RQ * (first + pl.program_id(0) * step)
+    base = pl.program_id(0) * step
+    start = 2 * RQ * (first + base)
     fields, stiffs, wholes = (scratch[2 * step * i : 2 * step * (i + 1)] for i in range(3))
 
     @pl.when(pl.program_id(0) == 0)
@@ -164,7 +167,7 @@
         for k in range(RQ):
             lanes = slice(k * window, (k + 1) * window)
             for side, source in enumerate((near_a, own, near_b)):
-                field[side * RQ + k] = source[c, :, lanes]
+                field[side * RQ + k] = source[2 * base + c, :, lanes]
     for c, (field, stiff) in enumerate(zip(fields, stiffs)):
         for k in range(RQ):
             local = RQ * c + k
@@ -186,8 +189,8 @@
     for c, whole in enumerate(wholes):
         lanes = slice(c % 2 * window, (c % 2 + 1) * window)
         for h in range(halves):
-            keep[h, c // 2, :, lanes] = whole[col ^ (2 * h)]
-            send[h, c // 2, :, lanes] = whole[col ^ (2 * h + 1)].astype(send.dtype)
+            keep[h, base + c // 2, :, lanes] = whole[col ^ (2 * h)]
+            send[h, base + c // 2, :, lanes] = whole[col ^ (2 * h + 1)].astype(send.dtype)
 
 
 def coarse_rows(table, place, off, diag, own, near_a, near_b, first, columns):
@@ -201,8 +204,6 @@
     def rows(i):
         return (i + first // step, 0, 0)
 
-    packed = pl.BlockSpec((2 * step, size, RQ * window), lambda i: (i, 0, 0))
-    result = pl.BlockSpec((halves, step, high, 2 * window), lambda i: (0, i, 0, 0))
     shape = (halves, count, high, 2 * window)
     return pl.pallas_call(
         functools.partial(coarse_kernel, first),
@@ -212,11 +213,11 @@
             SMEM,
             pl.BlockSpec((per * step, slots, size, size), lambda i: rows(i) + (0,)),
             pl.BlockSpec((per * step, size, size), rows),
-            packed,
-            packed,
-            packed,
-        ],
-        out_specs=[result, result],
+            VMEM,
+            VMEM,
+            VMEM,
+        ],
+        out_specs=[VMEM, VMEM],
         out_shape=[
             jax.ShapeDtypeStruct(shape, jnp.float32),
             jax.ShapeDtypeStruct(shape, own.dtype),
@@ -282,7 +283,7 @@
         out_shape=jax.ShapeDtypeStruct(shape, jnp.float32),
         scratch_shapes=[pltpu.VMEM(array.shape, array.dtype) for array in flat]
         + [pltpu.SemaphoreType.DMA((len(flat),))],
-        compiler_params=SMALL,
+        compiler_params=PARAMS,
         cost_estimate=cost(total, 4 * total),
     )(targets, place, *flat)
 
@@ -318,7 +319,7 @@
             pltpu.VMEM(theirs.shape, theirs.dtype),
             pltpu.SemaphoreType.DMA((3,)),
         ],
-        compiler_params=SMALL,
+        compiler_params=PARAMS,
         cost_estimate=cost(early.size, 10 * early.size),
     )(targets, place, early, mine, theirs)
 
@@ -336,12 +337,10 @@
 
 def finish(keep, *others):
     _, pairs, high, lanes = keep.shape
-    block = pl.BlockSpec((1, pairs, high, lanes), lambda i: (0, 0, 0, 0))
     return pl.pallas_call(
         finish_kernel,
-        grid=(1,),
-        in_specs=[block] * (1 + len(others)),
-        out_specs=pl.BlockSpec((2 * pairs, high, lanes // 2), lambda i: (0, 0, 0)),
+        in_specs=[VMEM] * (1 + len(others)),
+        out_specs=VMEM,
         out_shape=jax.ShapeDtypeStruct((2 * pairs, high, lanes // 2), jnp.float32),
         compiler_params=PARAMS,
         cost_estimate=cost(pairs * high * lanes, 10 * pairs * high * lanes),

time: 146 us -> 139 us (0.952)
  Pallas kernels: 42.3 us -> 31.5 us
  local copies, waits for them, and re-layouts: 0.68 us -> 10.5 us
  starting transfers between devices: 25.3 us -> 30.9 us
  other arithmetic: 8.92 us -> 3.49 us
  waiting for transfers between devices: 67.7 us -> 62.4 us
    unnamed x14 -> x36, local copies, waits for them, and re-layouts: 0.68 us -> 10.5 us
    pallas_call x3 -> x4, Pallas kernels: 16.5 us -> 11.5 us  [coarse_rows(): pl.pallas_call(functools.partial(coarse_kernel, first), grid=(count // st...]
    pallas_call x3 -> x4, Pallas kernels: 15.8 us -> 11.8 us  [prolong_rows(): pl.pallas_call(functools.partial(prolong_kernel, first), grid=(count // s...]
    ppermute x7 -> x9, waiting for transfers between devices: 47.7 us -> 44.3 us  [both(): near_b = lax.ppermute(block, 'col', pair_b)]
    convert_element_type x4 -> x5, other arithmetic: 2.45 us -> 0.16 us  [exchange(): send = (leave + odd.astype(jnp.float32)).astype(link)]
    ppermute x3 -> x4, starting transfers between devices: 4.64 us -> 6.62 us  [on_device(): other = lax.ppermute(total, 'row', flip(rows, 1))]
    ppermute x7 -> x9, starting transfers between devices: 2.29 us -> 4.21 us  [both(): near_a = lax.ppermute(block, 'col', pair_a)]
    convert_element_type x3 -> x4, other arithmetic: 2.07 us -> 0.22 us  [on_device(): total = sum((term[0].astype(jnp.float32) for term in terms)).astype(link)]
  transfers between devices with their start and end apart: 27 -> 34, of which waited for: 11 -> 9; matrix products, arithmetic and copies ran while one was open for 6% -> 3% of each run, Pallas kernels for 22% -> 21%
where the time goes in v5:
time: 139 us
  waiting for transfers between devices  62.4 us (45%)
  Pallas kernels  31.5 us (23%)
  starting transfers between devices  30.9 us (22%)
  local copies, waits for them, and re-layouts  10.5 us (8%)
  other arithmetic  3.49 us (3%)
    ppermute x9, waiting for transfers between devices, both(): near_b = lax.ppermute(block, 'col', pair_b)  44.3 us
    pallas_call x4, Pallas kernels, prolong_rows(): pl.pallas_call(functools.partial(prolong_kernel, first), grid=(count // s...  11.8 us
    pallas_call x4, Pallas kernels, coarse_rows(): pl.pallas_call(functools.partial(coarse_kernel, first), grid=(count // st...  11.5 us
    unnamed x36, local copies, waits for them, and re-layouts  10.5 us
    ppermute x9, waiting for transfers between devices, exchange(): arrived = (lax.ppermute(send, axis, route), 2)  9.25 us
    ppermute x9, starting transfers between devices, exchange(): arrived = (lax.ppermute(send, axis, route), 2)  9.24 us
    ppermute x4, starting transfers between devices, on_device(): other = lax.ppermute(total, 'row', flip(rows, 1))  6.62 us
    ppermute x9, starting transfers between devices, both(): near_b = lax.ppermute(block, 'col', pair_b)  6.61 us
  transfers between devices with their start and end apart: 34, of which 9 were waited for; matrix products, arithmetic and copies ran while one was open for 3% of the time, Pallas kernels for 21%

profile of v5, /device:TPU:0, one launch (start us, length us, event | category | flops | bytes accessed | tf_op | source)
XLA Modules:
  0.0 139.1 jit_solution(7718771270012108732)
XLA Ops:
  0.0 2.4 %collective-permute-start.1 = (s32[64]{0:T(128)}, s32[64]{0:T(128)}, u32[]{:S(2)}, u32[]{:S(2)}) collective-permute-start(s32[64]{0:T(128)} %param.15), channel_id=1, source_target_pairs={{0,3},{1,2},{2,1},{3,0},{4,7},{5,6},{6,5},{7,4},{8,11},{9,10},{10,... | collective-permute-start | bytes 776 | tf_op jit(solution)/shard_map/ppermute | solution.py:397
  2.4 0.7 collective-permute-start
  3.1 1.4 %copy-done.3 = bf16[64,96,96]{2,1,0:T(8,128)(2,1)S(1)} copy-done((bf16[64,96,96]{2,1,0:T(8,128)(2,1)S(1)}, bf16[64,96,96]{2,1,0:T(8,128)(2,1)}, u32[]{:S(2)}) %copy-start.3) | copy-done | bytes 1179672
  4.5 1.1 shard_map.94
  5.6 0.7 copy-done.8
  6.3 0.6 copy-done.10
  7.5 2.1 %collective-permute-start.2 = (s32[32]{0:T(128)}, s32[32]{0:T(128)}, u32[]{:S(2)}, u32[]{:S(2)}) collective-permute-start(s32[32]{0:T(128)} %bitcast_add_fusion), channel_id=1, source_target_pairs={{0,4},{4,0},{8,12},{12,8},{16,20},{20,16},{24,28},{28,24},{1,5},{5... | collective-permute-start | bytes 392 | tf_op jit(solution)/shard_map/ppermute | solution.py:407
  10.2 0.7 pad_add_fusion.2.place
  10.9 2.1 %shard_map.91 = bf16[6,96,384]{2,1,0:T(8,128)(2,1)} custom-call(bf16[64,96,96]{2,1,0:T(8,128)(2,1)} %own.7), custom_call_target="tpu_custom_call" | custom-call | bytes 1105920 | tf_op jit(solution)/shard_map/pallas_call | solution.py:54
  13.0 1.6 %collective-permute-start.4 = (bf16[6,96,384]{2,1,0:T(8,128)(2,1)}, bf16[6,96,384]{2,1,0:T(8,128)(2,1)S(1)}, u32[]{:S(2)}, u32[]{:S(2)}) collective-permute-start(bf16[6,96,384]{2,1,0:T(8,128)(2,1)} %shard_map.91), channel_id=1, source_target_pairs={{0,3},{1,2},{2,1},{3,0},{4,7},{5,6},{6,5},{7,4},{8,11},{9,10},{10,... | collective-permute-start | bytes 1327112 | tf_op jit(solution)/shard_map/ppermute | solution.py:397
  14.7 0.6 pad_add_fusion.1.targets
  15.4 0.7 pad_add_fusion.labels
  16.6 2.8 %copy-done = bf16[64,4,96,96]{3,2,1,0:T(8,128)(2,1)S(1)} copy-done((bf16[64,4,96,96]{3,2,1,0:T(8,128)(2,1)S(1)}, bf16[64,4,96,96]{3,2,1,0:T(8,128)(2,1)}, u32[]{:S(2)}) %copy-start) | copy-done | bytes 4718616
  19.4 1.4 %copy-done.1 = bf16[64,96,96]{2,1,0:T(8,128)(2,1)S(1)} copy-done((bf16[64,96,96]{2,1,0:T(8,128)(2,1)S(1)}, bf16[64,96,96]{2,1,0:T(8,128)(2,1)}, u32[]{:S(2)}) %copy-start.1) | copy-done | bytes 1179672
  20.8 1.4 %copy-done.4 = bf16[64,96,96]{2,1,0:T(8,128)(2,1)S(1)} copy-done((bf16[64,96,96]{2,1,0:T(8,128)(2,1)S(1)}, bf16[64,96,96]{2,1,0:T(8,128)(2,1)}, u32[]{:S(2)}) %copy-start.4) | copy-done | bytes 1179672
  22.2 1.4 %copy-done.5 = bf16[64,96,96]{2,1,0:T(8,128)(2,1)S(1)} copy-done((bf16[64,96,96]{2,1,0:T(8,128)(2,1)S(1)}, bf16[64,96,96]{2,1,0:T(8,128)(2,1)}, u32[]{:S(2)}) %copy-start.5) | copy-done | bytes 1179672
  23.6 0.7 copy-done.6
  24.3 3.3 %shard_map.95.own = bf16[8,96,384]{2,1,0:T(8,128)(2,1)S(1)} custom-call(s32[4,64]{1,0:T(4,128)S(1)} %copy-done.6, s32[3,64]{1,0:T(4,128)S(1)} %pad_add_fusion.labels, bf16[64,4,96,96]{3,2,1,0:T(8,128)(2,1)S(1)} %copy-done, bf16[64,96,96]{2,1,0:T(8,128)(2,1)S(1)} %copy-done.1, bf16[64,96,96]{2,1,0:T(8,128)(2,1)S(1)} %copy-done.5, ...), custom_call_target="tpu_custom_call" | custom-call | flops 339738624 | bytes 3244032 | tf_op jit(solution)/shard_map/pallas_call | solution.py:127
  28.4 5.2 %collective-permute-done.25.near_b = bf16[2,96,384]{2,1,0:T(8,128)(2,1)S(1)} collective-permute-done((bf16[2,96,384]{2,1,0:T(8,128)(2,1)S(1)}, bf16[2,96,384]{2,1,0:T(8,128)(2,1)S(1)}, u32[]{:S(2)}, u32[]{:S(2)}) %collective-permute-start.25) | collective-permute-done | bytes 147488 | tf_op jit(solution)/shard_map/ppermute | solution.py:397
  33.9 1.7 %shard_map.100.own = bf16[4,96,384]{2,1,0:T(8,128)(2,1)S(1)} custom-call(s32[4,64]{1,0:T(4,128)S(1)} %copy-done.6, s32[3,64]{1,0:T(4,128)S(1)} %pad_add_fusion.labels, bf16[64,4,96,96]{3,2,1,0:T(8,128)(2,1)S(1)} %copy-done, bf16[64,96,96]{2,1,0:T(8,128)(2,1)S(1)} %copy-done.1, bf16[64,96,96]{2,1,0:T(8,128)(2,1)S(1)} %copy-done.5, ...), custom_call_target="tpu_custom_call" | custom-call | flops 169869312 | bytes 1622016 | tf_op jit(solution)/shard_map/pallas_call | solution.py:127
  35.6 1.4 %collective-permute-start.18 = (bf16[4,96,384]{2,1,0:T(8,128)(2,1)S(1)}, bf16[4,96,384]{2,1,0:T(8,128)(2,1)S(1)}, u32[]{:S(2)}, u32[]{:S(2)}) collective-permute-start(bf16[4,96,384]{2,1,0:T(8,128)(2,1)S(1)} %copy-done.9), channel_id=1, source_target_pairs={{0,3},{1,2},{2,1},{3,0},{4,7},{5,6},{6,5},{7,4},{8,11},{9,10},{10,... | collective-permute-start | bytes 884744 | tf_op jit(solution)/shard_map/ppermute | solution.py:397
  37.6 3.9 %shard_map.92.own = bf16[12,96,384]{2,1,0:T(8,128)(2,1)S(1)} custom-call(s32[4,64]{1,0:T(4,128)S(1)} %copy-done.6, s32[3,64]{1,0:T(4,128)S(1)} %pad_add_fusion.labels, bf16[64,4,96,96]{3,2,1,0:T(8,128)(2,1)S(1)} %copy-done, bf16[64,96,96]{2,1,0:T(8,128)(2,1)S(1)} %copy-done.1, bf16[64,96,96]{2,1,0:T(8,128)(2,1)S(1)} %copy-done.5, ...), custom_call_target="tpu_custom_call" | custom-call | flops 509607936 | bytes 4866048 | tf_op jit(solution)/shard_map/pallas_call | solution.py:127
  41.5 13.4 %collective-permute-done.18.near_b = bf16[4,96,384]{2,1,0:T(8,128)(2,1)S(1)} collective-permute-done((bf16[4,96,384]{2,1,0:T(8,128)(2,1)S(1)}, bf16[4,96,384]{2,1,0:T(8,128)(2,1)S(1)}, u32[]{:S(2)}, u32[]{:S(2)}) %collective-permute-start.18) | collective-permute-done | bytes 294944 | tf_op jit(solution)/shard_map/ppermute | solution.py:397
  55.0 1.2 collective-permute-start.5
  56.2 2.8 %shard_map.97.own = bf16[8,96,384]{2,1,0:T(8,128)(2,1)S(1)} custom-call(s32[4,64]{1,0:T(4,128)S(1)} %copy-done.6, s32[3,64]{1,0:T(4,128)S(1)} %pad_add_fusion.labels, bf16[64,4,96,96]{3,2,1,0:T(8,128)(2,1)S(1)} %copy-done, bf16[64,96,96]{2,1,0:T(8,128)(2,1)S(1)} %copy-done.1, bf16[64,96,96]{2,1,0:T(8,128)(2,1)S(1)} %copy-done.5, ...), custom_call_target="tpu_custom_call" | custom-call | flops 339738624 | bytes 3244032 | tf_op jit(solution)/shard_map/pallas_call | solution.py:127
  59.0 2.3 %collective-permute-done.27.near_b = bf16[4,96,384]{2,1,0:T(8,128)(2,1)S(1)} collective-permute-done((bf16[4,96,384]{2,1,0:T(8,128)(2,1)S(1)}, bf16[4,96,384]{2,1,0:T(8,128)(2,1)S(1)}, u32[]{:S(2)}, u32[]{:S(2)}) %collective-permute-start.27) | collective-permute-done | bytes 294944 | tf_op jit(solution)/shard_map/ppermute | solution.py:397
  61.3 1.2 collective-permute-start.19
  62.5 1.7 %shard_map.101 = (f32[2,2,48,384]{3,2,1,0:T(8,128)S(1)}, bf16[2,2,48,384]{3,2,1,0:T(8,128)(2,1)S(1)}) custom-call(s32[4,64]{1,0:T(4,128)S(1)} %copy-done.6, s32[2]{0:T(128)S(1)} %copy-done.7, bf16[64,4,96,96]{3,2,1,0:T(8,128)(2,1)S(1)} %bitcast.20, bf16[64,96,96]{2,1,0:T(8,128)(2,1)S(1)} %copy-done.2, bf16[4,96,384]{2,1,0:T(8,128)(2,1)S(1)} %shard_map.100.own, ...), custom_call_target="tpu_custom_call" | custom-call | flops 198180864 | bytes 2359296 | tf_op jit(solution)/shard_map/pallas_call | solution.py:208
  64.8 2.9 %shard_map.96 = (f32[2,4,48,384]{3,2,1,0:T(8,128)S(1)}, bf16[2,4,48,384]{3,2,1,0:T(8,128)(2,1)S(1)}) custom-call(s32[4,64]{1,0:T(4,128)S(1)} %copy-done.6, s32[2]{0:T(128)S(1)} %copy-done.7, bf16[64,4,96,96]{3,2,1,0:T(8,128)(2,1)S(1)} %bitcast.20, bf16[64,96,96]{2,1,0:T(8,128)(2,1)S(1)} %copy-done.2, bf16[8,96,384]{2,1,0:T(8,128)(2,1)S(1)} %shard_map.95.own, ...), custom_call_target="tpu_custom_call" | custom-call | flops 396361728 | bytes 4718592 | tf_op jit(solution)/shard_map/pallas_call | solution.py:208
  67.8 1.6 %collective-permute-start.29 = (bf16[1,2,48,384]{3,2,1,0:T(8,128)(2,1)S(1)}, bf16[1,2,48,384]{3,2,1,0:T(8,128)(2,1)S(1)}, u32[]{:S(2)}, u32[]{:S(2)}) collective-permute-start(bf16[1,2,48,384]{3,2,1,0:T(8,128)(2,1)S(1)} %add_convert_fusion.8), channel_id=1, source_target_pairs={{0,2},{1,3},{2,0},{3,1},{4,6},{5,7},{6,4},{7,5},{8,10},{9,11},{10,... | collective-permute-start | bytes 221192 | tf_op jit(solution)/shard_map/ppermute | solution.py:362
  69.5 23.4 %collective-permute-done.20.near_b = bf16[8,96,384]{2,1,0:T(8,128)(2,1)S(1)} collective-permute-done((bf16[8,96,384]{2,1,0:T(8,128)(2,1)S(1)}, bf16[8,96,384]{2,1,0:T(8,128)(2,1)S(1)}, u32[]{:S(2)}, u32[]{:S(2)}) %collective-permute-start.20) | collective-permute-done | bytes 589856 | tf_op jit(solution)/shard_map/ppermute | solution.py:397
  92.9 2.9 %shard_map.98 = (f32[2,4,48,384]{3,2,1,0:T(8,128)S(1)}, bf16[2,4,48,384]{3,2,1,0:T(8,128)(2,1)S(1)}) custom-call(s32[4,64]{1,0:T(4,128)S(1)} %copy-done.6, s32[2]{0:T(128)S(1)} %copy-done.7, bf16[64,4,96,96]{3,2,1,0:T(8,128)(2,1)S(1)} %bitcast.20, bf16[64,96,96]{2,1,0:T(8,128)(2,1)S(1)} %copy-done.2, bf16[8,96,384]{2,1,0:T(8,128)(2,1)S(1)} %shard_map.97.own, ...), custom_call_target="tpu_custom_call" | custom-call | flops 396361728 | bytes 4718592 | tf_op jit(solution)/shard_map/pallas_call | solution.py:208
  95.8 0.9 collective-permute-start.21
  97.3 4.0 %shard_map.93 = (f32[2,6,48,384]{3,2,1,0:T(8,128)S(1)}, bf16[2,6,48,384]{3,2,1,0:T(8,128)(2,1)S(1)}) custom-call(s32[4,64]{1,0:T(4,128)S(1)} %copy-done.6, s32[2]{0:T(128)S(1)} %copy-done.7, bf16[64,4,96,96]{3,2,1,0:T(8,128)(2,1)S(1)} %bitcast.20, bf16[64,96,96]{2,1,0:T(8,128)(2,1)S(1)} %copy-done.2, bf16[12,96,384]{2,1,0:T(8,128)(2,1)S(1)} %shard_map.92.own, ...), custom_call_target="tpu_custom_call" | custom-call | flops 594542592 | bytes 7077888 | tf_op jit(solution)/shard_map/pallas_call | solution.py:208
  101.4 1.6 %collective-permute-start.22 = (bf16[1,4,48,384]{3,2,1,0:T(8,128)(2,1)S(1)}, bf16[1,4,48,384]{3,2,1,0:T(8,128)(2,1)S(1)}, u32[]{:S(2)}, u32[]{:S(2)}) collective-permute-start(bf16[1,4,48,384]{3,2,1,0:T(8,128)(2,1)S(1)} %add_convert_fusion.4), channel_id=1, source_target_pairs={{0,2},{1,3},{2,0},{3,1},{4,6},{5,7},{6,4},{7,5},{8,10},{9,11},{10,... | collective-permute-start | bytes 442376 | tf_op jit(solution)/shard_map/ppermute | solution.py:362
  103.2 2.1 %collective-permute-start.16 = (bf16[4,48,384]{2,1,0:T(8,128)(2,1)S(1)}, bf16[4,48,384]{2,1,0:T(8,128)(2,1)S(1)}, u32[]{:S(2)}, u32[]{:S(2)}) collective-permute-start(bf16[4,48,384]{2,1,0:T(8,128)(2,1)S(1)} %fusion.1.refs_2_), channel_id=1, source_target_pairs={{0,4},{4,0},{8,12},{12,8},{16,20},{20,16},{24,28},{28,24},{1,5},{5... | collective-permute-start | bytes 442376 | tf_op jit(solution)/shard_map/ppermute | solution.py:428
  105.6 2.1 %collective-permute-done.22 = bf16[1,4,48,384]{3,2,1,0:T(8,128)(2,1)S(1)} collective-permute-done((bf16[1,4,48,384]{3,2,1,0:T(8,128)(2,1)S(1)}, bf16[1,4,48,384]{3,2,1,0:T(8,128)(2,1)S(1)}, u32[]{:S(2)}, u32[]{:S(2)}) %collective-permute-start.22) | collective-permute-done | bytes 147488 | tf_op jit(solution)/shard_map/ppermute | solution.py:362
  107.8 2.4 %collective-permute-start.23 = (bf16[4,48,384]{2,1,0:T(8,128)(2,1)S(1)}, bf16[4,48,384]{2,1,0:T(8,128)(2,1)S(1)}, u32[]{:S(2)}, u32[]{:S(2)}) collective-permute-start(bf16[4,48,384]{2,1,0:T(8,128)(2,1)S(1)} %fusion.2.refs_4_), channel_id=1, source_target_pairs={{0,4},{4,0},{8,12},{12,8},{16,20},{20,16},{24,28},{28,24},{1,5},{5... | collective-permute-start | bytes 442376 | tf_op jit(solution)/shard_map/ppermute | solution.py:428
  110.2 2.4 %collective-permute-done.8 = bf16[1,6,48,384]{3,2,1,0:T(8,128)(2,1)S(1)} collective-permute-done((bf16[1,6,48,384]{3,2,1,0:T(8,128)(2,1)S(1)}, bf16[1,6,48,384]{3,2,1,0:T(8,128)(2,1)S(1)}, u32[]{:S(2)}, u32[]{:S(2)}) %collective-permute-start.8) | collective-permute-done | bytes 221216 | tf_op jit(solution)/shard_map/ppermute | solution.py:362
  112.7 1.8 %collective-permute-start.9 = (bf16[6,48,384]{2,1,0:T(8,128)(2,1)S(1)}, bf16[6,48,384]{2,1,0:T(8,128)(2,1)S(1)}, u32[]{:S(2)}, u32[]{:S(2)}) collective-permute-start(bf16[6,48,384]{2,1,0:T(8,128)(2,1)S(1)} %fusion.refs_0_), channel_id=1, source_target_pairs={{0,4},{4,0},{8,12},{12,8},{16,20},{20,16},{24,28},{28,24},{1,5},{5... | collective-permute-start | bytes 663560 | tf_op jit(solution)/shard_map/ppermute | solution.py:428
  114.9 5.6 %collective-permute-done.9.refs_1_ = bf16[6,48,384]{2,1,0:T(8,128)(2,1)S(1)} collective-permute-done((bf16[6,48,384]{2,1,0:T(8,128)(2,1)S(1)}, bf16[6,48,384]{2,1,0:T(8,128)(2,1)S(1)}, u32[]{:S(2)}, u32[]{:S(2)}) %collective-permute-start.9) | collective-permute-done | bytes 221216 | tf_op jit(solution)/shard_map/ppermute | solution.py:428
  120.5 2.8 %shard_map.99.early = f32[33,48,192]{2,1,0:T(8,128)S(1)} custom-call(s32[2,32]{1,0:T(2,128)S(1)} %pad_add_fusion.1.targets, s32[2]{0:T(128)S(1)} %copy-done.7, bf16[6,48,384]{2,1,0:T(8,128)(2,1)S(1)} %fusion.refs_0_, bf16[6,48,384]{2,1,0:T(8,128)(2,1)S(1)} %collective-permute-done.9.refs_1_, bf16[4,48,384]{2,1,0:T(8,128)(2,1)S(1)} %fusion.1.refs_2_, ...), custom_call_target="tpu_custom_call" | custom-call | flops 516096 | bytes 2064384 | tf_op jit(solution)/shard_map/pallas_call | solution.py:279
  123.3 1.3 shard_map.102
  124.7 1.6 %collective-permute-start.32 = (bf16[1,4,48,384]{3,2,1,0:T(8,128)(2,1)S(1)}, bf16[1,4,48,384]{3,2,1,0:T(8,128)(2,1)S(1)}, u32[]{:S(2)}, u32[]{:S(2)}) collective-permute-start(bf16[1,4,48,384]{3,2,1,0:T(8,128)(2,1)S(1)} %get-tuple-element.40), channel_id=1, source_target_pairs={{0,8},{4,12},{8,0},{12,4},{16,24},{20,28},{24,16},{28,20},{1,9},{5... | collective-permute-start | bytes 442376 | tf_op jit(solution)/shard_map/ppermute | solution.py:359
  126.8 3.3 %collective-permute-done.32 = bf16[1,4,48,384]{3,2,1,0:T(8,128)(2,1)S(1)} collective-permute-done((bf16[1,4,48,384]{3,2,1,0:T(8,128)(2,1)S(1)}, bf16[1,4,48,384]{3,2,1,0:T(8,128)(2,1)S(1)}, u32[]{:S(2)}, u32[]{:S(2)}) %collective-permute-start.32) | collective-permute-done | bytes 147488 | tf_op jit(solution)/shard_map/ppermute | solution.py:359
  130.1 3.4 %collective-permute-start.33 = (bf16[1,4,48,384]{3,2,1,0:T(8,128)(2,1)S(1)}, bf16[1,4,48,384]{3,2,1,0:T(8,128)(2,1)S(1)}, u32[]{:S(2)}, u32[]{:S(2)}) collective-permute-start(bf16[1,4,48,384]{3,2,1,0:T(8,128)(2,1)S(1)} %add_convert_fusion.2), channel_id=1, source_target_pairs={{0,16},{4,20},{8,24},{12,28},{16,0},{20,4},{24,8},{28,12},{1,17},{... | collective-permute-start | bytes 442376 | tf_op jit(solution)/shard_map/ppermute | solution.py:362
  133.5 4.7 %collective-permute-done.33.refs_1_ = bf16[1,4,48,384]{3,2,1,0:T(8,128)(2,1)S(1)} collective-permute-done((bf16[1,4,48,384]{3,2,1,0:T(8,128)(2,1)S(1)}, bf16[1,4,48,384]{3,2,1,0:T(8,128)(2,1)S(1)}, u32[]{:S(2)}, u32[]{:S(2)}) %collective-permute-start.33) | collective-permute-done | bytes 147488 | tf_op jit(solution)/shard_map/ppermute | solution.py:362
  138.2 0.9 shard_map.103
  (84 shorter events, 6.4 us)
Async XLA Ops:
  0.0 13.0 %collective-permute-start.1 = (s32[64]{0:T(128)}, s32[64]{0:T(128)}, u32[]{:S(2)}, u32[]{:S(2)}) collective-permute-start(s32[64]{0:T(128)} %param.15), channel_id=1, source_target_pairs={{0,3},{1,2},{2,1},{3,0},{4,7},{5,6},{6,5},{7,4},{8,11},{9,10},{10,... | collective-permute-start | bytes 776 | tf_op jit(solution)/shard_map/ppermute | solution.py:397
  2.4 12.9 %collective-permute-start = (s32[64]{0:T(128)}, s32[64]{0:T(128)}, u32[]{:S(2)}, u32[]{:S(2)}) collective-permute-start(s32[64]{0:T(128)} %param.15), channel_id=1, source_target_pairs={{0,1},{1,0},{2,3},{3,2},{4,5},{5,4},{6,7},{7,6},{8,9},{9,8},{10,11... | collective-permute-start | bytes 776 | tf_op jit(solution)/shard_map/ppermute | solution.py:398
  3.1 1.4 %copy-start.3 = (bf16[64,96,96]{2,1,0:T(8,128)(2,1)S(1)}, bf16[64,96,96]{2,1,0:T(8,128)(2,1)}, u32[]{:S(2)}) copy-start(bf16[64,96,96]{2,1,0:T(8,128)(2,1)} %own.7) | copy-start | bytes 3538948
  4.5 2.5 %copy-start.14 = (s32[32]{0:T(128)S(1)}, s32[32]{0:T(128)}, u32[]{:S(2)}) copy-start(s32[32]{0:T(128)} %param.17) | copy-start | bytes 388
  4.5 2.5 %copy-start.15 = (s32[32,1]{0,1:T(1,128)S(1)}, s32[32,1]{0,1:T(1,128)}, u32[]{:S(2)}) copy-start(s32[32,1]{0,1:T(1,128)} %param.16) | copy-start | bytes 388
  4.5 5.1 %copy-start.12 = (s32[64,4]{0,1:T(4,128)S(1)}, s32[64,4]{0,1:T(4,128)}, u32[]{:S(2)}) copy-start(s32[64,4]{0,1:T(4,128)} %param.10) | copy-start | bytes 3076
  4.5 5.1 %copy-start.13 = (s32[64,4]{0,1:T(4,128)S(1)}, s32[64,4]{0,1:T(4,128)}, u32[]{:S(2)}) copy-start(s32[64,4]{0,1:T(4,128)} %param.11) | copy-start | bytes 3076
  7.0 9.2 %collective-permute-start.10 = (bf16[4,96,384]{2,1,0:T(8,128)(2,1)}, bf16[4,96,384]{2,1,0:T(8,128)(2,1)}, u32[]{:S(2)}, u32[]{:S(2)}) collective-permute-start(bf16[4,96,384]{2,1,0:T(8,128)(2,1)} %get-tuple-element.29), channel_id=1, source_target_pairs={{0,1},{1,0},{2,3},{3,2},{4,5},{5,4},{6,7},{7,6},{8,9},{9,8},{10,11... | collective-permute-start | bytes 884744 | tf_op jit(solution)/shard_map/ppermute | solution.py:398
  7.0 9.7 %collective-permute-start.11 = (bf16[4,96,384]{2,1,0:T(8,128)(2,1)}, bf16[4,96,384]{2,1,0:T(8,128)(2,1)}, u32[]{:S(2)}, u32[]{:S(2)}) collective-permute-start(bf16[4,96,384]{2,1,0:T(8,128)(2,1)} %get-tuple-element.29), channel_id=1, source_target_pairs={{0,3},{1,2},{2,1},{3,0},{4,7},{5,6},{6,5},{7,4},{8,11},{9,10},{10,... | collective-permute-start | bytes 884744 | tf_op jit(solution)/shard_map/ppermute | solution.py:397
  7.5 5.5 %collective-permute-start.2 = (s32[32]{0:T(128)}, s32[32]{0:T(128)}, u32[]{:S(2)}, u32[]{:S(2)}) collective-permute-start(s32[32]{0:T(128)} %bitcast_add_fusion), channel_id=1, source_target_pairs={{0,4},{4,0},{8,12},{12,8},{16,20},{20,16},{24,28},{28,24},{1,5},{5... | collective-permute-start | bytes 392 | tf_op jit(solution)/shard_map/ppermute | solution.py:407
  13.0 24.0 %collective-permute-start.3 = (bf16[6,96,384]{2,1,0:T(8,128)(2,1)}, bf16[6,96,384]{2,1,0:T(8,128)(2,1)S(1)}, u32[]{:S(2)}, u32[]{:S(2)}) collective-permute-start(bf16[6,96,384]{2,1,0:T(8,128)(2,1)} %shard_map.91), channel_id=1, source_target_pairs={{0,1},{1,0},{2,3},{3,2},{4,5},{5,4},{6,7},{7,6},{8,9},{9,8},{10,11... | collective-permute-start | bytes 1327112 | tf_op jit(solution)/shard_map/ppermute | solution.py:398
  13.0 24.4 %collective-permute-start.4 = (bf16[6,96,384]{2,1,0:T(8,128)(2,1)}, bf16[6,96,384]{2,1,0:T(8,128)(2,1)S(1)}, u32[]{:S(2)}, u32[]{:S(2)}) collective-permute-start(bf16[6,96,384]{2,1,0:T(8,128)(2,1)} %shard_map.91), channel_id=1, source_target_pairs={{0,3},{1,2},{2,1},{3,0},{4,7},{5,6},{6,5},{7,4},{8,11},{9,10},{10,... | collective-permute-start | bytes 1327112 | tf_op jit(solution)/shard_map/ppermute | solution.py:397
  15.3 12.6 %collective-permute-start.24 = (bf16[2,96,384]{2,1,0:T(8,128)(2,1)}, bf16[2,96,384]{2,1,0:T(8,128)(2,1)S(1)}, u32[]{:S(2)}, u32[]{:S(2)}) collective-permute-start(bf16[2,96,384]{2,1,0:T(8,128)(2,1)} %copy-done.10), channel_id=1, source_target_pairs={{0,1},{1,0},{2,3},{3,2},{4,5},{5,4},{6,7},{7,6},{8,9},{9,8},{10,11... | collective-permute-start | bytes 442376 | tf_op jit(solution)/shard_map/ppermute | solution.py:398
  16.1 19.5 %collective-permute-start.17 = (bf16[4,96,384]{2,1,0:T(8,128)(2,1)}, bf16[4,96,384]{2,1,0:T(8,128)(2,1)S(1)}, u32[]{:S(2)}, u32[]{:S(2)}) collective-permute-start(bf16[4,96,384]{2,1,0:T(8,128)(2,1)} %copy-done.8), channel_id=1, source_target_pairs={{0,1},{1,0},{2,3},{3,2},{4,5},{5,4},{6,7},{7,6},{8,9},{9,8},{10,11... | collective-permute-start | bytes 884744 | tf_op jit(solution)/shard_map/ppermute | solution.py:398
  16.6 2.8 %copy-start = (bf16[64,4,96,96]{3,2,1,0:T(8,128)(2,1)S(1)}, bf16[64,4,96,96]{3,2,1,0:T(8,128)(2,1)}, u32[]{:S(2)}) copy-start(bf16[64,4,96,96]{3,2,1,0:T(8,128)(2,1)} %off.15) | copy-start | bytes 14155780
  19.4 1.4 %copy-start.1 = (bf16[64,96,96]{2,1,0:T(8,128)(2,1)S(1)}, bf16[64,96,96]{2,1,0:T(8,128)(2,1)}, u32[]{:S(2)}) copy-start(bf16[64,96,96]{2,1,0:T(8,128)(2,1)} %diag.15) | copy-start | bytes 3538948
  20.8 1.4 %copy-start.4 = (bf16[64,96,96]{2,1,0:T(8,128)(2,1)S(1)}, bf16[64,96,96]{2,1,0:T(8,128)(2,1)}, u32[]{:S(2)}) copy-start(bf16[64,96,96]{2,1,0:T(8,128)(2,1)} %own.7) | copy-start | bytes 3538948
  24.3 3.6 %copy-start.11 = (bf16[2,96,384]{2,1,0:T(8,128)(2,1)S(1)}, bf16[2,96,384]{2,1,0:T(8,128)(2,1)}, u32[]{:S(2)}) copy-start(bf16[2,96,384]{2,1,0:T(8,128)(2,1)} %copy-done.10) | copy-start | bytes 442372
  27.6 8.0 %copy-start.9 = (bf16[4,96,384]{2,1,0:T(8,128)(2,1)S(1)}, bf16[4,96,384]{2,1,0:T(8,128)(2,1)}, u32[]{:S(2)}) copy-start(bf16[4,96,384]{2,1,0:T(8,128)(2,1)} %copy-done.8) | copy-start | bytes 884740
  27.7 34.8 %collective-permute-start.12 = (bf16[8,96,384]{2,1,0:T(8,128)(2,1)S(1)}, bf16[8,96,384]{2,1,0:T(8,128)(2,1)S(1)}, u32[]{:S(2)}, u32[]{:S(2)}) collective-permute-start(bf16[8,96,384]{2,1,0:T(8,128)(2,1)S(1)} %shard_map.95.own), channel_id=1, source_target_pairs={{0,1},{1,0},{2,3},{3,2},{4,5},{5,4},{6,7},{7,6},{8,9},{9,8},{10,11... | collective-permute-start | bytes 1769480 | tf_op jit(solution)/shard_map/ppermute | solution.py:398
  27.9 5.6 %collective-permute-start.25 = (bf16[2,96,384]{2,1,0:T(8,128)(2,1)S(1)}, bf16[2,96,384]{2,1,0:T(8,128)(2,1)S(1)}, u32[]{:S(2)}, u32[]{:S(2)}) collective-permute-start(bf16[2,96,384]{2,1,0:T(8,128)(2,1)S(1)} %copy-done.11), channel_id=1, source_target_pairs={{0,3},{1,2},{2,1},{3,0},{4,7},{5,6},{6,5},{7,4},{8,11},{9,10},{10,... | collective-permute-start | bytes 442376 | tf_op jit(solution)/shard_map/ppermute | solution.py:397
  33.5 30.7 %collective-permute-start.13 = (bf16[8,96,384]{2,1,0:T(8,128)(2,1)S(1)}, bf16[8,96,384]{2,1,0:T(8,128)(2,1)S(1)}, u32[]{:S(2)}, u32[]{:S(2)}) collective-permute-start(bf16[8,96,384]{2,1,0:T(8,128)(2,1)S(1)} %shard_map.95.own), channel_id=1, source_target_pairs={{0,3},{1,2},{2,1},{3,0},{4,7},{5,6},{6,5},{7,4},{8,11},{9,10},{10,... | collective-permute-start | bytes 1769480 | tf_op jit(solution)/shard_map/ppermute | solution.py:397
  33.9 28.6 %slice-start = ((s8[6291456]{0:T(1024)(128)(4,1)}), s8[4194304]{0:T(1024)(128)(4,1)S(1)}, s32[]{:S(2)}) async-start(s8[6291456]{0:T(1024)(128)(4,1)} %bitcast.19), calls=%async_computation | async-start | bytes 8388608
  35.6 26.9 %slice-start.1 = ((s8[6291456]{0:T(1024)(128)(4,1)}), s8[2097152]{0:T(1024)(128)(4,1)S(1)}, s32[]{:S(2)}) async-start(s8[6291456]{0:T(1024)(128)(4,1)} %bitcast.19), calls=%async_computation.1 | async-start | bytes 4194304
  35.6 19.3 %collective-permute-start.18 = (bf16[4,96,384]{2,1,0:T(8,128)(2,1)S(1)}, bf16[4,96,384]{2,1,0:T(8,128)(2,1)S(1)}, u32[]{:S(2)}, u32[]{:S(2)}) collective-permute-start(bf16[4,96,384]{2,1,0:T(8,128)(2,1)S(1)} %copy-done.9), channel_id=1, source_target_pairs={{0,3},{1,2},{2,1},{3,0},{4,7},{5,6},{6,5},{7,4},{8,11},{9,10},{10,... | collective-permute-start | bytes 884744 | tf_op jit(solution)/shard_map/ppermute | solution.py:397
  37.1 19.0 %collective-permute-start.26 = (bf16[4,96,384]{2,1,0:T(8,128)(2,1)S(1)}, bf16[4,96,384]{2,1,0:T(8,128)(2,1)S(1)}, u32[]{:S(2)}, u32[]{:S(2)}) collective-permute-start(bf16[4,96,384]{2,1,0:T(8,128)(2,1)S(1)} %shard_map.100.own), channel_id=1, source_target_pairs={{0,1},{1,0},{2,3},{3,2},{4,5},{5,4},{6,7},{7,6},{8,9},{9,8},{10,11... | collective-permute-start | bytes 884744 | tf_op jit(solution)/shard_map/ppermute | solution.py:398
  37.4 23.9 %collective-permute-start.27 = (bf16[4,96,384]{2,1,0:T(8,128)(2,1)S(1)}, bf16[4,96,384]{2,1,0:T(8,128)(2,1)S(1)}, u32[]{:S(2)}, u32[]{:S(2)}) collective-permute-start(bf16[4,96,384]{2,1,0:T(8,128)(2,1)S(1)} %shard_map.100.own), channel_id=1, source_target_pairs={{0,3},{1,2},{2,1},{3,0},{4,7},{5,6},{6,5},{7,4},{8,11},{9,10},{10,... | collective-permute-start | bytes 884744 | tf_op jit(solution)/shard_map/ppermute | solution.py:397
  41.5 21.0 %copy-start.2 = (bf16[64,96,96]{2,1,0:T(8,128)(2,1)S(1)}, bf16[64,96,96]{2,1,0:T(8,128)(2,1)}, u32[]{:S(2)}) copy-start(bf16[64,96,96]{2,1,0:T(8,128)(2,1)} %diag.15) | copy-start | bytes 3538948
  41.5 21.0 %copy-start.7 = (s32[2]{0:T(128)S(1)}, s32[2]{0:T(128)}, u32[]{:S(2)}) copy-start(s32[2]{0:T(128)} %pad_add_fusion.2.place) | copy-start | bytes 28
  55.0 42.3 %collective-permute-start.5 = (bf16[12,96,384]{2,1,0:T(8,128)(2,1)S(1)}, bf16[12,96,384]{2,1,0:T(8,128)(2,1)S(1)}, u32[]{:S(2)}, u32[]{:S(2)}) collective-permute-start(bf16[12,96,384]{2,1,0:T(8,128)(2,1)S(1)} %shard_map.92.own), channel_id=1, source_target_pairs={{0,1},{1,0},{2,3},{3,2},{4,5},{5,4},{6,7},{7,6},{8,9},{9,8},{10,11... | collective-permute-start | bytes 2654216 | tf_op jit(solution)/shard_map/ppermute | solution.py:398
  56.1 41.2 %collective-permute-start.6 = (bf16[12,96,384]{2,1,0:T(8,128)(2,1)S(1)}, bf16[12,96,384]{2,1,0:T(8,128)(2,1)S(1)}, u32[]{:S(2)}, u32[]{:S(2)}) collective-permute-start(bf16[12,96,384]{2,1,0:T(8,128)(2,1)S(1)} %shard_map.92.own), channel_id=1, source_target_pairs={{0,3},{1,2},{2,1},{3,0},{4,7},{5,6},{6,5},{7,4},{8,11},{9,10},{10,... | collective-permute-start | bytes 2654216 | tf_op jit(solution)/shard_map/ppermute | solution.py:397
  61.3 6.6 %collective-permute-start.19 = (bf16[8,96,384]{2,1,0:T(8,128)(2,1)S(1)}, bf16[8,96,384]{2,1,0:T(8,128)(2,1)S(1)}, u32[]{:S(2)}, u32[]{:S(2)}) collective-permute-start(bf16[8,96,384]{2,1,0:T(8,128)(2,1)S(1)} %shard_map.97.own), channel_id=1, source_target_pairs={{0,1},{1,0},{2,3},{3,2},{4,5},{5,4},{6,7},{7,6},{8,9},{9,8},{10,11... | collective-permute-start | bytes 1769480 | tf_op jit(solution)/shard_map/ppermute | solution.py:398
  62.4 30.4 %collective-permute-start.20 = (bf16[8,96,384]{2,1,0:T(8,128)(2,1)S(1)}, bf16[8,96,384]{2,1,0:T(8,128)(2,1)S(1)}, u32[]{:S(2)}, u32[]{:S(2)}) collective-permute-start(bf16[8,96,384]{2,1,0:T(8,128)(2,1)S(1)} %shard_map.97.own), channel_id=1, source_target_pairs={{0,3},{1,2},{2,1},{3,0},{4,7},{5,6},{6,5},{7,4},{8,11},{9,10},{10,... | collective-permute-start | bytes 1769480 | tf_op jit(solution)/shard_map/ppermute | solution.py:397
  64.2 3.5 %collective-permute-start.28 = (bf16[2,2,48,384]{3,2,1,0:T(8,128)(2,1)S(1)}, bf16[2,2,48,384]{3,2,1,0:T(8,128)(2,1)S(1)}, u32[]{:S(2)}, u32[]{:S(2)}) collective-permute-start(bf16[2,2,48,384]{3,2,1,0:T(8,128)(2,1)S(1)} %get-tuple-element.37), channel_id=1, source_target_pairs={{0,1},{1,0},{2,3},{3,2},{4,5},{5,4},{6,7},{7,6},{8,9},{9,8},{10,11... | collective-permute-start | bytes 442376 | tf_op jit(solution)/shard_map/ppermute | solution.py:362
  67.7 29.0 %collective-permute-start.14 = (bf16[2,4,48,384]{3,2,1,0:T(8,128)(2,1)S(1)}, bf16[2,4,48,384]{3,2,1,0:T(8,128)(2,1)S(1)}, u32[]{:S(2)}, u32[]{:S(2)}) collective-permute-start(bf16[2,4,48,384]{3,2,1,0:T(8,128)(2,1)S(1)} %get-tuple-element.31), channel_id=1, source_target_pairs={{0,1},{1,0},{2,3},{3,2},{4,5},{5,4},{6,7},{7,6},{8,9},{9,8},{10,11... | collective-permute-start | bytes 884744 | tf_op jit(solution)/shard_map/ppermute | solution.py:362
  67.8 46.7 %collective-permute-start.29 = (bf16[1,2,48,384]{3,2,1,0:T(8,128)(2,1)S(1)}, bf16[1,2,48,384]{3,2,1,0:T(8,128)(2,1)S(1)}, u32[]{:S(2)}, u32[]{:S(2)}) collective-permute-start(bf16[1,2,48,384]{3,2,1,0:T(8,128)(2,1)S(1)} %add_convert_fusion.8), channel_id=1, source_target_pairs={{0,2},{1,3},{2,0},{3,1},{4,6},{5,7},{6,4},{7,5},{8,10},{9,11},{10,... | collective-permute-start | bytes 221192 | tf_op jit(solution)/shard_map/ppermute | solution.py:362
  95.8 5.6 %collective-permute-start.21 = (bf16[2,4,48,384]{3,2,1,0:T(8,128)(2,1)S(1)}, bf16[2,4,48,384]{3,2,1,0:T(8,128)(2,1)S(1)}, u32[]{:S(2)}, u32[]{:S(2)}) collective-permute-start(bf16[2,4,48,384]{3,2,1,0:T(8,128)(2,1)S(1)} %get-tuple-element.34), channel_id=1, source_target_pairs={{0,1},{1,0},{2,3},{3,2},{4,5},{5,4},{6,7},{7,6},{8,9},{9,8},{10,11... | collective-permute-start | bytes 884744 | tf_op jit(solution)/shard_map/ppermute | solution.py:362
  96.7 6.4 %collective-permute-start.15 = (bf16[1,4,48,384]{3,2,1,0:T(8,128)(2,1)S(1)}, bf16[1,4,48,384]{3,2,1,0:T(8,128)(2,1)S(1)}, u32[]{:S(2)}, u32[]{:S(2)}) collective-permute-start(bf16[1,4,48,384]{3,2,1,0:T(8,128)(2,1)S(1)} %add_convert_fusion.6), channel_id=1, source_target_pairs={{0,2},{1,3},{2,0},{3,1},{4,6},{5,7},{6,4},{7,5},{8,10},{9,11},{10,... | collective-permute-start | bytes 442376 | tf_op jit(solution)/shard_map/ppermute | solution.py:362
  101.3 3.9 %collective-permute-start.7 = (bf16[2,6,48,384]{3,2,1,0:T(8,128)(2,1)S(1)}, bf16[2,6,48,384]{3,2,1,0:T(8,128)(2,1)S(1)}, u32[]{:S(2)}, u32[]{:S(2)}) collective-permute-start(bf16[2,6,48,384]{3,2,1,0:T(8,128)(2,1)S(1)} %get-tuple-element.28), channel_id=1, source_target_pairs={{0,1},{1,0},{2,3},{3,2},{4,5},{5,4},{6,7},{7,6},{8,9},{9,8},{10,11... | collective-permute-start | bytes 1327112 | tf_op jit(solution)/shard_map/ppermute | solution.py:362
  101.4 6.3 %collective-permute-start.22 = (bf16[1,4,48,384]{3,2,1,0:T(8,128)(2,1)S(1)}, bf16[1,4,48,384]{3,2,1,0:T(8,128)(2,1)S(1)}, u32[]{:S(2)}, u32[]{:S(2)}) collective-permute-start(bf16[1,4,48,384]{3,2,1,0:T(8,128)(2,1)S(1)} %add_convert_fusion.4), channel_id=1, source_target_pairs={{0,2},{1,3},{2,0},{3,1},{4,6},{5,7},{6,4},{7,5},{8,10},{9,11},{10,... | collective-permute-start | bytes 442376 | tf_op jit(solution)/shard_map/ppermute | solution.py:362
  103.2 11.7 %collective-permute-start.16 = (bf16[4,48,384]{2,1,0:T(8,128)(2,1)S(1)}, bf16[4,48,384]{2,1,0:T(8,128)(2,1)S(1)}, u32[]{:S(2)}, u32[]{:S(2)}) collective-permute-start(bf16[4,48,384]{2,1,0:T(8,128)(2,1)S(1)} %fusion.1.refs_2_), channel_id=1, source_target_pairs={{0,4},{4,0},{8,12},{12,8},{16,20},{20,16},{24,28},{28,24},{1,5},{5... | collective-permute-start | bytes 442376 | tf_op jit(solution)/shard_map/ppermute | solution.py:428
  105.3 7.3 %collective-permute-start.8 = (bf16[1,6,48,384]{3,2,1,0:T(8,128)(2,1)S(1)}, bf16[1,6,48,384]{3,2,1,0:T(8,128)(2,1)S(1)}, u32[]{:S(2)}, u32[]{:S(2)}) collective-permute-start(bf16[1,6,48,384]{3,2,1,0:T(8,128)(2,1)S(1)} %add_convert_fusion.1), channel_id=1, source_target_pairs={{0,2},{1,3},{2,0},{3,1},{4,6},{5,7},{6,4},{7,5},{8,10},{9,11},{10,... | collective-permute-start | bytes 663560 | tf_op jit(solution)/shard_map/ppermute | solution.py:362
  107.8 7.1 %collective-permute-start.23 = (bf16[4,48,384]{2,1,0:T(8,128)(2,1)S(1)}, bf16[4,48,384]{2,1,0:T(8,128)(2,1)S(1)}, u32[]{:S(2)}, u32[]{:S(2)}) collective-permute-start(bf16[4,48,384]{2,1,0:T(8,128)(2,1)S(1)} %fusion.2.refs_4_), channel_id=1, source_target_pairs={{0,4},{4,0},{8,12},{12,8},{16,20},{20,16},{24,28},{28,24},{1,5},{5... | collective-permute-start | bytes 442376 | tf_op jit(solution)/shard_map/ppermute | solution.py:428
  112.7 7.8 %collective-permute-start.9 = (bf16[6,48,384]{2,1,0:T(8,128)(2,1)S(1)}, bf16[6,48,384]{2,1,0:T(8,128)(2,1)S(1)}, u32[]{:S(2)}, u32[]{:S(2)}) collective-permute-start(bf16[6,48,384]{2,1,0:T(8,128)(2,1)S(1)} %fusion.refs_0_), channel_id=1, source_target_pairs={{0,4},{4,0},{8,12},{12,8},{16,20},{20,16},{24,28},{28,24},{1,5},{5... | collective-permute-start | bytes 663560 | tf_op jit(solution)/shard_map/ppermute | solution.py:428
  114.5 8.8 %collective-permute-start.30 = (bf16[2,48,384]{2,1,0:T(8,128)(2,1)S(1)}, bf16[2,48,384]{2,1,0:T(8,128)(2,1)S(1)}, u32[]{:S(2)}, u32[]{:S(2)}) collective-permute-start(bf16[2,48,384]{2,1,0:T(8,128)(2,1)S(1)} %fusion.3.mine), channel_id=1, source_target_pairs={{0,4},{4,0},{8,12},{12,8},{16,20},{20,16},{24,28},{28,24},{1,5},{5... | collective-permute-start | bytes 221192 | tf_op jit(solution)/shard_map/ppermute | solution.py:428
  124.7 5.4 %collective-permute-start.32 = (bf16[1,4,48,384]{3,2,1,0:T(8,128)(2,1)S(1)}, bf16[1,4,48,384]{3,2,1,0:T(8,128)(2,1)S(1)}, u32[]{:S(2)}, u32[]{:S(2)}) collective-permute-start(bf16[1,4,48,384]{3,2,1,0:T(8,128)(2,1)S(1)} %get-tuple-element.40), channel_id=1, source_target_pairs={{0,8},{4,12},{8,0},{12,4},{16,24},{20,28},{24,16},{28,20},{1,9},{5... | collective-permute-start | bytes 442376 | tf_op jit(solution)/shard_map/ppermute | solution.py:359
  126.3 7.2 %collective-permute-start.31 = (bf16[1,4,48,384]{3,2,1,0:T(8,128)(2,1)S(1)}, bf16[1,4,48,384]{3,2,1,0:T(8,128)(2,1)S(1)}, u32[]{:S(2)}, u32[]{:S(2)}) collective-permute-start(bf16[1,4,48,384]{3,2,1,0:T(8,128)(2,1)S(1)} %get-tuple-element.39), channel_id=1, source_target_pairs={{0,8},{4,12},{8,0},{12,4},{16,24},{20,28},{24,16},{28,20},{1,9},{5... | collective-permute-start | bytes 442376 | tf_op jit(solution)/shard_map/ppermute | solution.py:360
  130.1 8.1 %collective-permute-start.33 = (bf16[1,4,48,384]{3,2,1,0:T(8,128)(2,1)S(1)}, bf16[1,4,48,384]{3,2,1,0:T(8,128)(2,1)S(1)}, u32[]{:S(2)}, u32[]{:S(2)}) collective-permute-start(bf16[1,4,48,384]{3,2,1,0:T(8,128)(2,1)S(1)} %add_convert_fusion.2), channel_id=1, source_target_pairs={{0,16},{4,20},{8,24},{12,28},{16,0},{20,4},{24,8},{28,12},{1,17},{... | collective-permute-start | bytes 442376 | tf_op jit(solution)/shard_map/ppermute | solution.py:362
  (4 other events, 3.4 us)
